TPU v7x, 256 devices: a whole 4x4x8 slice. The times are simulated.
256 devices in a mesh: seq: 16 (over z, x_lo), db: 16 (over x_hi, y, core).
Axes of the slice: x: 4 (x_hi: 2, x_lo: 2; x = x_hi * 2 + x_lo), y: 4, z: 8, core: 2. Of those that a mesh axis runs over, the one named last changes fastest.
Arguments:
- decoder_states: bfloat16 [16384, 4096], P('seq'), may hold values from -6 to 6
- query_weight: bfloat16 [4096, 4096], P(None, 'db'), may hold values from -0.09375 to 0.09375
- output_weight: bfloat16 [4096, 4096], P('db'), may hold values from -0.5 to 0.5
- neighbour_kv: bfloat16 [128, 128, 2, 4096], P('seq', None, None, 'db'), may hold values from -110 to 110
- neighbour_shard: int32 [256, 2], P('seq'), may hold values from 0 to 15, all different within a row; in each aligned block of 16 rows (0 to 15, 16 to 31, ...) at most 3 rows name the same one
- neighbour_entry: int32 [256, 2], P('seq'), may hold values from 0 to 7
- neighbour_count: int32 [256], P('seq'), may hold values from 1 to 2
Outputs:
- cross_out: bfloat16 [16384, 4096], P('seq', 'db')
Inputs may be any that keep to these rules, and one draw needn't show every extreme that they name: `neighbour_shard`: in each aligned block of 16 spans (the spans of one index of seq), no shard is named by more than 3 spans and one shard is named by exactly 3; the 2 neighbours of one span lie on different shards.
All inputs are finite; a program needn't handle non-finite values.
Results may differ from a plain program's by a relative error of at most 0.017.
Values may be sent and summed in bfloat16 or wider, within the bound.
A program may use at most 128 MiB of HBM per device.

v0:
```python
import math

import jax
import jax.numpy as jnp
from jax import lax
from jax.sharding import PartitionSpec as P

HD = 128
SPAN = 64
K = 2


def on_device(
    decoder_states,
    query_weight,
    output_weight,
    neighbour_kv,
    neighbour_shard,
    neighbour_entry,
    neighbour_count,
):
    tok_rows = decoder_states.shape[0]
    span_total = tok_rows // SPAN
    row_width = query_weight.shape[1]
    heads_here = row_width // HD
    ent_dev = neighbour_kv.shape[0]
    key_len = neighbour_kv.shape[1]
    queries = jnp.dot(decoder_states, query_weight, preferred_element_type=jnp.float32).astype(
        jnp.bfloat16
    )
    queries = queries.reshape(span_total, SPAN, heads_here, HD)
    owners = neighbour_shard.reshape(-1)
    entries = neighbour_entry.reshape(-1)
    item_count = owners.shape[0]
    empty_blocks = jnp.zeros((item_count,) + neighbour_kv.shape[1:], jnp.bfloat16)
    shard_rows = lax.all_gather(neighbour_kv, "seq", axis=0, tiled=True)
    shard_len = shard_rows.shape[0]
    local_idx = owners * ent_dev + entries
    inside = (local_idx >= 0) & (local_idx < shard_len)
    taken_rows = jnp.take(shard_rows, jnp.clip(local_idx, 0, shard_len - 1), axis=0)
    blocks = jnp.where(inside[:, None, None, None], taken_rows, empty_blocks)
    blocks = blocks.reshape(span_total, K, key_len, 2, heads_here, HD)
    key_rows = blocks[:, :, :, 0]
    val_rows = blocks[:, :, :, 1]
    scores = jnp.einsum(
        "cqhd,cknhd->chqkn", queries, key_rows, preferred_element_type=jnp.float32
    ) * (1.0 / math.sqrt(HD))
    live_slots = jnp.arange(K, dtype=jnp.int32)[None, :] < neighbour_count[:, None]
    masked = live_slots[:, None, None, :, None]
    scores = jnp.where(masked, scores, -1e30)
    top_score = jnp.max(scores, axis=(3, 4), keepdims=True)
    exponent = jnp.where(masked, jnp.exp(scores - top_score), 0.0)
    probs_bf = (exponent / jnp.sum(exponent, axis=(3, 4), keepdims=True)).astype(jnp.bfloat16)
    context = jnp.einsum(
        "chqkn,cknhd->cqhd", probs_bf, val_rows, preferred_element_type=jnp.float32
    )
    context = context.astype(jnp.bfloat16).reshape(tok_rows, row_width)
    partial_value = jnp.dot(context, output_weight, preferred_element_type=jnp.float32)
    return lax.psum_scatter(
        partial_value.astype(jnp.bfloat16), "db", scatter_dimension=1, tiled=True
    )


def solution(mesh):
    in_specs = (
        P("seq", None),
        P(None, "db"),
        P("db", None),
        P("seq", None, None, "db"),
        P("seq", None),
        P("seq", None),
        P("seq"),
    )
    out_specs = P("seq", "db")
    return jax.shard_map(
        on_device, mesh=mesh, in_specs=in_specs, out_specs=out_specs, check_vma=False
    )
```

profile of v0, /device:TPU:1, one launch (start us, length us, event | category | flops | bytes accessed | tf_op | source)
XLA Modules:
  0.0 518.9 jit_solution(15466624254692914322)
XLA Ops:
  6.5 0.0 all-gather.2.cloned.1.call-start
  6.5 2.5 copy.28
  9.1 0.0 all-gather.2.cloned.1.call-update
  9.1 0.0 reduce-scatter.2.cloned.1.call-start
  9.2 0.1 copy.29
  9.3 0.1 min.12
  9.3 0.1 copy.26
  9.4 0.1 copy.27
  9.5 6.3 %convolution_convert_fusion.1 = bf16[1024,256]{1,0:T(8,128)(2,1)S(1)} fusion(bf16[1024,4096]{1,0:T(8,128)(2,1)} %param.7, bf16[4096,256]{1,0:T(8,128)(2,1)} %param.8), kind=kOutput, calls=%fused_computation.13 | convolution fusion | flops 2147745792 | bytes 11010048 | tf_op jit(solution)/shard_map/dot_general | solution.py:28
  15.9 0.1 reshape.92
  16.0 0.0 copy-done.3
  16.0 0.1 iota_compare_fusion
  16.1 347.9 %all-gather.2.cloned.1.call-done = bf16[128,128,2,256]{3,1,2,0:T(8,128)(2,1)} async-done(((bf16[8,128,2,256]{3,1,2,0:T(8,128)(2,1)}), bf16[128,128,2,256]{3,1,2,0:T(8,128)(2,1)}) %all-gather.2.cloned.1.call-update) | async-done | bytes 16777232 | tf_op jit(solution)/shard_map/all_gather | solution.py:36
  364.0 8.5 %gather_fusion = bf16[32,128,2,256]{3,1,2,0:T(8,128)(2,1)} fusion(bf16[128,128,2,256]{3,1,2,0:T(8,128)(2,1)} %all-gather.2.cloned.1.call-done, s32[1024]{0:T(1024)S(1)} %pad_clamp_fusion), kind=kCustom, calls=%fused_computation | custom fusion | bytes 8388736 | tf_op jit(solution)/shard_map/jit(_take)/gather | solution.py:40
  372.5 6.5 %copy.30 = bf16[32,128,2,256]{1,3,2,0:T(8,128)(2,1)} copy(bf16[32,128,2,256]{3,1,2,0:T(8,128)(2,1)} %gather_fusion) | data formatting | bytes 8388608 | tf_op jit(solution)/shard_map/jit(_take)/gather | solution.py:40
  379.0 6.2 %copy.31 = bf16[16,2,128,2,2,128]{5,2,1,4,0,3:T(8,128)(2,1)} copy(bf16[16,2,128,2,2,128]{2,5,4,3,1,0:T(8,128)(2,1)} %bitcast.35) | data formatting | bytes 8388608 | tf_op jit(solution)/shard_map/jit(_take)/gather | solution.py:40
  385.2 2.9 select_select_fusion
  388.1 1.0 fusion.2
  389.1 1.2 fusion.3
  390.3 1.1 fusion.6
  391.4 0.5 copy.33
  391.9 5.6 %convolution_convert_fusion = bf16[1024,4096]{1,0:T(8,128)(2,1)} fusion(bf16[256,4096]{1,0:T(8,128)(2,1)S(1)} %copy-done, bf16[128,8,2,128]{3,2,1,0:T(2,128)(2,1)S(1)} %bitcast.36), kind=kOutput, calls=%fused_computation.1 | convolution fusion | flops 2151677952 | bytes 11010048 | tf_op jit(solution)/shard_map/dot_general | solution.py:58
  397.5 0.0 reduce-scatter.2.cloned.1.call-update
  397.5 114.5 %reduce-scatter.2.cloned.1.call-done = bf16[1024,256]{1,0:T(8,128)(2,1)} async-done(((bf16[1024,4096]{1,0:T(8,128)(2,1)}), bf16[1024,256]{1,0:T(8,128)(2,1)}) %reduce-scatter.2.cloned.1.call-update) | async-done | bytes 524304 | tf_op jit(solution)/shard_map/reduce_scatter | solution.py:59
  (10 shorter events, 0.0 us)
Async XLA Ops:
  6.5 385.4 %copy-start = (bf16[256,4096]{1,0:T(8,128)(2,1)S(1)}, bf16[256,4096]{1,0:T(8,128)(2,1)}, u32[]{:S(2)}) copy-start(bf16[256,4096]{1,0:T(8,128)(2,1)} %param.9) | copy-start | bytes 6291460
  6.5 2.6 copy-start.2
  6.5 2.6 copy-start.1
  6.5 357.5 %all-gather.2.cloned.1.call-start = ((), (), s32[]{:S(2)}) async-start(), calls=%async_computation.1 | async-start | bytes 17825792 | tf_op jit(solution)/shard_map/all_gather | solution.py:36
  9.1 502.9 %reduce-scatter.2.cloned.1.call-start = ((), (), s32[]{:S(2)}) async-start(), calls=%async_computation.2 | async-start | bytes 8912896 | tf_op jit(solution)/shard_map/reduce_scatter | solution.py:59
  9.5 6.5 %copy-start.3 = (s32[16]{0:T(128)S(1)}, s32[16]{0:T(128)}, u32[]{:S(2)}) copy-start(s32[16]{0:T(128)} %param.13) | copy-start | bytes 196
Sparse Core Ops, SparseCore 0:
  9.2 354.7 all-gather.1
  397.6 114.3 reduce-scatter.1
where the time goes:
time: 519 us
  waiting for transfers between devices  462 us (89%)
  local copies, waits for them, and re-layouts  24.8 us (5%)
  matrix products  13.9 us (3%)
  between operations  13.5 us (3%)
    all_gather x1, waiting for transfers between devices, on_device(): shard_rows = lax.all_gather(neighbour_kv, 'seq', axis=0, tiled=True)  348 us
    reduce_scatter x1, waiting for transfers between devices, on_device(): lax.psum_scatter(partial_value.astype(jnp.bfloat16), 'db', scatter_dimens...  114 us
    gather x3, local copies, waits for them, and re-layouts, on_device(): jnp.take(shard_rows, jnp.clip(local_idx, 0, shard_len - 1), axis=0)  21.2 us
  transfers between devices with their start and end apart: 2, of which 2 were waited for; matrix products, arithmetic and copies ran while one was open for 1% of the time, Pallas kernels for 0%

commit v1 on v0

--- a/solution.py
+++ b/solution.py
@@ -8,6 +8,37 @@
 HD = 128
 SPAN = 64
 K = 2
+CAP = 3
+
+
+def request_tables(neighbour_shard, neighbour_entry, neighbour_count, me, n_seq):
+    spans_here = neighbour_shard.shape[0]
+    table = jnp.concatenate(
+        [neighbour_shard, neighbour_entry, neighbour_count[:, None]], axis=1
+    )
+    table_all = lax.all_gather(table, "seq", axis=0, tiled=False)
+    shard_all = table_all[:, :, 0:K]
+    entry_all = table_all[:, :, K : 2 * K]
+    count_all = table_all[:, :, 2 * K]
+    live_all = jnp.arange(K, dtype=jnp.int32)[None, None, :] < count_all[:, :, None]
+    shard_flat = shard_all.reshape(n_seq, spans_here * K)
+    entry_flat = entry_all.reshape(n_seq, spans_here * K)
+    live_flat = live_all.reshape(n_seq, spans_here * K)
+    match = (shard_flat == me) & live_flat
+    rank = jnp.cumsum(match.astype(jnp.int32), axis=1) - 1
+    slots = jnp.arange(CAP, dtype=jnp.int32)
+    pick = match[:, :, None] & (rank[:, :, None] == slots[None, None, :])
+    send_entry = jnp.sum(jnp.where(pick, entry_flat[:, :, None], 0), axis=1)
+    own_shard = neighbour_shard.reshape(-1)
+    own_live = (
+        jnp.arange(K, dtype=jnp.int32)[None, :] < neighbour_count[:, None]
+    ).reshape(-1)
+    same = (own_shard[None, :] == own_shard[:, None]) & own_live[None, :]
+    earlier = jnp.arange(own_shard.shape[0])[None, :] < jnp.arange(own_shard.shape[0])[:, None]
+    own_rank = jnp.sum((same & earlier).astype(jnp.int32), axis=1)
+    own_rank = jnp.minimum(own_rank, CAP - 1)
+    recv_idx = own_shard * CAP + own_rank
+    return send_entry, recv_idx
 
 
 def on_device(
@@ -23,22 +54,23 @@
     span_total = tok_rows // SPAN
     row_width = query_weight.shape[1]
     heads_here = row_width // HD
-    ent_dev = neighbour_kv.shape[0]
     key_len = neighbour_kv.shape[1]
+    n_seq = lax.psum(1, "seq")
+    me = lax.axis_index("seq")
     queries = jnp.dot(decoder_states, query_weight, preferred_element_type=jnp.float32).astype(
         jnp.bfloat16
     )
     queries = queries.reshape(span_total, SPAN, heads_here, HD)
-    owners = neighbour_shard.reshape(-1)
-    entries = neighbour_entry.reshape(-1)
-    item_count = owners.shape[0]
-    empty_blocks = jnp.zeros((item_count,) + neighbour_kv.shape[1:], jnp.bfloat16)
-    shard_rows = lax.all_gather(neighbour_kv, "seq", axis=0, tiled=True)
-    shard_len = shard_rows.shape[0]
-    local_idx = owners * ent_dev + entries
-    inside = (local_idx >= 0) & (local_idx < shard_len)
-    taken_rows = jnp.take(shard_rows, jnp.clip(local_idx, 0, shard_len - 1), axis=0)
-    blocks = jnp.where(inside[:, None, None, None], taken_rows, empty_blocks)
+
+    send_entry, recv_idx = request_tables(
+        neighbour_shard, neighbour_entry, neighbour_count, me, n_seq
+    )
+    send_buf = jnp.take(neighbour_kv, send_entry.reshape(-1), axis=0)
+    send_buf = send_buf.reshape((n_seq, CAP) + neighbour_kv.shape[1:])
+    recv_buf = lax.all_to_all(send_buf, "seq", 0, 0, tiled=True)
+    recv_buf = recv_buf.reshape((n_seq * CAP,) + neighbour_kv.shape[1:])
+    blocks = jnp.take(recv_buf, recv_idx, axis=0)
+
     blocks = blocks.reshape(span_total, K, key_len, 2, heads_here, HD)
     key_rows = blocks[:, :, :, 0]
     val_rows = blocks[:, :, :, 1]

time: 519 us -> 353 us (0.68)
  waiting for transfers between devices: 462 us -> 242 us
  blocking collectives: 0 us -> 30.4 us
  local copies, waits for them, and re-layouts: 24.8 us -> 36.2 us
  other arithmetic: 4.19 us -> 11.8 us
    all_gather x1 -> x0, waiting for transfers between devices: 348 us -> none  [on_device(): shard_rows = lax.all_gather(neighbour_kv, 'seq', axis=0, tiled=True)]
    all_to_all x0 -> x1, waiting for transfers between devices: none -> 132 us  [on_device(): recv_buf = lax.all_to_all(send_buf, 'seq', 0, 0, tiled=True)]
    all_gather x0 -> x1, blocking collectives: none -> 30.4 us  [request_tables(): table_all = lax.all_gather(table, 'seq', axis=0, tiled=False)]
    gather x3 -> x4, local copies, waits for them, and re-layouts: 21.2 us -> 33.8 us  [the longest x3 18.3 us: on_device(): blocks = jnp.take(recv_buf, recv_idx, axis=0)]
    select_n x2 -> x4, other arithmetic: 2.88 us -> 8.98 us  [the longest x2 6.3 us: on_device(): send_buf = jnp.take(neighbour_kv, send_entry.reshape(-1), axis=0)]
  transfers between devices with their start and end apart: 2 -> 2, of which waited for: 2 -> 2; matrix products, arithmetic and copies ran while one was open for 1% -> 2% of each run, Pallas kernels for 0% -> 0%
where the time goes in v1:
time: 353 us
  waiting for transfers between devices  242 us (69%)
  local copies, waits for them, and re-layouts  36.2 us (10%)
  blocking collectives  30.4 us (9%)
  matrix products  14 us (4%)
  between operations  13.6 us (4%)
  other arithmetic  11.8 us (3%)
  starting transfers between devices  4.98 us (1%)
    all_to_all x1, waiting for transfers between devices, on_device(): recv_buf = lax.all_to_all(send_buf, 'seq', 0, 0, tiled=True)  132 us
    reduce_scatter x1, waiting for transfers between devices, on_device(): lax.psum_scatter(partial_value.astype(jnp.bfloat16), 'db', scatter_dimens...  110 us
    all_gather x1, blocking collectives, request_tables(): table_all = lax.all_gather(table, 'seq', axis=0, tiled=False)  30.4 us
    gather x3, local copies, waits for them, and re-layouts, on_device(): blocks = jnp.take(recv_buf, recv_idx, axis=0)  18.3 us
    gather x1, local copies, waits for them, and re-layouts, on_device(): send_buf = jnp.take(neighbour_kv, send_entry.reshape(-1), axis=0)  15.6 us
  transfers between devices with their start and end apart: 2, of which 2 were waited for; matrix products, arithmetic and copies ran while one was open for 2% of the time, Pallas kernels for 0%

profile of v1, /device:TPU:1, one launch (start us, length us, event | category | flops | bytes accessed | tf_op | source)
XLA Modules:
  0.0 352.7 jit_solution(5759936729236275683)
XLA Ops:
  6.5 0.9 add_bitcast_fusion
  7.4 30.4 %all-gather.1 = s32[16,16,5]{1,2,0:T(8,128)S(1)} all-gather(s32[1,16,5]{1,2,0:T(8,128)S(1)} %add_bitcast_fusion), channel_id=2, replica_groups=mesh['seq'=16,'db'=16] {'seq'}, dimensions={0}, use_global_device_ids=true | all-gather | bytes 5440 | tf_op jit(solution)/shard_map/all_gather | solution.py:19
  38.3 0.2 reduce_window_sum.11
  38.8 0.2 select_reduce_fusion
  39.1 0.1 copy.73
  39.2 15.6 %gather_fusion = bf16[48,128,2,256]{3,2,1,0:T(2,128)(2,1)} fusion(bf16[8,128,2,256]{3,2,1,0:T(2,128)(2,1)} %param.10, s32[1024]{0:T(1024)S(1)} %pad_clamp_fusion.1), kind=kCustom, calls=%fused_computation | custom fusion | bytes 12583104 | tf_op jit(solution)/shard_map/jit(_take)/gather | solution.py:68
  54.8 6.3 %copy_select_fusion = bf16[16,3,128,2,256]{4,2,3,1,0:T(8,128)(2,1)} fusion(bf16[16,3,128,2,256]{4,3,2,1,0:T(2,128)(2,1)} %bitcast.51, pred[16,3]{1,0:T(8,128)(4,1)S(1)} %copy.73), kind=kLoop, calls=%fused_computation.3 | loop fusion | flops 3145728 | bytes 12582960 | tf_op jit(solution)/shard_map/jit(_take)/select_n | solution.py:68
  61.1 4.8 %all-to-all-start = ((bf16[16,3,128,2,256]{4,2,3,1,0:T(8,128)(2,1)}), bf16[16,3,128,2,256]{4,2,3,1,0:T(8,128)(2,1)}, u32[]{:S(2)}, u32[]{:S(2)}) async-start(bf16[16,3,128,2,256]{4,2,3,1,0:T(8,128)(2,1)} %copy_select_fusion), calls=%async_computation | async-start | bytes 12582912 | tf_op jit(solution)/shard_map/all_to_all | solution.py:70
  65.9 0.2 reduce-scatter.2.cloned.1.call-start
  66.7 0.2 convert_reduce_fusion
  67.0 0.1 copy.65
  67.1 6.3 %convolution_convert_fusion.1 = bf16[1024,256]{1,0:T(8,128)(2,1)S(1)} fusion(bf16[1024,4096]{1,0:T(8,128)(2,1)} %param.7, bf16[4096,256]{1,0:T(8,128)(2,1)} %param.8), kind=kOutput, calls=%fused_computation.15 | convolution fusion | flops 2147745792 | bytes 11010048 | tf_op jit(solution)/shard_map/dot_general | solution.py:60
  73.5 0.1 reshape.199
  73.7 132.2 %all-to-all-done = bf16[16,3,128,2,256]{4,2,3,1,0:T(8,128)(2,1)} async-done(((bf16[16,3,128,2,256]{4,2,3,1,0:T(8,128)(2,1)}), bf16[16,3,128,2,256]{4,2,3,1,0:T(8,128)(2,1)}, u32[]{:S(2)}, u32[]{:S(2)}) %all-to-all-start) | async-done | bytes 6291488 | tf_op jit(solution)/shard_map/all_to_all | solution.py:70
  205.9 5.6 %gather_fusion.1 = bf16[32,128,2,256]{3,1,2,0:T(8,128)(2,1)} fusion(bf16[48,128,2,256]{3,1,2,0:T(8,128)(2,1)} %bitcast.7, s32[1024]{0:T(1024)S(1)} %pad_clamp_fusion), kind=kCustom, calls=%fused_computation.1 | custom fusion | bytes 8388736 | tf_op jit(solution)/shard_map/jit(_take)/gather | solution.py:72
  211.5 6.4 %copy.77 = bf16[32,128,2,256]{1,3,2,0:T(8,128)(2,1)} copy(bf16[32,128,2,256]{3,1,2,0:T(8,128)(2,1)} %gather_fusion.1) | data formatting | bytes 8388608 | tf_op jit(solution)/shard_map/jit(_take)/gather | solution.py:72
  217.9 6.2 %copy.78 = bf16[16,2,128,2,2,128]{5,2,1,4,0,3:T(8,128)(2,1)} copy(bf16[16,2,128,2,2,128]{2,5,4,3,1,0:T(8,128)(2,1)} %bitcast.52) | data formatting | bytes 8388608 | tf_op jit(solution)/shard_map/jit(_take)/gather | solution.py:72
  224.1 2.7 broadcast_select_fusion
  226.8 1.0 fusion.2
  227.8 1.2 fusion.3
  229.0 1.1 fusion.6
  230.1 0.5 copy.80
  230.7 5.6 %convolution_convert_fusion = bf16[1024,4096]{1,0:T(8,128)(2,1)} fusion(bf16[256,4096]{1,0:T(8,128)(2,1)S(1)} %copy-done, bf16[128,8,2,128]{3,2,1,0:T(2,128)(2,1)S(1)} %bitcast.53), kind=kOutput, calls=%fused_computation.2 | convolution fusion | flops 2151677952 | bytes 11010048 | tf_op jit(solution)/shard_map/dot_general | solution.py:90
  236.3 109.6 %reduce-scatter.2.cloned.1.call-done = bf16[1024,256]{1,0:T(8,128)(2,1)} async-done(((bf16[1024,4096]{1,0:T(8,128)(2,1)}), bf16[1024,256]{1,0:T(8,128)(2,1)}) %reduce-scatter.2.cloned.1.call-update) | async-done | bytes 524304 | tf_op jit(solution)/shard_map/reduce_scatter | solution.py:91
  (42 shorter events, 1.7 us)
Async XLA Ops:
  6.5 224.1 %copy-start = (bf16[256,4096]{1,0:T(8,128)(2,1)S(1)}, bf16[256,4096]{1,0:T(8,128)(2,1)}, u32[]{:S(2)}) copy-start(bf16[256,4096]{1,0:T(8,128)(2,1)} %param.9) | copy-start | bytes 6291460
  61.1 5.0 %copy-start.1 = (s32[16,2]{0,1:T(2,128)S(1)}, s32[16,2]{0,1:T(2,128)}, u32[]{:S(2)}) copy-start(s32[16,2]{0,1:T(2,128)} %param.11) | copy-start | bytes 388
  61.1 5.1 %copy-start.2 = (s32[16]{0:T(128)S(1)}, s32[16]{0:T(128)}, u32[]{:S(2)}) copy-start(s32[16]{0:T(128)} %param.13) | copy-start | bytes 196
  61.1 144.7 %all-to-all-start = ((bf16[16,3,128,2,256]{4,2,3,1,0:T(8,128)(2,1)}), bf16[16,3,128,2,256]{4,2,3,1,0:T(8,128)(2,1)}, u32[]{:S(2)}, u32[]{:S(2)}) async-start(bf16[16,3,128,2,256]{4,2,3,1,0:T(8,128)(2,1)} %copy_select_fusion), calls=%async_computation | async-start | bytes 12582912 | tf_op jit(solution)/shard_map/all_to_all | solution.py:70
  65.9 280.0 %reduce-scatter.2.cloned.1.call-start = ((), (), s32[]{:S(2)}) async-start(), calls=%async_computation.2 | async-start | bytes 8912896 | tf_op jit(solution)/shard_map/reduce_scatter | solution.py:91
Sparse Core Ops, SparseCore 0:
  236.4 109.4 reduce-scatter.1

commit v2 on v0

v2 whole, which is shorter than its diff:
```python
import math

import jax
import jax.numpy as jnp
from jax import lax
from jax.sharding import PartitionSpec as P

HD = 128
SPAN = 64
K = 2
CAP = 3


def slot_places(neighbour_shard, neighbour_count):
    own_shard = neighbour_shard.reshape(-1)
    slots = own_shard.shape[0]
    own_live = (
        jnp.arange(K, dtype=jnp.int32)[None, :] < neighbour_count[:, None]
    ).reshape(-1)
    same = (own_shard[None, :] == own_shard[:, None]) & own_live[None, :]
    earlier = jnp.arange(slots)[None, :] < jnp.arange(slots)[:, None]
    own_rank = jnp.minimum(jnp.sum((same & earlier).astype(jnp.int32), axis=1), CAP - 1)
    return own_live, own_shard * CAP + own_rank


def on_device(
    decoder_states,
    query_weight,
    output_weight,
    neighbour_kv,
    neighbour_shard,
    neighbour_entry,
    neighbour_count,
):
    tok_rows = decoder_states.shape[0]
    span_total = tok_rows // SPAN
    row_width = query_weight.shape[1]
    heads_here = row_width // HD
    key_len = neighbour_kv.shape[1]
    n_seq = lax.psum(1, "seq")
    places_total = n_seq * CAP
    queries = jnp.dot(decoder_states, query_weight, preferred_element_type=jnp.float32).astype(
        jnp.bfloat16
    )
    queries = queries.reshape(span_total, SPAN, row_width)

    live, place = slot_places(neighbour_shard, neighbour_count)
    target = jnp.where(live, place, places_total)
    span_of_slot = jnp.arange(span_total * K, dtype=jnp.int32) // K
    send_q = jnp.zeros((places_total, SPAN, row_width), jnp.bfloat16)
    send_q = send_q.at[target].set(queries[span_of_slot], mode="drop")
    send_e = jnp.zeros((places_total,), jnp.int32)
    send_e = send_e.at[target].set(neighbour_entry.reshape(-1), mode="drop")
    recv_q = lax.all_to_all(
        send_q.reshape(n_seq, CAP, SPAN, row_width), "seq", 0, 0, tiled=True
    ).reshape(places_total, SPAN, heads_here, HD)
    recv_e = lax.all_to_all(send_e.reshape(n_seq, CAP), "seq", 0, 0, tiled=True).reshape(-1)

    blocks = jnp.take(neighbour_kv, recv_e, axis=0)
    blocks = blocks.reshape(places_total, key_len, 2, heads_here, HD)
    key_rows = blocks[:, :, 0]
    val_rows = blocks[:, :, 1]
    scores = jnp.einsum(
        "pqhd,pnhd->phqn", recv_q, key_rows, preferred_element_type=jnp.float32
    ) * (1.0 / math.sqrt(HD))
    top = jnp.max(scores, axis=3, keepdims=True)
    weights = jnp.exp(scores - top)
    total = jnp.sum(weights, axis=3, keepdims=True)
    part = jnp.einsum(
        "phqn,pnhd->pqhd", weights.astype(jnp.bfloat16), val_rows,
        preferred_element_type=jnp.float32,
    )
    part = part / jnp.transpose(total, (0, 2, 1, 3))
    stats = jnp.concatenate([top, total], axis=3)
    back_ctx = lax.all_to_all(
        part.astype(jnp.bfloat16).reshape(n_seq, CAP, SPAN, row_width), "seq", 0, 0, tiled=True
    ).reshape(places_total, SPAN, heads_here, HD)
    back_stats = lax.all_to_all(
        stats.reshape(n_seq, CAP, heads_here, SPAN, 2), "seq", 0, 0, tiled=True
    ).reshape(places_total, heads_here, SPAN, 2)

    slot_ctx = jnp.take(back_ctx, place, axis=0).reshape(span_total, K, SPAN, heads_here, HD)
    slot_stats = jnp.take(back_stats, place, axis=0).reshape(span_total, K, heads_here, SPAN, 2)
    live_k = live.reshape(span_total, K)[:, :, None, None]
    slot_top = jnp.where(live_k, slot_stats[..., 0], -jnp.inf)
    best = jnp.max(slot_top, axis=1, keepdims=True)
    scale = jnp.where(live_k, jnp.exp(slot_top - best) * slot_stats[..., 1], 0.0)
    share = scale / jnp.sum(scale, axis=1, keepdims=True)
    share = jnp.transpose(share, (0, 1, 3, 2))[..., None]
    slot_vals = jnp.where(live_k[..., None], slot_ctx.astype(jnp.float32), 0.0)
    context = jnp.sum(share * slot_vals, axis=1)
    context = context.astype(jnp.bfloat16).reshape(tok_rows, row_width)
    partial_value = jnp.dot(context, output_weight, preferred_element_type=jnp.float32)
    return lax.psum_scatter(
        partial_value.astype(jnp.bfloat16), "db", scatter_dimension=1, tiled=True
    )


def solution(mesh):
    in_specs = (
        P("seq", None),
        P(None, "db"),
        P("db", None),
        P("seq", None, None, "db"),
        P("seq", None),
        P("seq", None),
        P("seq"),
    )
    out_specs = P("seq", "db")
    return jax.shard_map(
        on_device, mesh=mesh, in_specs=in_specs, out_specs=out_specs, check_vma=False
    )
```

time: 519 us -> 300 us (0.58)
  waiting for transfers between devices: 462 us -> 142 us
  local copies, waits for them, and re-layouts: 24.8 us -> 74 us
  starting transfers between devices: 0.04 us -> 32.7 us
  other arithmetic: 4.19 us -> 15.4 us
  matrix products: 13.9 us -> 20.4 us
    all_gather x1 -> x0, waiting for transfers between devices: 348 us -> none  [on_device(): shard_rows = lax.all_gather(neighbour_kv, 'seq', axis=0, tiled=True)]
    all_to_all x0 -> x4, starting transfers between devices: none -> 32.6 us  [the longest x1 10 us: on_device(): lax.all_to_all(send_e.reshape(n_seq, CAP), 'seq', 0, 0, tiled=True)]
    all_to_all x0 -> x4, waiting for transfers between devices: none -> 31.5 us  [the longest x1 31.5 us: on_device(): lax.all_to_all(part.astype(jnp.bfloat16).reshape(n_seq, CAP, SPAN, row_wi...]
    gather x3 -> x6, local copies, waits for them, and re-layouts: 21.2 us -> 45.1 us  [the longest x3 38.8 us: on_device(): blocks = jnp.take(neighbour_kv, recv_e, axis=0)]
    reshape x1 -> x7, local copies, waits for them, and re-layouts: 0.12 us -> 11.1 us  [the longest x1 3.75 us: on_device(): part.astype(jnp.bfloat16).reshape(n_seq, CAP, SPAN, row_width)]
    dot_general x2, matrix products: 2.03 us -> 8.51 us  [the longest x1 4.73 us: on_device(): jnp.einsum('pqhd,pnhd->phqn', recv_q, key_rows, preferred_element_type=jn...]
    scatter x0 -> x2, local copies, waits for them, and re-layouts: none -> 5.88 us  [the longest x1 5.21 us: on_device(): send_q = send_q.at[target].set(queries[span_of_slot], mode='drop')]
    reduce_sum x1 -> x4, other arithmetic: 1.22 us -> 6.69 us  [the longest x1 4.47 us: on_device(): context = jnp.sum(share * slot_vals, axis=1)]
  transfers between devices with their start and end apart: 2 -> 5, of which waited for: 2 -> 2; matrix products, arithmetic and copies ran while one was open for 1% -> 25% of each run, Pallas kernels for 0% -> 0%
where the time goes in v2:
time: 300 us; the launch traced here: 298 us
  waiting for transfers between devices  142 us (47%)
  local copies, waits for them, and re-layouts  74 us (25%)
  starting transfers between devices  32.7 us (11%)
  matrix products  20.4 us (7%)
  other arithmetic  15.4 us (5%)
  between operations  13.7 us (5%)
    reduce_scatter x1, waiting for transfers between devices, on_device(): lax.psum_scatter(partial_value.astype(jnp.bfloat16), 'db', scatter_dimens...  111 us
    gather x3, local copies, waits for them, and re-layouts, on_device(): blocks = jnp.take(neighbour_kv, recv_e, axis=0)  38.8 us
    all_to_all x1, waiting for transfers between devices, on_device(): lax.all_to_all(part.astype(jnp.bfloat16).reshape(n_seq, CAP, SPAN, row_wi...  31.5 us
    all_to_all x1, starting transfers between devices, on_device(): lax.all_to_all(send_e.reshape(n_seq, CAP), 'seq', 0, 0, tiled=True)  10 us
    all_to_all x1, starting transfers between devices, on_device(): lax.all_to_all(send_q.reshape(n_seq, CAP, SPAN, row_width), 'seq', 0, 0,...  7.61 us
    all_to_all x1, starting transfers between devices, on_device(): lax.all_to_all(part.astype(jnp.bfloat16).reshape(n_seq, CAP, SPAN, row_wi...  7.59 us
    all_to_all x1, starting transfers between devices, on_device(): lax.all_to_all(stats.reshape(n_seq, CAP, heads_here, SPAN, 2), 'seq', 0,...  7.36 us
    dot_general x1, matrix products, on_device(): jnp.dot(decoder_states, query_weight, preferred_element_type=jnp.float32)  6.31 us
  transfers between devices with their start and end apart: 5, of which 2 were waited for; matrix products, arithmetic and copies ran while one was open for 25% of the time, Pallas kernels for 0%

profile of v2, /device:TPU:1, one launch (start us, length us, event | category | flops | bytes accessed | tf_op | source)
XLA Modules:
  0.0 298.3 jit_solution(2349011017089471201)
XLA Ops:
  11.0 10.0 %all-to-all-start.1 = ((s32[16,1,3]{2,1,0:T(1,128)}), s32[16,1,3]{2,1,0:T(1,128)S(1)}, u32[]{:S(2)}, u32[]{:S(2)}) async-start(s32[16,1,3]{2,1,0:T(1,128)} %bitcast.5), calls=%async_computation.1 | async-start | bytes 16384 | tf_op jit(solution)/shard_map/all_to_all | solution.py:57
  21.0 6.3 %convolution_convert_fusion.1 = bf16[1024,256]{1,0:T(8,128)(2,1)S(1)} fusion(bf16[1024,4096]{1,0:T(8,128)(2,1)} %param.7, bf16[4096,256]{1,0:T(8,128)(2,1)} %param.8), kind=kOutput, calls=%fused_computation.23 | convolution fusion | flops 2147745792 | bytes 11010048 | tf_op jit(solution)/shard_map/dot_general | solution.py:42
  27.4 1.6 gather_fusion
  30.3 5.2 %scatter_fusion = bf16[48,64,256]{2,1,0:T(8,128)(2,1)} fusion(bf16[48,64,256]{2,1,0:T(8,128)(2,1)} %broadcast_in_dim.86, s32[32]{0:T(128)S(1)} %get-tuple-element.10, bf16[32,64,256]{2,1,0:T(8,128)(2,1)} %gather_fusion), kind=kCustom, calls=%fused_computation.4 | custom fusion | bytes 3145856 | tf_op jit(solution)/shard_map/scatter | solution.py:51
  35.5 7.6 %all-to-all-start = ((bf16[16,3,64,256]{3,2,1,0:T(8,128)(2,1)}), bf16[16,3,64,256]{3,2,1,0:T(8,128)(2,1)}, u32[]{:S(2)}, u32[]{:S(2)}) async-start(bf16[16,3,64,256]{3,2,1,0:T(8,128)(2,1)} %bitcast.68), calls=%async_computation | async-start | bytes 3145728 | tf_op jit(solution)/shard_map/all_to_all | solution.py:54
  43.3 14.4 %gather_fusion.1 = bf16[48,128,2,256]{3,2,1,0:T(2,128)(2,1)} fusion(bf16[8,128,2,256]{3,2,1,0:T(2,128)(2,1)S(1)} %copy-done.1, s32[1024]{0:T(1024)S(1)} %pad_clamp_fusion.1), kind=kCustom, calls=%fused_computation.1 | custom fusion | bytes 12583104 | tf_op jit(solution)/shard_map/jit(_take)/gather | solution.py:59
  57.6 15.8 %copy.51 = bf16[48,128,2,256]{1,3,2,0:T(8,128)(2,1)} copy(bf16[48,128,2,256]{3,2,1,0:T(2,128)(2,1)} %gather_fusion.1) | data formatting | bytes 12582912 | tf_op jit(solution)/shard_map/jit(_take)/gather | solution.py:59
  73.4 8.6 %copy.52 = bf16[48,128,2,2,128]{4,1,3,0,2:T(8,128)(2,1)} copy(bf16[48,128,2,2,128]{1,4,3,2,0:T(8,128)(2,1)} %bitcast.67) | data formatting | bytes 12582912 | tf_op jit(solution)/shard_map/jit(_take)/gather | solution.py:59
  83.4 6.2 %broadcast_select_fusion = bf16[48,128,2,2,128]{4,1,3,0,2:T(8,128)(2,1)} fusion(bf16[48,128,2,2,128]{4,1,3,0,2:T(8,128)(2,1)} %copy.52, pred[48]{0:T(512)(128)(4,1)S(1)} %compare_and_fusion.1), kind=kLoop, calls=%fused_computation.7 | loop fusion | flops 3145728 | bytes 12582960 | tf_op jit(solution)/shard_map/jit(_take)/select_n | solution.py:59
  89.5 3.5 %reshape.275 = bf16[48,64,2,128]{3,2,1,0:T(2,128)(2,1)} reshape(bf16[16,3,64,256]{3,2,1,0:T(8,128)(2,1)} %all-to-all-done) | data formatting | bytes 3145728 | tf_op jit(solution)/shard_map/reshape | solution.py:56
  93.0 4.7 %multiply_reduce_fusion = (f32[48,2,64]{2,1,0:T(2,128)S(1)}, f32[48,2,64,128]{3,2,1,0:T(8,128)S(1)}) fusion(bf16[48,128,2,2,128]{4,1,3,0,2:T(8,128)(2,1)} %broadcast_select_fusion, bf16[48,64,2,128]{3,2,1,0:T(2,128)(2,1)} %reshape.275), kind=kOutput, calls=%fused_computation.15 | convolution fusion | flops 202893312 | bytes 7888896 | tf_op jit(solution)/shard_map/pqhd,pnhd->phqn/dot_general | solution.py:63
  97.8 1.7 copy-done.2
  99.5 1.9 fusion.4
  102.2 7.4 %all-to-all-start.2 = ((f32[16,1,768]{2,1,0:T(1,128)}), f32[16,1,768]{2,1,0:T(1,128)S(1)}, u32[]{:S(2)}, u32[]{:S(2)}) async-start(f32[16,1,768]{2,1,0:T(1,128)} %reshape.344), calls=%async_computation.2 | async-start | bytes 98304 | tf_op jit(solution)/shard_map/all_to_all | solution.py:78
  109.6 3.8 %fusion.2 = bf16[48,64,2,128]{3,1,2,0:T(8,128)(2,1)S(1)} fusion(bf16[48,128,2,2,128]{4,1,3,0,2:T(8,128)(2,1)} %broadcast_select_fusion, f32[48,2,64,128]{3,2,1,0:T(8,128)} %copy-done.2, f32[48,64,2]{1,2,0:T(2,128)S(1)} %bitcast.76, f32[48,2,64]{2,1,0:T(2,128)S(1)} %get-tuple-element.11), kind=kOutput, calls=%fused_computation.13 | convolution fusion | flops 205258752 | bytes 7913472 | tf_op jit(solution)/shard_map/phqn,pnhd->pqhd/dot_general | solution.py:69
  113.3 2.8 copy.57
  116.1 3.8 %reshape.280 = bf16[16,3,64,256]{3,2,1,0:T(8,128)(2,1)} reshape(bf16[48,64,2,128]{3,2,1,0:T(2,128)(2,1)} %copy.57) | data formatting | bytes 3145728 | tf_op jit(solution)/shard_map/reshape | solution.py:76
  119.9 7.6 %all-to-all-start.3 = ((bf16[16,3,64,256]{3,2,1,0:T(8,128)(2,1)}), bf16[16,3,64,256]{3,2,1,0:T(8,128)(2,1)}, u32[]{:S(2)}, u32[]{:S(2)}) async-start(bf16[16,3,64,256]{3,2,1,0:T(8,128)(2,1)} %reshape.280), calls=%async_computation.3 | async-start | bytes 3145728 | tf_op jit(solution)/shard_map/all_to_all | solution.py:75
  131.6 31.5 %all-to-all-done.3 = bf16[16,3,64,256]{3,2,1,0:T(8,128)(2,1)} async-done(((bf16[16,3,64,256]{3,2,1,0:T(8,128)(2,1)}), bf16[16,3,64,256]{3,2,1,0:T(8,128)(2,1)}, u32[]{:S(2)}, u32[]{:S(2)}) %all-to-all-start.3) | async-done | bytes 1572896 | tf_op jit(solution)/shard_map/all_to_all | solution.py:75
  163.1 3.5 %reshape.281 = bf16[48,64,2,128]{3,2,1,0:T(2,128)(2,1)} reshape(bf16[16,3,64,256]{3,2,1,0:T(8,128)(2,1)} %all-to-all-done.3) | data formatting | bytes 3145728 | tf_op jit(solution)/shard_map/reshape | solution.py:77
  166.6 4.1 %gather_fusion.3 = bf16[32,64,2,128]{3,2,1,0:T(2,128)(2,1)S(1)} fusion(bf16[48,64,2,128]{3,2,1,0:T(2,128)(2,1)} %reshape.281, s32[1024]{0:T(1024)S(1)} %pad_clamp_fusion), kind=kCustom, calls=%fused_computation.3 | custom fusion | bytes 2097280 | tf_op jit(solution)/shard_map/jit(_take)/gather | solution.py:82
  170.6 4.5 %multiply_reduce_fusion.1 = bf16[16,64,2,128]{3,2,1,0:T(2,128)(2,1)S(1)} fusion(pred[16,2]{1,0:T(8,128)(4,1)S(1)} %iota_compare_fusion.1, pred[16,2]{1,0:T(8,128)(4,1)S(1)} %compare_and_fusion, f32[16,2,64,2]{3,2,1,0:T(8,128)} %copy.56, bf16[32,64,2,128]{3,2,1,0:T(2,128)(2,1)S(1)} %gather_fusion.3), kind=kLoop, calls=%fused_computation.18 | loop fusion | flops 2359296 | bytes 1589312 | tf_op jit(solution)/shard_map/reduce_sum | solution.py:91
  175.1 5.6 %convolution_convert_fusion = bf16[1024,4096]{1,0:T(8,128)(2,1)} fusion(bf16[256,4096]{1,0:T(8,128)(2,1)S(1)} %copy-done, bf16[128,8,2,128]{3,2,1,0:T(2,128)(2,1)S(1)} %bitcast.69), kind=kOutput, calls=%fused_computation.6 | convolution fusion | flops 2151677952 | bytes 11010048 | tf_op jit(solution)/shard_map/dot_general | solution.py:93
  180.7 110.8 %reduce-scatter.2.cloned.1.call-done = bf16[1024,256]{1,0:T(8,128)(2,1)} async-done(((bf16[1024,4096]{1,0:T(8,128)(2,1)}), bf16[1024,256]{1,0:T(8,128)(2,1)}) %reduce-scatter.2.cloned.1.call-update) | async-done | bytes 524304 | tf_op jit(solution)/shard_map/reduce_scatter | solution.py:94
  (50 shorter events, 12.0 us)
Async XLA Ops:
  6.5 168.6 %copy-start = (bf16[256,4096]{1,0:T(8,128)(2,1)S(1)}, bf16[256,4096]{1,0:T(8,128)(2,1)}, u32[]{:S(2)}) copy-start(bf16[256,4096]{1,0:T(8,128)(2,1)} %param.9) | copy-start | bytes 6291460
  11.0 24.5 %all-to-all-start.1 = ((s32[16,1,3]{2,1,0:T(1,128)}), s32[16,1,3]{2,1,0:T(1,128)S(1)}, u32[]{:S(2)}, u32[]{:S(2)}) async-start(s32[16,1,3]{2,1,0:T(1,128)} %bitcast.5), calls=%async_computation.1 | async-start | bytes 16384 | tf_op jit(solution)/shard_map/all_to_all | solution.py:57
  30.3 12.9 %copy-start.1 = (bf16[8,128,2,256]{3,2,1,0:T(2,128)(2,1)S(1)}, bf16[8,128,2,256]{3,2,1,0:T(2,128)(2,1)}, u32[]{:S(2)}) copy-start(bf16[8,128,2,256]{3,2,1,0:T(2,128)(2,1)} %param.10) | copy-start | bytes 3145732
  35.5 54.0 %all-to-all-start = ((bf16[16,3,64,256]{3,2,1,0:T(8,128)(2,1)}), bf16[16,3,64,256]{3,2,1,0:T(8,128)(2,1)}, u32[]{:S(2)}, u32[]{:S(2)}) async-start(bf16[16,3,64,256]{3,2,1,0:T(8,128)(2,1)} %bitcast.68), calls=%async_computation | async-start | bytes 3145728 | tf_op jit(solution)/shard_map/all_to_all | solution.py:54
  97.8 1.7 copy-start.2
  102.2 17.7 %all-to-all-start.2 = ((f32[16,1,768]{2,1,0:T(1,128)}), f32[16,1,768]{2,1,0:T(1,128)S(1)}, u32[]{:S(2)}, u32[]{:S(2)}) async-start(f32[16,1,768]{2,1,0:T(1,128)} %reshape.344), calls=%async_computation.2 | async-start | bytes 98304 | tf_op jit(solution)/shard_map/all_to_all | solution.py:78
  119.9 43.2 %all-to-all-start.3 = ((bf16[16,3,64,256]{3,2,1,0:T(8,128)(2,1)}), bf16[16,3,64,256]{3,2,1,0:T(8,128)(2,1)}, u32[]{:S(2)}, u32[]{:S(2)}) async-start(bf16[16,3,64,256]{3,2,1,0:T(8,128)(2,1)} %reshape.280), calls=%async_computation.3 | async-start | bytes 3145728 | tf_op jit(solution)/shard_map/all_to_all | solution.py:75
  127.5 164.0 %reduce-scatter.2.cloned.1.call-start = ((), (), s32[]{:S(2)}) async-start(), calls=%async_computation.5 | async-start | bytes 8912896 | tf_op jit(solution)/shard_map/reduce_scatter | solution.py:94
Sparse Core Ops, SparseCore 0:
  180.8 110.6 reduce-scatter.1

commit v3 on v2

--- a/solution.py
+++ b/solution.py
@@ -55,6 +55,13 @@
         send_q.reshape(n_seq, CAP, SPAN, row_width), "seq", 0, 0, tiled=True
     ).reshape(places_total, SPAN, heads_here, HD)
     recv_e = lax.all_to_all(send_e.reshape(n_seq, CAP), "seq", 0, 0, tiled=True).reshape(-1)
+    n_db = lax.psum(1, "db")
+    features = output_weight.shape[1] // n_db
+    weight_cols = lax.all_to_all(
+        output_weight.reshape(row_width, n_db, features), "db", 1, 0, tiled=True
+    )
+    weight_cols = weight_cols.reshape(n_db, row_width, features)
+    weight_cols, recv_q = lax.optimization_barrier((weight_cols, recv_q))
 
     blocks = jnp.take(neighbour_kv, recv_e, axis=0)
     blocks = blocks.reshape(places_total, key_len, 2, heads_here, HD)
@@ -90,10 +97,11 @@
     slot_vals = jnp.where(live_k[..., None], slot_ctx.astype(jnp.float32), 0.0)
     context = jnp.sum(share * slot_vals, axis=1)
     context = context.astype(jnp.bfloat16).reshape(tok_rows, row_width)
-    partial_value = jnp.dot(context, output_weight, preferred_element_type=jnp.float32)
-    return lax.psum_scatter(
-        partial_value.astype(jnp.bfloat16), "db", scatter_dimension=1, tiled=True
+    contexts = lax.all_gather(context, "db", axis=0, tiled=False)
+    out = jnp.einsum(
+        "str,srf->tf", contexts, weight_cols, preferred_element_type=jnp.float32
     )
+    return out.astype(jnp.bfloat16)
 
 
 def solution(mesh):

time: 300 us -> 306 us (1.020)
  starting transfers between devices: 32.7 us -> 40.3 us
  local copies, waits for them, and re-layouts: 74 us -> 68.5 us
  waiting for transfers between devices: 142 us -> 147 us
    reduce_scatter x1 -> x0, waiting for transfers between devices: 111 us -> none  [on_device(): lax.psum_scatter(partial_value.astype(jnp.bfloat16), 'db', scatter_dimens...]
    all_gather x0 -> x1, waiting for transfers between devices: none -> 80.1 us  [on_device(): contexts = lax.all_gather(context, 'db', axis=0, tiled=False)]
    all_to_all x1, waiting for transfers between devices: 0.01 us -> 34.2 us  [on_device(): lax.all_to_all(send_q.reshape(n_seq, CAP, SPAN, row_width), 'seq', 0, 0,...]
    all_to_all x0 -> x1, starting transfers between devices: none -> 11.5 us  [on_device(): lax.all_to_all(output_weight.reshape(row_width, n_db, features), 'db', 1,...]
    all_to_all x1, starting transfers between devices: 7.36 us -> 3.68 us  [on_device(): lax.all_to_all(stats.reshape(n_seq, CAP, heads_here, SPAN, 2), 'seq', 0,...]
  transfers between devices with their start and end apart: 5 -> 6, of which waited for: 2 -> 3; matrix products, arithmetic and copies ran while one was open for 25% -> 24% of each run, Pallas kernels for 0% -> 0%
where the time goes in v3:
time: 306 us; the launch traced here: 305 us
  waiting for transfers between devices  147 us (48%)
  local copies, waits for them, and re-layouts  68.5 us (22%)
  starting transfers between devices  40.3 us (13%)
  matrix products  21 us (7%)
  other arithmetic  14.2 us (5%)
  between operations  13.7 us (4%)
    all_gather x1, waiting for transfers between devices, on_device(): contexts = lax.all_gather(context, 'db', axis=0, tiled=False)  80.1 us
    gather x3, local copies, waits for them, and re-layouts, on_device(): blocks = jnp.take(neighbour_kv, recv_e, axis=0)  38.8 us
    all_to_all x1, waiting for transfers between devices, on_device(): lax.all_to_all(send_q.reshape(n_seq, CAP, SPAN, row_width), 'seq', 0, 0,...  34.2 us
    all_to_all x1, waiting for transfers between devices, on_device(): lax.all_to_all(part.astype(jnp.bfloat16).reshape(n_seq, CAP, SPAN, row_wi...  32.7 us
    all_to_all x1, starting transfers between devices, on_device(): lax.all_to_all(output_weight.reshape(row_width, n_db, features), 'db', 1,...  11.5 us
    all_to_all x1, starting transfers between devices, on_device(): lax.all_to_all(send_e.reshape(n_seq, CAP), 'seq', 0, 0, tiled=True)  10 us
    all_to_all x1, starting transfers between devices, on_device(): lax.all_to_all(send_q.reshape(n_seq, CAP, SPAN, row_width), 'seq', 0, 0,...  7.73 us
    all_to_all x1, starting transfers between devices, on_device(): lax.all_to_all(part.astype(jnp.bfloat16).reshape(n_seq, CAP, SPAN, row_wi...  7.3 us
  transfers between devices with their start and end apart: 6, of which 3 were waited for; matrix products, arithmetic and copies ran while one was open for 24% of the time, Pallas kernels for 0%

profile of v3, /device:TPU:1, one launch (start us, length us, event | category | flops | bytes accessed | tf_op | source)
XLA Modules:
  0.0 304.7 jit_solution(16311860538181110165)
XLA Ops:
  11.0 10.0 %all-to-all-start.2 = ((s32[16,1,3]{2,1,0:T(1,128)}), s32[16,1,3]{2,1,0:T(1,128)S(1)}, u32[]{:S(2)}, u32[]{:S(2)}) async-start(s32[16,1,3]{2,1,0:T(1,128)} %bitcast.8), calls=%async_computation.2 | async-start | bytes 16384 | tf_op jit(solution)/shard_map/all_to_all | solution.py:57
  21.1 5.7 %convolution_convert_fusion = bf16[1024,256]{1,0:T(8,128)(2,1)S(1)} fusion(bf16[1024,4096]{1,0:T(8,128)(2,1)} %param.7, bf16[4096,256]{1,0:T(8,128)(2,1)S(1)} %copy-done), kind=kOutput, calls=%fused_computation.25 | convolution fusion | flops 2147745792 | bytes 11010048 | tf_op jit(solution)/shard_map/dot_general | solution.py:42
  28.8 4.6 %scatter_fusion = bf16[48,64,256]{2,1,0:T(8,128)(2,1)} fusion(bf16[48,64,256]{2,1,0:T(8,128)(2,1)} %broadcast_in_dim.86, s32[32]{0:T(128)S(1)} %get-tuple-element.14, bf16[32,64,256]{2,1,0:T(8,128)(2,1)S(1)} %gather_fusion), kind=kCustom, calls=%fused_computation.4 | custom fusion | bytes 3145856 | tf_op jit(solution)/shard_map/scatter | solution.py:51
  33.3 7.7 %all-to-all-start.1 = ((bf16[16,3,64,256]{3,2,1,0:T(8,128)(2,1)}), bf16[16,3,64,256]{3,2,1,0:T(8,128)(2,1)}, u32[]{:S(2)}, u32[]{:S(2)}) async-start(bf16[16,3,64,256]{3,2,1,0:T(8,128)(2,1)} %bitcast.7), calls=%async_computation.1 | async-start | bytes 3145728 | tf_op jit(solution)/shard_map/all_to_all | solution.py:54
  42.6 34.2 %all-to-all-done.1 = bf16[16,3,64,256]{3,2,1,0:T(8,128)(2,1)} async-done(((bf16[16,3,64,256]{3,2,1,0:T(8,128)(2,1)}), bf16[16,3,64,256]{3,2,1,0:T(8,128)(2,1)}, u32[]{:S(2)}, u32[]{:S(2)}) %all-to-all-start.1) | async-done | bytes 1572896 | tf_op jit(solution)/shard_map/all_to_all | solution.py:54
  76.8 11.5 %all-to-all-start = ((bf16[256,16,256]{2,0,1:T(8,128)(2,1)}), bf16[256,16,256]{2,0,1:T(8,128)(2,1)}, u32[]{:S(2)}, u32[]{:S(2)}) async-start(bf16[256,16,256]{2,0,1:T(8,128)(2,1)} %bitcast.77), calls=%async_computation | async-start | bytes 4194304 | tf_op jit(solution)/shard_map/all_to_all | solution.py:60
  88.4 14.3 %gather_fusion.1 = bf16[48,128,2,256]{3,2,1,0:T(2,128)(2,1)} fusion(bf16[8,128,2,256]{3,2,1,0:T(2,128)(2,1)S(1)} %copy-done.2, s32[1024]{0:T(1024)S(1)} %pad_clamp_fusion.1), kind=kCustom, calls=%fused_computation.1 | custom fusion | bytes 12583104 | tf_op jit(solution)/shard_map/jit(_take)/gather | solution.py:66
  102.8 15.8 %copy.57 = bf16[48,128,2,256]{1,3,2,0:T(8,128)(2,1)} copy(bf16[48,128,2,256]{3,2,1,0:T(2,128)(2,1)} %gather_fusion.1) | data formatting | bytes 12582912 | tf_op jit(solution)/shard_map/jit(_take)/gather | solution.py:66
  118.6 8.6 %copy.58 = bf16[48,128,2,2,128]{4,1,3,0,2:T(8,128)(2,1)} copy(bf16[48,128,2,2,128]{1,4,3,2,0:T(8,128)(2,1)} %bitcast.76) | data formatting | bytes 12582912 | tf_op jit(solution)/shard_map/jit(_take)/gather | solution.py:66
  128.5 6.2 %broadcast_select_fusion = bf16[48,128,2,2,128]{4,1,3,0,2:T(8,128)(2,1)} fusion(bf16[48,128,2,2,128]{4,1,3,0,2:T(8,128)(2,1)} %copy.58, pred[48]{0:T(512)(128)(4,1)S(1)} %compare_and_fusion.1), kind=kLoop, calls=%fused_computation.6 | loop fusion | flops 3145728 | bytes 12582960 | tf_op jit(solution)/shard_map/jit(_take)/select_n | solution.py:66
  134.7 2.4 reshape.292
  137.1 4.3 %multiply_reduce_fusion = (f32[48,2,64]{2,1,0:T(2,128)S(1)}, f32[48,2,64,128]{3,2,1,0:T(8,128)S(1)}) fusion(bf16[48,128,2,2,128]{4,1,3,0,2:T(8,128)(2,1)} %broadcast_select_fusion, bf16[48,64,2,128]{3,2,1,0:T(2,128)(2,1)S(1)} %reshape.292), kind=kOutput, calls=%fused_computation.14 | convolution fusion | flops 202893312 | bytes 7888896 | tf_op jit(solution)/shard_map/pqhd,pnhd->phqn/dot_general | solution.py:70
  141.3 1.7 copy-done.3
  143.0 1.9 fusion.4
  145.7 3.7 %all-to-all-start.3 = ((f32[16,1,768]{2,1,0:T(1,128)}), f32[16,1,768]{2,1,0:T(1,128)S(1)}, u32[]{:S(2)}, u32[]{:S(2)}) async-start(f32[16,1,768]{2,1,0:T(1,128)} %reshape.362), calls=%async_computation.3 | async-start | bytes 98304 | tf_op jit(solution)/shard_map/all_to_all | solution.py:85
  149.4 3.8 %fusion.2 = bf16[48,64,2,128]{3,1,2,0:T(8,128)(2,1)S(1)} fusion(bf16[48,128,2,2,128]{4,1,3,0,2:T(8,128)(2,1)} %broadcast_select_fusion, f32[48,2,64,128]{3,2,1,0:T(8,128)} %copy-done.3, f32[48,64,2]{1,2,0:T(2,128)S(1)} %bitcast.85, f32[48,2,64]{2,1,0:T(2,128)S(1)} %get-tuple-element.15), kind=kOutput, calls=%fused_computation.12 | convolution fusion | flops 205258752 | bytes 7913472 | tf_op jit(solution)/shard_map/phqn,pnhd->pqhd/dot_general | solution.py:76
  154.8 2.3 reshape.297
  157.1 7.3 %all-to-all-start.4 = ((bf16[16,3,64,256]{3,2,1,0:T(8,128)(2,1)}), bf16[16,3,64,256]{3,2,1,0:T(8,128)(2,1)S(1)}, u32[]{:S(2)}, u32[]{:S(2)}) async-start(bf16[16,3,64,256]{3,2,1,0:T(8,128)(2,1)} %reshape.297), calls=%async_computation.4 | async-start | bytes 3145728 | tf_op jit(solution)/shard_map/all_to_all | solution.py:82
  167.5 32.7 %all-to-all-done.4 = bf16[16,3,64,256]{3,2,1,0:T(8,128)(2,1)S(1)} async-done(((bf16[16,3,64,256]{3,2,1,0:T(8,128)(2,1)}), bf16[16,3,64,256]{3,2,1,0:T(8,128)(2,1)S(1)}, u32[]{:S(2)}, u32[]{:S(2)}) %all-to-all-start.4) | async-done | bytes 1572896 | tf_op jit(solution)/shard_map/all_to_all | solution.py:82
  200.3 1.9 reshape.298
  202.1 4.1 %gather_fusion.3 = bf16[32,64,2,128]{3,2,1,0:T(2,128)(2,1)S(1)} fusion(bf16[48,64,2,128]{3,2,1,0:T(2,128)(2,1)} %reshape.298, s32[1024]{0:T(1024)S(1)} %pad_clamp_fusion), kind=kCustom, calls=%fused_computation.3 | custom fusion | bytes 2097280 | tf_op jit(solution)/shard_map/jit(_take)/gather | solution.py:89
  206.2 3.2 %multiply_reduce_fusion.1 = bf16[16,64,2,128]{3,2,1,0:T(2,128)(2,1)S(1)} fusion(pred[16,2]{1,0:T(8,128)(4,1)S(1)} %iota_compare_fusion.1, pred[16,2]{1,0:T(8,128)(4,1)S(1)} %compare_and_fusion, f32[16,2,64,2]{3,2,1,0:T(8,128)S(1)} %copy.62, bf16[32,64,2,128]{3,2,1,0:T(2,128)(2,1)S(1)} %gather_fusion.3), kind=kLoop, calls=%fused_computation.18 | loop fusion | flops 2359296 | bytes 1589312 | tf_op jit(solution)/shard_map/reduce_sum | solution.py:98
  210.5 80.1 %all-gather.2.cloned.1.call-done = bf16[16,1024,256]{2,1,0:T(8,128)(2,1)} async-done(((bf16[1,1024,256]{2,1,0:T(8,128)(2,1)}), bf16[16,1024,256]{2,1,0:T(8,128)(2,1)}) %all-gather.2.cloned.1.call-update) | async-done | bytes 8388624 | tf_op jit(solution)/shard_map/all_gather | solution.py:100
  290.6 7.2 %fusion.9 = bf16[1024,256]{1,0:T(8,128)(2,1)} fusion(bf16[16,1024,256]{2,1,0:T(8,128)(2,1)} %all-gather.2.cloned.1.call-done, bf16[16,256,256]{2,1,0:T(8,128)(2,1)} %bitcast.2), kind=kOutput, calls=%fused_computation.24 | convolution fusion | flops 2147745792 | bytes 11010048 | tf_op jit(solution)/shard_map/str,srf->tf/dot_general | solution.py:101
  (58 shorter events, 15.9 us)
Async XLA Ops:
  6.5 14.5 %copy-start = (bf16[4096,256]{1,0:T(8,128)(2,1)S(1)}, bf16[4096,256]{1,0:T(8,128)(2,1)}, u32[]{:S(2)}) copy-start(bf16[4096,256]{1,0:T(8,128)(2,1)} %param.8) | copy-start | bytes 6291460
  11.0 22.3 %all-to-all-start.2 = ((s32[16,1,3]{2,1,0:T(1,128)}), s32[16,1,3]{2,1,0:T(1,128)S(1)}, u32[]{:S(2)}, u32[]{:S(2)}) async-start(s32[16,1,3]{2,1,0:T(1,128)} %bitcast.8), calls=%async_computation.2 | async-start | bytes 16384 | tf_op jit(solution)/shard_map/all_to_all | solution.py:57
  33.3 7.7 %copy-start.4 = (bf16[256,4096]{1,0:T(8,128)(2,1)S(1)}, bf16[256,4096]{1,0:T(8,128)(2,1)}, u32[]{:S(2)}) copy-start(bf16[256,4096]{1,0:T(8,128)(2,1)} %param.9) | copy-start | bytes 6291460
  33.3 43.4 %all-to-all-start.1 = ((bf16[16,3,64,256]{3,2,1,0:T(8,128)(2,1)}), bf16[16,3,64,256]{3,2,1,0:T(8,128)(2,1)}, u32[]{:S(2)}, u32[]{:S(2)}) async-start(bf16[16,3,64,256]{3,2,1,0:T(8,128)(2,1)} %bitcast.7), calls=%async_computation.1 | async-start | bytes 3145728 | tf_op jit(solution)/shard_map/all_to_all | solution.py:54
  42.6 45.8 %copy-start.2 = (bf16[8,128,2,256]{3,2,1,0:T(2,128)(2,1)S(1)}, bf16[8,128,2,256]{3,2,1,0:T(2,128)(2,1)}, u32[]{:S(2)}) copy-start(bf16[8,128,2,256]{3,2,1,0:T(2,128)(2,1)} %param.10) | copy-start | bytes 3145732
  76.8 60.3 %all-to-all-start = ((bf16[256,16,256]{2,0,1:T(8,128)(2,1)}), bf16[256,16,256]{2,0,1:T(8,128)(2,1)}, u32[]{:S(2)}, u32[]{:S(2)}) async-start(bf16[256,16,256]{2,0,1:T(8,128)(2,1)} %bitcast.77), calls=%async_computation | async-start | bytes 4194304 | tf_op jit(solution)/shard_map/all_to_all | solution.py:60
  141.3 1.7 copy-start.3
  145.7 11.4 %all-to-all-start.3 = ((f32[16,1,768]{2,1,0:T(1,128)}), f32[16,1,768]{2,1,0:T(1,128)S(1)}, u32[]{:S(2)}, u32[]{:S(2)}) async-start(f32[16,1,768]{2,1,0:T(1,128)} %reshape.362), calls=%async_computation.3 | async-start | bytes 98304 | tf_op jit(solution)/shard_map/all_to_all | solution.py:85
  157.1 43.2 %all-to-all-start.4 = ((bf16[16,3,64,256]{3,2,1,0:T(8,128)(2,1)}), bf16[16,3,64,256]{3,2,1,0:T(8,128)(2,1)S(1)}, u32[]{:S(2)}, u32[]{:S(2)}) async-start(bf16[16,3,64,256]{3,2,1,0:T(8,128)(2,1)} %reshape.297), calls=%async_computation.4 | async-start | bytes 3145728 | tf_op jit(solution)/shard_map/all_to_all | solution.py:82
  164.4 126.2 %all-gather.2.cloned.1.call-start = ((), (), s32[]{:S(2)}) async-start(), calls=%async_computation.5 | async-start | bytes 8912896 | tf_op jit(solution)/shard_map/all_gather | solution.py:100
  290.6 7.3 %copy-start.1 = (bf16[4096,256]{1,0:T(8,128)(2,1)S(1)}, bf16[4096,256]{1,0:T(8,128)(2,1)}, u32[]{:S(2)}) copy-start(bf16[4096,256]{1,0:T(8,128)(2,1)} %param.8) | copy-start | bytes 6291460
Sparse Core Ops, SparseCore 0:
  210.7 79.9 all-gather.1

commit v4 on v3

--- a/solution.py
+++ b/solution.py
@@ -61,7 +61,6 @@
         output_weight.reshape(row_width, n_db, features), "db", 1, 0, tiled=True
     )
     weight_cols = weight_cols.reshape(n_db, row_width, features)
-    weight_cols, recv_q = lax.optimization_barrier((weight_cols, recv_q))
 
     blocks = jnp.take(neighbour_kv, recv_e, axis=0)
     blocks = blocks.reshape(places_total, key_len, 2, heads_here, HD)
@@ -78,6 +77,7 @@
         preferred_element_type=jnp.float32,
     )
     part = part / jnp.transpose(total, (0, 2, 1, 3))
+    weight_cols, part = lax.optimization_barrier((weight_cols, part))
     stats = jnp.concatenate([top, total], axis=3)
     back_ctx = lax.all_to_all(
         part.astype(jnp.bfloat16).reshape(n_seq, CAP, SPAN, row_width), "seq", 0, 0, tiled=True

time: 306 us -> 306 us (level)
  transfers between devices with their start and end apart: 6 -> 6, of which waited for: 3 -> 3; matrix products, arithmetic and copies ran while one was open for 24% -> 26% of each run, Pallas kernels for 0% -> 0%
where the time goes in v4:
time: 306 us; the launch traced here: 305 us
  waiting for transfers between devices  147 us (48%)
  local copies, waits for them, and re-layouts  68.5 us (22%)
  starting transfers between devices  40.3 us (13%)
  matrix products  21 us (7%)
  other arithmetic  14.2 us (5%)
  between operations  13.7 us (4%)
    all_gather x1, waiting for transfers between devices, on_device(): contexts = lax.all_gather(context, 'db', axis=0, tiled=False)  80.1 us
    gather x3, local copies, waits for them, and re-layouts, on_device(): blocks = jnp.take(neighbour_kv, recv_e, axis=0)  38.8 us
    all_to_all x1, waiting for transfers between devices, on_device(): lax.all_to_all(send_q.reshape(n_seq, CAP, SPAN, row_width), 'seq', 0, 0,...  34.2 us
    all_to_all x1, waiting for transfers between devices, on_device(): lax.all_to_all(part.astype(jnp.bfloat16).reshape(n_seq, CAP, SPAN, row_wi...  32.7 us
    all_to_all x1, starting transfers between devices, on_device(): lax.all_to_all(output_weight.reshape(row_width, n_db, features), 'db', 1,...  11.5 us
    all_to_all x1, starting transfers between devices, on_device(): lax.all_to_all(send_e.reshape(n_seq, CAP), 'seq', 0, 0, tiled=True)  10 us
    all_to_all x1, starting transfers between devices, on_device(): lax.all_to_all(send_q.reshape(n_seq, CAP, SPAN, row_width), 'seq', 0, 0,...  7.7 us
    all_to_all x1, starting transfers between devices, on_device(): lax.all_to_all(part.astype(jnp.bfloat16).reshape(n_seq, CAP, SPAN, row_wi...  7.3 us
  transfers between devices with their start and end apart: 6, of which 3 were waited for; matrix products, arithmetic and copies ran while one was open for 26% of the time, Pallas kernels for 0%

profile of v4, /device:TPU:1, one launch (start us, length us, event | category | flops | bytes accessed | tf_op | source)
XLA Modules:
  0.0 304.7 jit_solution(16310530912846331193)
XLA Ops:
  11.0 10.0 %all-to-all-start.1 = ((s32[16,1,3]{2,1,0:T(1,128)}), s32[16,1,3]{2,1,0:T(1,128)S(1)}, u32[]{:S(2)}, u32[]{:S(2)}) async-start(s32[16,1,3]{2,1,0:T(1,128)} %bitcast.5), calls=%async_computation.1 | async-start | bytes 16384 | tf_op jit(solution)/shard_map/all_to_all | solution.py:57
  21.1 5.7 %convolution_convert_fusion = bf16[1024,256]{1,0:T(8,128)(2,1)S(1)} fusion(bf16[1024,4096]{1,0:T(8,128)(2,1)} %param.7, bf16[4096,256]{1,0:T(8,128)(2,1)S(1)} %copy-done), kind=kOutput, calls=%fused_computation.24 | convolution fusion | flops 2147745792 | bytes 11010048 | tf_op jit(solution)/shard_map/dot_general | solution.py:42
  28.8 4.6 %scatter_fusion = bf16[48,64,256]{2,1,0:T(8,128)(2,1)} fusion(bf16[48,64,256]{2,1,0:T(8,128)(2,1)} %broadcast_in_dim.86, s32[32]{0:T(128)S(1)} %get-tuple-element.14, bf16[32,64,256]{2,1,0:T(8,128)(2,1)S(1)} %gather_fusion), kind=kCustom, calls=%fused_computation.4 | custom fusion | bytes 3145856 | tf_op jit(solution)/shard_map/scatter | solution.py:51
  33.3 7.7 %all-to-all-start = ((bf16[16,3,64,256]{3,2,1,0:T(8,128)(2,1)}), bf16[16,3,64,256]{3,2,1,0:T(8,128)(2,1)}, u32[]{:S(2)}, u32[]{:S(2)}) async-start(bf16[16,3,64,256]{3,2,1,0:T(8,128)(2,1)} %bitcast.4), calls=%async_computation | async-start | bytes 3145728 | tf_op jit(solution)/shard_map/all_to_all | solution.py:54
  42.6 34.2 %all-to-all-done = bf16[16,3,64,256]{3,2,1,0:T(8,128)(2,1)} async-done(((bf16[16,3,64,256]{3,2,1,0:T(8,128)(2,1)}), bf16[16,3,64,256]{3,2,1,0:T(8,128)(2,1)}, u32[]{:S(2)}, u32[]{:S(2)}) %all-to-all-start) | async-done | bytes 1572896 | tf_op jit(solution)/shard_map/all_to_all | solution.py:54
  76.8 11.5 %all-to-all-start.3 = ((bf16[256,16,256]{2,0,1:T(8,128)(2,1)}), bf16[256,16,256]{2,0,1:T(8,128)(2,1)}, u32[]{:S(2)}, u32[]{:S(2)}) async-start(bf16[256,16,256]{2,0,1:T(8,128)(2,1)} %bitcast.75), calls=%async_computation.3 | async-start | bytes 4194304 | tf_op jit(solution)/shard_map/all_to_all | solution.py:60
  88.4 14.3 %gather_fusion.1 = bf16[48,128,2,256]{3,2,1,0:T(2,128)(2,1)} fusion(bf16[8,128,2,256]{3,2,1,0:T(2,128)(2,1)S(1)} %copy-done.2, s32[1024]{0:T(1024)S(1)} %pad_clamp_fusion.1), kind=kCustom, calls=%fused_computation.1 | custom fusion | bytes 12583104 | tf_op jit(solution)/shard_map/jit(_take)/gather | solution.py:65
  102.7 15.8 %copy.56 = bf16[48,128,2,256]{1,3,2,0:T(8,128)(2,1)} copy(bf16[48,128,2,256]{3,2,1,0:T(2,128)(2,1)} %gather_fusion.1) | data formatting | bytes 12582912 | tf_op jit(solution)/shard_map/jit(_take)/gather | solution.py:65
  118.6 8.6 %copy.57 = bf16[48,128,2,2,128]{4,1,3,0,2:T(8,128)(2,1)} copy(bf16[48,128,2,2,128]{1,4,3,2,0:T(8,128)(2,1)} %bitcast.74) | data formatting | bytes 12582912 | tf_op jit(solution)/shard_map/jit(_take)/gather | solution.py:65
  128.5 6.2 %broadcast_select_fusion = bf16[48,128,2,2,128]{4,1,3,0,2:T(8,128)(2,1)} fusion(bf16[48,128,2,2,128]{4,1,3,0,2:T(8,128)(2,1)} %copy.57, pred[48]{0:T(512)(128)(4,1)S(1)} %compare_and_fusion.1), kind=kLoop, calls=%fused_computation.6 | loop fusion | flops 3145728 | bytes 12582960 | tf_op jit(solution)/shard_map/jit(_take)/select_n | solution.py:65
  134.7 2.4 reshape.290
  137.0 4.3 %multiply_reduce_fusion = (f32[48,2,64]{2,1,0:T(2,128)S(1)}, f32[48,2,64,128]{3,2,1,0:T(8,128)S(1)}) fusion(bf16[48,128,2,2,128]{4,1,3,0,2:T(8,128)(2,1)} %broadcast_select_fusion, bf16[48,64,2,128]{3,2,1,0:T(2,128)(2,1)S(1)} %reshape.290), kind=kOutput, calls=%fused_computation.13 | convolution fusion | flops 202893312 | bytes 7888896 | tf_op jit(solution)/shard_map/pqhd,pnhd->phqn/dot_general | solution.py:69
  141.3 1.7 copy-done.3
  143.0 1.9 fusion.3
  145.7 3.7 %all-to-all-start.2 = ((f32[16,1,768]{2,1,0:T(1,128)}), f32[16,1,768]{2,1,0:T(1,128)S(1)}, u32[]{:S(2)}, u32[]{:S(2)}) async-start(f32[16,1,768]{2,1,0:T(1,128)} %reshape.362), calls=%async_computation.2 | async-start | bytes 98304 | tf_op jit(solution)/shard_map/all_to_all | solution.py:85
  149.4 3.8 %bitcast_divide_fusion = bf16[48,64,2,128]{3,1,2,0:T(8,128)(2,1)S(1)} fusion(bf16[48,128,2,2,128]{4,1,3,0,2:T(8,128)(2,1)} %broadcast_select_fusion, f32[48,2,64,128]{3,2,1,0:T(8,128)} %copy-done.3, f32[48,64,2]{1,2,0:T(2,128)S(1)} %bitcast.83, f32[48,2,64]{2,1,0:T(2,128)S(1)} %get-tuple-element.15), kind=kOutput, calls=%fused_computation.11 | convolution fusion | flops 205258752 | bytes 7913472 | tf_op jit(solution)/shard_map/phqn,pnhd->pqhd/dot_general | solution.py:75
  154.8 2.3 reshape.297
  157.1 7.3 %all-to-all-start.4 = ((bf16[16,3,64,256]{3,2,1,0:T(8,128)(2,1)}), bf16[16,3,64,256]{3,2,1,0:T(8,128)(2,1)S(1)}, u32[]{:S(2)}, u32[]{:S(2)}) async-start(bf16[16,3,64,256]{3,2,1,0:T(8,128)(2,1)} %reshape.297), calls=%async_computation.4 | async-start | bytes 3145728 | tf_op jit(solution)/shard_map/all_to_all | solution.py:82
  167.5 32.7 %all-to-all-done.4 = bf16[16,3,64,256]{3,2,1,0:T(8,128)(2,1)S(1)} async-done(((bf16[16,3,64,256]{3,2,1,0:T(8,128)(2,1)}), bf16[16,3,64,256]{3,2,1,0:T(8,128)(2,1)S(1)}, u32[]{:S(2)}, u32[]{:S(2)}) %all-to-all-start.4) | async-done | bytes 1572896 | tf_op jit(solution)/shard_map/all_to_all | solution.py:82
  200.2 1.9 reshape.298
  202.1 4.1 %gather_fusion.3 = bf16[32,64,2,128]{3,2,1,0:T(2,128)(2,1)S(1)} fusion(bf16[48,64,2,128]{3,2,1,0:T(2,128)(2,1)} %reshape.298, s32[1024]{0:T(1024)S(1)} %pad_clamp_fusion), kind=kCustom, calls=%fused_computation.3 | custom fusion | bytes 2097280 | tf_op jit(solution)/shard_map/jit(_take)/gather | solution.py:89
  206.2 3.2 %multiply_reduce_fusion.1 = bf16[16,64,2,128]{3,2,1,0:T(2,128)(2,1)S(1)} fusion(pred[16,2]{1,0:T(8,128)(4,1)S(1)} %iota_compare_fusion.1, pred[16,2]{1,0:T(8,128)(4,1)S(1)} %compare_and_fusion, f32[16,2,64,2]{3,2,1,0:T(8,128)S(1)} %copy.61, bf16[32,64,2,128]{3,2,1,0:T(2,128)(2,1)S(1)} %gather_fusion.3), kind=kLoop, calls=%fused_computation.17 | loop fusion | flops 2359296 | bytes 1589312 | tf_op jit(solution)/shard_map/reduce_sum | solution.py:98
  210.5 80.1 %all-gather.2.cloned.1.call-done = bf16[16,1024,256]{2,1,0:T(8,128)(2,1)} async-done(((bf16[1,1024,256]{2,1,0:T(8,128)(2,1)}), bf16[16,1024,256]{2,1,0:T(8,128)(2,1)}) %all-gather.2.cloned.1.call-update) | async-done | bytes 8388624 | tf_op jit(solution)/shard_map/all_gather | solution.py:100
  290.6 7.2 %fusion.8 = bf16[1024,256]{1,0:T(8,128)(2,1)} fusion(bf16[16,1024,256]{2,1,0:T(8,128)(2,1)} %all-gather.2.cloned.1.call-done, bf16[16,256,256]{2,1,0:T(8,128)(2,1)} %bitcast.19), kind=kOutput, calls=%fused_computation.23 | convolution fusion | flops 2147745792 | bytes 11010048 | tf_op jit(solution)/shard_map/str,srf->tf/dot_general | solution.py:101
  (58 shorter events, 15.9 us)
Async XLA Ops:
  6.5 14.5 %copy-start = (bf16[4096,256]{1,0:T(8,128)(2,1)S(1)}, bf16[4096,256]{1,0:T(8,128)(2,1)}, u32[]{:S(2)}) copy-start(bf16[4096,256]{1,0:T(8,128)(2,1)} %param.8) | copy-start | bytes 6291460
  11.0 22.4 %all-to-all-start.1 = ((s32[16,1,3]{2,1,0:T(1,128)}), s32[16,1,3]{2,1,0:T(1,128)S(1)}, u32[]{:S(2)}, u32[]{:S(2)}) async-start(s32[16,1,3]{2,1,0:T(1,128)} %bitcast.5), calls=%async_computation.1 | async-start | bytes 16384 | tf_op jit(solution)/shard_map/all_to_all | solution.py:57
  33.3 7.7 %copy-start.4 = (bf16[256,4096]{1,0:T(8,128)(2,1)S(1)}, bf16[256,4096]{1,0:T(8,128)(2,1)}, u32[]{:S(2)}) copy-start(bf16[256,4096]{1,0:T(8,128)(2,1)} %param.9) | copy-start | bytes 6291460
  33.3 43.4 %all-to-all-start = ((bf16[16,3,64,256]{3,2,1,0:T(8,128)(2,1)}), bf16[16,3,64,256]{3,2,1,0:T(8,128)(2,1)}, u32[]{:S(2)}, u32[]{:S(2)}) async-start(bf16[16,3,64,256]{3,2,1,0:T(8,128)(2,1)} %bitcast.4), calls=%async_computation | async-start | bytes 3145728 | tf_op jit(solution)/shard_map/all_to_all | solution.py:54
  42.6 45.8 %copy-start.2 = (bf16[8,128,2,256]{3,2,1,0:T(2,128)(2,1)S(1)}, bf16[8,128,2,256]{3,2,1,0:T(2,128)(2,1)}, u32[]{:S(2)}) copy-start(bf16[8,128,2,256]{3,2,1,0:T(2,128)(2,1)} %param.10) | copy-start | bytes 3145732
  76.8 68.9 %all-to-all-start.3 = ((bf16[256,16,256]{2,0,1:T(8,128)(2,1)}), bf16[256,16,256]{2,0,1:T(8,128)(2,1)}, u32[]{:S(2)}, u32[]{:S(2)}) async-start(bf16[256,16,256]{2,0,1:T(8,128)(2,1)} %bitcast.75), calls=%async_computation.3 | async-start | bytes 4194304 | tf_op jit(solution)/shard_map/all_to_all | solution.py:60
  141.3 1.7 copy-start.3
  145.7 11.4 %all-to-all-start.2 = ((f32[16,1,768]{2,1,0:T(1,128)}), f32[16,1,768]{2,1,0:T(1,128)S(1)}, u32[]{:S(2)}, u32[]{:S(2)}) async-start(f32[16,1,768]{2,1,0:T(1,128)} %reshape.362), calls=%async_computation.2 | async-start | bytes 98304 | tf_op jit(solution)/shard_map/all_to_all | solution.py:85
  157.1 43.2 %all-to-all-start.4 = ((bf16[16,3,64,256]{3,2,1,0:T(8,128)(2,1)}), bf16[16,3,64,256]{3,2,1,0:T(8,128)(2,1)S(1)}, u32[]{:S(2)}, u32[]{:S(2)}) async-start(bf16[16,3,64,256]{3,2,1,0:T(8,128)(2,1)} %reshape.297), calls=%async_computation.4 | async-start | bytes 3145728 | tf_op jit(solution)/shard_map/all_to_all | solution.py:82
  164.4 126.2 %all-gather.2.cloned.1.call-start = ((), (), s32[]{:S(2)}) async-start(), calls=%async_computation.5 | async-start | bytes 8912896 | tf_op jit(solution)/shard_map/all_gather | solution.py:100
  290.6 7.3 %copy-start.1 = (bf16[4096,256]{1,0:T(8,128)(2,1)S(1)}, bf16[4096,256]{1,0:T(8,128)(2,1)}, u32[]{:S(2)}) copy-start(bf16[4096,256]{1,0:T(8,128)(2,1)} %param.8) | copy-start | bytes 6291460
Sparse Core Ops, SparseCore 0:
  210.6 79.9 all-gather.1

commit v5 on v4

--- a/solution.py
+++ b/solution.py
@@ -1,14 +1,19 @@
+import functools
 import math
 
 import jax
 import jax.numpy as jnp
 from jax import lax
+from jax.experimental import pallas as pl
+from jax.experimental.pallas import tpu as pltpu
 from jax.sharding import PartitionSpec as P
 
 HD = 128
 SPAN = 64
 K = 2
 CAP = 3
+LANES = 128
+MESH = pl.DeviceIdType.MESH
 
 
 def slot_places(neighbour_shard, neighbour_count):
@@ -21,6 +26,151 @@
     earlier = jnp.arange(slots)[None, :] < jnp.arange(slots)[:, None]
     own_rank = jnp.minimum(jnp.sum((same & earlier).astype(jnp.int32), axis=1), CAP - 1)
     return own_live, own_shard * CAP + own_rank
+
+
+def peer_copy(src, dst, send_sem, recv_sem, device):
+    return pltpu.make_async_remote_copy(
+        src_ref=src, dst_ref=dst, send_sem=send_sem, recv_sem=recv_sem,
+        device_id=device, device_id_type=MESH,
+    )
+
+
+def out_kernel(n_seq, n_db, features, send_q, send_e, w_loc, recv_q, recv_e, w_cols,
+               qs, qr, es, er, ws, wr, ls):
+    me_s = lax.axis_index("seq")
+    me_d = lax.axis_index("db")
+
+    def w_src(d):
+        return w_loc.at[:, pl.ds(pl.multiple_of(d * features, features), features)]
+
+    barrier = pltpu.get_barrier_semaphore()
+
+    @pl.loop(1, n_seq)
+    def _(o):
+        pl.semaphore_signal(barrier, inc=1, device_id=(lax.rem(me_s + o, n_seq), me_d),
+                            device_id_type=MESH)
+
+    @pl.loop(1, n_db)
+    def _(o):
+        pl.semaphore_signal(barrier, inc=1, device_id=(me_s, lax.rem(me_d + o, n_db)),
+                            device_id_type=MESH)
+
+    pl.semaphore_wait(barrier, (n_seq - 1) + (n_db - 1))
+
+    own = [
+        pltpu.make_async_copy(send_q.at[me_s], recv_q.at[me_s], ls.at[0]),
+        pltpu.make_async_copy(send_e.at[me_s], recv_e.at[me_s], ls.at[1]),
+        pltpu.make_async_copy(w_src(me_d), w_cols.at[me_d], ls.at[2]),
+    ]
+    for c in own:
+        c.start()
+
+    @pl.loop(1, n_db)
+    def _(o):
+        d = lax.rem(me_d + o, n_db)
+        peer_copy(w_src(d), w_cols.at[me_d], ws.at[d], wr.at[me_d], (me_s, d)).start()
+
+    @pl.loop(1, n_seq)
+    def _(o):
+        d = lax.rem(me_s + o, n_seq)
+        peer_copy(send_e.at[d], recv_e.at[me_s], es.at[d], er.at[me_s], (d, me_d)).start()
+        peer_copy(send_q.at[d], recv_q.at[me_s], qs.at[d], qr.at[me_s], (d, me_d)).start()
+
+    for c in own:
+        c.wait()
+
+    @pl.loop(1, n_seq)
+    def _(o):
+        d = lax.rem(me_s + o, n_seq)
+        s = lax.rem(me_s + n_seq - o, n_seq)
+        peer_copy(send_e.at[d], recv_e.at[me_s], es.at[d], er.at[me_s], (d, me_d)).wait_send()
+        peer_copy(send_q.at[d], recv_q.at[me_s], qs.at[d], qr.at[me_s], (d, me_d)).wait_send()
+        peer_copy(send_e.at[me_s], recv_e.at[s], es.at[s], er.at[s], (s, me_d)).wait_recv()
+        peer_copy(send_q.at[me_s], recv_q.at[s], qs.at[s], qr.at[s], (s, me_d)).wait_recv()
+
+    @pl.loop(1, n_db)
+    def _(o):
+        d = lax.rem(me_d + o, n_db)
+        s = lax.rem(me_d + n_db - o, n_db)
+        peer_copy(w_src(d), w_cols.at[me_d], ws.at[d], wr.at[me_d], (me_s, d)).wait_send()
+        peer_copy(w_src(me_d), w_cols.at[s], ws.at[s], wr.at[s], (me_s, s)).wait_recv()
+
+
+def back_kernel(n_seq, ctx, stats, back_ctx, back_stats, cs, cr, ss, sr, ls):
+    me_s = lax.axis_index("seq")
+    me_d = lax.axis_index("db")
+    barrier = pltpu.get_barrier_semaphore()
+
+    @pl.loop(1, n_seq)
+    def _(o):
+        pl.semaphore_signal(barrier, inc=1, device_id=(lax.rem(me_s + o, n_seq), me_d),
+                            device_id_type=MESH)
+
+    pl.semaphore_wait(barrier, n_seq - 1)
+
+    own = [
+        pltpu.make_async_copy(ctx.at[me_s], back_ctx.at[me_s], ls.at[0]),
+        pltpu.make_async_copy(stats.at[me_s], back_stats.at[me_s], ls.at[1]),
+    ]
+    for c in own:
+        c.start()
+
+    @pl.loop(1, n_seq)
+    def _(o):
+        d = lax.rem(me_s + o, n_seq)
+        peer_copy(stats.at[d], back_stats.at[me_s], ss.at[d], sr.at[me_s], (d, me_d)).start()
+        peer_copy(ctx.at[d], back_ctx.at[me_s], cs.at[d], cr.at[me_s], (d, me_d)).start()
+
+    for c in own:
+        c.wait()
+
+    @pl.loop(1, n_seq)
+    def _(o):
+        d = lax.rem(me_s + o, n_seq)
+        s = lax.rem(me_s + n_seq - o, n_seq)
+        peer_copy(stats.at[d], back_stats.at[me_s], ss.at[d], sr.at[me_s], (d, me_d)).wait_send()
+        peer_copy(ctx.at[d], back_ctx.at[me_s], cs.at[d], cr.at[me_s], (d, me_d)).wait_send()
+        peer_copy(stats.at[me_s], back_stats.at[s], ss.at[s], sr.at[s], (s, me_d)).wait_recv()
+        peer_copy(ctx.at[me_s], back_ctx.at[s], cs.at[s], cr.at[s], (s, me_d)).wait_recv()
+
+
+def any_spec():
+    return pl.BlockSpec(memory_space=pl.ANY)
+
+
+def exchange_out(send_q, send_e, w_loc, n_seq, n_db):
+    features = w_loc.shape[1] // n_db
+    dma = pltpu.SemaphoreType.DMA
+    return pl.pallas_call(
+        functools.partial(out_kernel, n_seq, n_db, features),
+        out_shape=(
+            jax.ShapeDtypeStruct(send_q.shape, send_q.dtype),
+            jax.ShapeDtypeStruct(send_e.shape, send_e.dtype),
+            jax.ShapeDtypeStruct((n_db, w_loc.shape[0], features), w_loc.dtype),
+        ),
+        in_specs=[any_spec()] * 3,
+        out_specs=(any_spec(), any_spec(), any_spec()),
+        scratch_shapes=[
+            dma((n_seq,)), dma((n_seq,)), dma((n_seq,)), dma((n_seq,)),
+            dma((n_db,)), dma((n_db,)), dma((3,)),
+        ],
+        compiler_params=pltpu.CompilerParams(collective_id=0, has_side_effects=True),
+    )(send_q, send_e, w_loc)
+
+
+def exchange_back(ctx, stats, n_seq):
+    dma = pltpu.SemaphoreType.DMA
+    return pl.pallas_call(
+        functools.partial(back_kernel, n_seq),
+        out_shape=(
+            jax.ShapeDtypeStruct(ctx.shape, ctx.dtype),
+            jax.ShapeDtypeStruct(stats.shape, stats.dtype),
+        ),
+        in_specs=[any_spec()] * 2,
+        out_specs=(any_spec(), any_spec()),
+        scratch_shapes=[dma((n_seq,)), dma((n_seq,)), dma((n_seq,)), dma((n_seq,)), dma((2,))],
+        compiler_params=pltpu.CompilerParams(collective_id=1, has_side_effects=True),
+    )(ctx, stats)
 
 
 def on_device(
@@ -38,6 +188,7 @@
     heads_here = row_width // HD
     key_len = neighbour_kv.shape[1]
     n_seq = lax.psum(1, "seq")
+    n_db = lax.psum(1, "db")
     places_total = n_seq * CAP
     queries = jnp.dot(decoder_states, query_weight, preferred_element_type=jnp.float32).astype(
         jnp.bfloat16
@@ -51,16 +202,12 @@
     send_q = send_q.at[target].set(queries[span_of_slot], mode="drop")
     send_e = jnp.zeros((places_total,), jnp.int32)
     send_e = send_e.at[target].set(neighbour_entry.reshape(-1), mode="drop")
-    recv_q = lax.all_to_all(
-        send_q.reshape(n_seq, CAP, SPAN, row_width), "seq", 0, 0, tiled=True
-    ).reshape(places_total, SPAN, heads_here, HD)
-    recv_e = lax.all_to_all(send_e.reshape(n_seq, CAP), "seq", 0, 0, tiled=True).reshape(-1)
-    n_db = lax.psum(1, "db")
-    features = output_weight.shape[1] // n_db
-    weight_cols = lax.all_to_all(
-        output_weight.reshape(row_width, n_db, features), "db", 1, 0, tiled=True
-    )
-    weight_cols = weight_cols.reshape(n_db, row_width, features)
+    send_e = jnp.pad(send_e.reshape(n_seq, CAP), ((0, 0), (0, LANES - CAP)))
+    recv_q, recv_e, weight_cols = exchange_out(
+        send_q.reshape(n_seq, CAP, SPAN, row_width), send_e, output_weight, n_seq, n_db
+    )
+    recv_q = recv_q.reshape(places_total, SPAN, heads_here, HD)
+    recv_e = recv_e[:, :CAP].reshape(-1)
 
     blocks = jnp.take(neighbour_kv, recv_e, axis=0)
     blocks = blocks.reshape(places_total, key_len, 2, heads_here, HD)
@@ -77,14 +224,14 @@
         preferred_element_type=jnp.float32,
     )
     part = part / jnp.transpose(total, (0, 2, 1, 3))
-    weight_cols, part = lax.optimization_barrier((weight_cols, part))
     stats = jnp.concatenate([top, total], axis=3)
-    back_ctx = lax.all_to_all(
-        part.astype(jnp.bfloat16).reshape(n_seq, CAP, SPAN, row_width), "seq", 0, 0, tiled=True
-    ).reshape(places_total, SPAN, heads_here, HD)
-    back_stats = lax.all_to_all(
-        stats.reshape(n_seq, CAP, heads_here, SPAN, 2), "seq", 0, 0, tiled=True
-    ).reshape(places_total, heads_here, SPAN, 2)
+    back_ctx, back_stats = exchange_back(
+        part.astype(jnp.bfloat16).reshape(n_seq, CAP, SPAN, row_width),
+        stats.reshape(n_seq, CAP * heads_here * SPAN * 2 // LANES, LANES),
+        n_seq,
+    )
+    back_ctx = back_ctx.reshape(places_total, SPAN, heads_here, HD)
+    back_stats = back_stats.reshape(places_total, heads_here, SPAN, 2)
 
     slot_ctx = jnp.take(back_ctx, place, axis=0).reshape(span_total, K, SPAN, heads_here, HD)
     slot_stats = jnp.take(back_stats, place, axis=0).reshape(span_total, K, heads_here, SPAN, 2)
@@ -97,6 +244,7 @@
     slot_vals = jnp.where(live_k[..., None], slot_ctx.astype(jnp.float32), 0.0)
     context = jnp.sum(share * slot_vals, axis=1)
     context = context.astype(jnp.bfloat16).reshape(tok_rows, row_width)
+
     contexts = lax.all_gather(context, "db", axis=0, tiled=False)
     out = jnp.einsum(
         "str,srf->tf", contexts, weight_cols, preferred_element_type=jnp.float32

time: 306 us -> 293 us (0.958)
  Pallas kernels: 0 us -> 93 us
  waiting for transfers between devices: 147 us -> 79.3 us
  starting transfers between devices: 40.3 us -> 0.01 us
  local copies, waits for them, and re-layouts: 68.5 us -> 77.2 us
  other arithmetic: 14.2 us -> 10.9 us
    pallas_call x0 -> x2, Pallas kernels: none -> 93 us  [the longest x1 49.5 us: exchange_out(): pl.pallas_call(functools.partial(out_kernel, n_seq, n_db, features), out_...]
    all_to_all x5 -> x0, waiting for transfers between devices: 66.9 us -> none  [the longest x1 34.2 us: on_device(): lax.all_to_all(send_q.reshape(n_seq, CAP, SPAN, row_width), 'seq', 0, 0,...]
    all_to_all x5 -> x0, starting transfers between devices: 40.3 us -> none  [the longest x1 11.5 us: on_device(): lax.all_to_all(output_weight.reshape(row_width, n_db, features), 'db', 1,...]
    reshape x5 -> x7, local copies, waits for them, and re-layouts: 5.92 us -> 16.3 us  [the longest x1 4.84 us: on_device(): back_stats = back_stats.reshape(places_total, heads_here, SPAN, 2)]
  transfers between devices with their start and end apart: 6 -> 1, of which waited for: 3 -> 1; matrix products, arithmetic and copies ran while one was open for 26% -> 0% of each run, Pallas kernels for 0% -> 0%
where the time goes in v5:
time: 293 us; the launch traced here: 292 us
  Pallas kernels  93 us (32%)
  waiting for transfers between devices  79.3 us (27%)
  local copies, waits for them, and re-layouts  77.2 us (26%)
  matrix products  18.4 us (6%)
  between operations  13.7 us (5%)
  other arithmetic  10.9 us (4%)
    all_gather x1, waiting for transfers between devices, on_device(): contexts = lax.all_gather(context, 'db', axis=0, tiled=False)  79.3 us
    pallas_call x1, Pallas kernels, exchange_out(): pl.pallas_call(functools.partial(out_kernel, n_seq, n_db, features), out_...  49.5 us
    pallas_call x1, Pallas kernels, exchange_back(): pl.pallas_call(functools.partial(back_kernel, n_seq), out_shape=(jax.Shap...  43.5 us
    gather x3, local copies, waits for them, and re-layouts, on_device(): blocks = jnp.take(neighbour_kv, recv_e, axis=0)  38.8 us
    dot_general x1, matrix products, on_device(): jnp.einsum('str,srf->tf', contexts, weight_cols, preferred_element_type=j...  7.25 us
    dot_general x1, matrix products, on_device(): jnp.dot(decoder_states, query_weight, preferred_element_type=jnp.float32)  6.5 us
  transfers between devices with their start and end apart: 1, of which 1 were waited for; matrix products, arithmetic and copies ran while one was open for 0% of the time, Pallas kernels for 0%

profile of v5, /device:TPU:1, one launch (start us, length us, event | category | flops | bytes accessed | tf_op | source)
XLA Modules:
  0.0 292.5 jit_solution(13810399257204906712)
XLA Ops:
  11.9 6.5 %convolution_convert_fusion = bf16[1024,256]{1,0:T(8,128)(2,1)} fusion(bf16[1024,4096]{1,0:T(8,128)(2,1)} %param.7, bf16[4096,256]{1,0:T(8,128)(2,1)S(1)} %copy-done), kind=kOutput, calls=%fused_computation.24 | convolution fusion | flops 2147745792 | bytes 11010048 | tf_op jit(solution)/shard_map/dot_general | solution.py:193
  18.4 1.7 gather_fusion
  20.2 1.8 scatter_fusion
  23.2 49.5 %shard_map.73 = (bf16[16,3,64,256]{3,2,1,0:T(8,128)(2,1)}, s32[16,128]{1,0:T(8,128)}, bf16[16,256,256]{2,1,0:T(8,128)(2,1)}) custom-call(bf16[16,3,64,256]{3,2,1,0:T(8,128)(2,1)} %bitcast.85, s32[16,128]{1,0:T(8,128)} %pad.4.send_e, bf16[256,4096]{1,0:T(8,128)(2,1)} %w_loc.1), custom_call_target="tpu_custom_call" | custom-call | tf_op jit(solution)/shard_map/pallas_call | solution.py:144
  74.6 3.5 %reshape.282 = bf16[48,64,2,128]{3,2,1,0:T(2,128)(2,1)} reshape(bf16[16,3,64,256]{3,2,1,0:T(8,128)(2,1)} %get-tuple-element.11) | data formatting | bytes 3145728 | tf_op jit(solution)/shard_map/reshape | solution.py:209
  78.1 14.3 %gather_fusion.1 = bf16[48,128,2,256]{3,2,1,0:T(2,128)(2,1)} fusion(bf16[8,128,2,256]{3,2,1,0:T(2,128)(2,1)S(1)} %copy-done.2, s32[1024]{0:T(1024)S(1)} %pad_clamp_fusion.1), kind=kCustom, calls=%fused_computation.1 | custom fusion | bytes 12583104 | tf_op jit(solution)/shard_map/jit(_take)/gather | solution.py:212
  92.4 15.8 %copy.77 = bf16[48,128,2,256]{1,3,2,0:T(8,128)(2,1)} copy(bf16[48,128,2,256]{3,2,1,0:T(2,128)(2,1)} %gather_fusion.1) | data formatting | bytes 12582912 | tf_op jit(solution)/shard_map/jit(_take)/gather | solution.py:212
  108.2 8.6 %copy.78 = bf16[48,128,2,2,128]{4,1,3,0,2:T(8,128)(2,1)} copy(bf16[48,128,2,2,128]{1,4,3,2,0:T(8,128)(2,1)} %bitcast.84) | data formatting | bytes 12582912 | tf_op jit(solution)/shard_map/jit(_take)/gather | solution.py:212
  116.9 3.6 %broadcast_select_fusion = bf16[48,128,2,2,128]{4,1,3,0,2:T(8,128)(2,1)S(1)} fusion(bf16[48,128,2,2,128]{4,1,3,0,2:T(8,128)(2,1)} %copy.78, pred[48]{0:T(512)(128)(4,1)S(1)} %compare_and_fusion), kind=kLoop, calls=%fused_computation.6 | loop fusion | flops 3145728 | bytes 12582960 | tf_op jit(solution)/shard_map/jit(_take)/select_n | solution.py:212
  120.5 2.4 multiply_reduce_fusion
  122.9 1.9 fusion.3
  124.9 2.2 fusion.2
  127.1 1.6 copy.82
  128.7 2.3 reshape.283.ctx
  131.0 2.3 copy.84
  133.3 4.0 %reshape.284.stats = f32[16,6,128]{2,1,0:T(8,128)} reshape(f32[48,2,64,2]{3,2,1,0:T(8,128)} %copy.84) | data formatting | bytes 98304 | tf_op jit(solution)/shard_map/reshape | solution.py:230
  137.3 43.5 %shard_map.74 = (bf16[16,3,64,256]{3,2,1,0:T(8,128)(2,1)}, f32[16,6,128]{2,1,0:T(8,128)}) custom-call(bf16[16,3,64,256]{3,2,1,0:T(8,128)(2,1)} %reshape.283.ctx, f32[16,6,128]{2,1,0:T(8,128)} %reshape.284.stats), custom_call_target="tpu_custom_call" | custom-call | tf_op jit(solution)/shard_map/pallas_call | solution.py:163
  180.8 2.4 reshape.286
  183.2 4.8 %reshape.285 = f32[48,2,64,2]{3,2,1,0:T(8,128)} reshape(f32[16,6,128]{2,1,0:T(8,128)S(1)} %copy-done.5) | data formatting | bytes 98304 | tf_op jit(solution)/shard_map/reshape | solution.py:234
  188.0 2.7 gather_fusion.3
  190.7 2.6 gather_fusion.2
  194.7 3.2 %multiply_reduce_fusion.1 = bf16[16,64,2,128]{3,2,1,0:T(2,128)(2,1)S(1)} fusion(pred[16,2]{1,0:T(8,128)(4,1)S(1)} %iota_compare_fusion.1, pred[16,2]{1,0:T(8,128)(4,1)S(1)} %copy.87, f32[16,2,64,2]{3,2,1,0:T(8,128)S(1)} %copy.86, bf16[32,64,2,128]{3,2,1,0:T(2,128)(2,1)S(1)} %gather_fusion.3), kind=kLoop, calls=%fused_computation.17 | loop fusion | flops 2359296 | bytes 1589312 | tf_op jit(solution)/shard_map/reduce_sum | solution.py:245
  199.1 79.3 %all-gather.2.cloned.1.call-done = bf16[16,1024,256]{2,1,0:T(8,128)(2,1)} async-done(((bf16[1,1024,256]{2,1,0:T(8,128)(2,1)}), bf16[16,1024,256]{2,1,0:T(8,128)(2,1)}) %all-gather.2.cloned.1.call-update) | async-done | bytes 8388624 | tf_op jit(solution)/shard_map/all_gather | solution.py:248
  278.4 7.2 %fusion.9 = bf16[1024,256]{1,0:T(8,128)(2,1)} fusion(bf16[16,1024,256]{2,1,0:T(8,128)(2,1)} %all-gather.2.cloned.1.call-done, bf16[16,256,256]{2,1,0:T(8,128)(2,1)} %get-tuple-element.14), kind=kOutput, calls=%fused_computation.23 | convolution fusion | flops 2147745792 | bytes 11010048 | tf_op jit(solution)/shard_map/str,srf->tf/dot_general | solution.py:249
  (56 shorter events, 11.1 us)
Async XLA Ops:
  6.5 5.3 %copy-start = (bf16[4096,256]{1,0:T(8,128)(2,1)S(1)}, bf16[4096,256]{1,0:T(8,128)(2,1)}, u32[]{:S(2)}) copy-start(bf16[4096,256]{1,0:T(8,128)(2,1)} %param.8) | copy-start | bytes 6291460
  6.5 271.8 %all-gather.2.cloned.1.call-start = ((), (), s32[]{:S(2)}) async-start(), calls=%async_computation | async-start | bytes 8912896 | tf_op jit(solution)/shard_map/all_gather | solution.py:248
  20.2 54.2 %copy-start.6 = (s32[16,2]{0,1:T(2,128)S(1)}, s32[16,2]{0,1:T(2,128)}, u32[]{:S(2)}) copy-start(s32[16,2]{0,1:T(2,128)} %param.11) | copy-start | bytes 388
  22.0 1.1 copy-start.3
  23.2 54.9 %copy-start.2 = (bf16[8,128,2,256]{3,2,1,0:T(2,128)(2,1)S(1)}, bf16[8,128,2,256]{3,2,1,0:T(2,128)(2,1)}, u32[]{:S(2)}) copy-start(bf16[8,128,2,256]{3,2,1,0:T(2,128)(2,1)} %param.10) | copy-start | bytes 3145732
  116.9 3.6 %copy-start.4 = (bf16[48,64,2,128]{3,2,1,0:T(2,128)(2,1)S(1)}, bf16[48,64,2,128]{3,2,1,0:T(2,128)(2,1)}, u32[]{:S(2)}) copy-start(bf16[48,64,2,128]{3,2,1,0:T(2,128)(2,1)} %reshape.282) | copy-start | bytes 4718596
  180.8 2.4 copy-start.5
  278.4 7.3 %copy-start.1 = (bf16[4096,256]{1,0:T(8,128)(2,1)S(1)}, bf16[4096,256]{1,0:T(8,128)(2,1)}, u32[]{:S(2)}) copy-start(bf16[4096,256]{1,0:T(8,128)(2,1)} %param.8) | copy-start | bytes 6291460
Sparse Core Ops, SparseCore 0:
  199.2 79.1 all-gather.1

commit v6 on v5

--- a/solution.py
+++ b/solution.py
@@ -132,6 +132,52 @@
         peer_copy(ctx.at[d], back_ctx.at[me_s], cs.at[d], cr.at[me_s], (d, me_d)).wait_send()
         peer_copy(stats.at[me_s], back_stats.at[s], ss.at[s], sr.at[s], (s, me_d)).wait_recv()
         peer_copy(ctx.at[me_s], back_ctx.at[s], cs.at[s], cr.at[s], (s, me_d)).wait_recv()
+
+
+def attend_kernel(scale, heads, e_ref, q_ref, kv0, kv1, kv2, ctx_ref, stats_ref):
+    for j, kv_ref in enumerate((kv0, kv1, kv2)):
+        width = heads * HD
+        for h in range(heads):
+            q = q_ref[0, j, :, h * HD:(h + 1) * HD]
+            k = kv_ref[0, :, h * HD:(h + 1) * HD]
+            v = kv_ref[0, :, width + h * HD:width + (h + 1) * HD]
+            s = lax.dot_general(
+                q, k, (((1,), (1,)), ((), ())), preferred_element_type=jnp.float32
+            ) * scale
+            top = jnp.max(s, axis=1, keepdims=True)
+            w = jnp.exp(s - top)
+            total = jnp.sum(w, axis=1, keepdims=True)
+            ctx = jnp.dot(w.astype(jnp.bfloat16), v, preferred_element_type=jnp.float32)
+            ctx_ref[0, j, :, h * HD:(h + 1) * HD] = (ctx / total).astype(ctx_ref.dtype)
+            stats_ref[0, j, :, 2 * h:2 * h + 1] = top
+            stats_ref[0, j, :, 2 * h + 1:2 * h + 2] = total
+
+
+def attend(recv_q, recv_e, kv_flat, heads):
+    n_src, cap, span, width = recv_q.shape
+    key_len = kv_flat.shape[1]
+
+    def kv_spec(j):
+        return pl.BlockSpec((1, key_len, kv_flat.shape[2]), lambda i, e: (e[i * CAP + j], 0, 0))
+
+    grid_spec = pltpu.PrefetchScalarGridSpec(
+        num_scalar_prefetch=1,
+        grid=(n_src,),
+        in_specs=[pl.BlockSpec((1, cap, span, width), lambda i, e: (i, 0, 0, 0))]
+        + [kv_spec(j) for j in range(CAP)],
+        out_specs=[
+            pl.BlockSpec((1, cap, span, width), lambda i, e: (i, 0, 0, 0)),
+            pl.BlockSpec((1, cap, span, 2 * heads), lambda i, e: (i, 0, 0, 0)),
+        ],
+    )
+    return pl.pallas_call(
+        functools.partial(attend_kernel, 1.0 / math.sqrt(HD), heads),
+        grid_spec=grid_spec,
+        out_shape=(
+            jax.ShapeDtypeStruct(recv_q.shape, jnp.bfloat16),
+            jax.ShapeDtypeStruct((n_src, cap, span, 2 * heads), jnp.float32),
+        ),
+    )(recv_e, recv_q, kv_flat, kv_flat, kv_flat)
 
 
 def any_spec():
@@ -206,41 +252,22 @@
     recv_q, recv_e, weight_cols = exchange_out(
         send_q.reshape(n_seq, CAP, SPAN, row_width), send_e, output_weight, n_seq, n_db
     )
-    recv_q = recv_q.reshape(places_total, SPAN, heads_here, HD)
     recv_e = recv_e[:, :CAP].reshape(-1)
-
-    blocks = jnp.take(neighbour_kv, recv_e, axis=0)
-    blocks = blocks.reshape(places_total, key_len, 2, heads_here, HD)
-    key_rows = blocks[:, :, 0]
-    val_rows = blocks[:, :, 1]
-    scores = jnp.einsum(
-        "pqhd,pnhd->phqn", recv_q, key_rows, preferred_element_type=jnp.float32
-    ) * (1.0 / math.sqrt(HD))
-    top = jnp.max(scores, axis=3, keepdims=True)
-    weights = jnp.exp(scores - top)
-    total = jnp.sum(weights, axis=3, keepdims=True)
-    part = jnp.einsum(
-        "phqn,pnhd->pqhd", weights.astype(jnp.bfloat16), val_rows,
-        preferred_element_type=jnp.float32,
-    )
-    part = part / jnp.transpose(total, (0, 2, 1, 3))
-    stats = jnp.concatenate([top, total], axis=3)
+    kv_flat = neighbour_kv.reshape(neighbour_kv.shape[0], key_len, 2 * row_width)
+    part, stats = attend(recv_q, recv_e, kv_flat, heads_here)
     back_ctx, back_stats = exchange_back(
-        part.astype(jnp.bfloat16).reshape(n_seq, CAP, SPAN, row_width),
-        stats.reshape(n_seq, CAP * heads_here * SPAN * 2 // LANES, LANES),
-        n_seq,
+        part, stats.reshape(n_seq, CAP * SPAN * 2 * heads_here // LANES, LANES), n_seq
     )
     back_ctx = back_ctx.reshape(places_total, SPAN, heads_here, HD)
-    back_stats = back_stats.reshape(places_total, heads_here, SPAN, 2)
+    back_stats = back_stats.reshape(places_total, SPAN, heads_here, 2)
 
     slot_ctx = jnp.take(back_ctx, place, axis=0).reshape(span_total, K, SPAN, heads_here, HD)
-    slot_stats = jnp.take(back_stats, place, axis=0).reshape(span_total, K, heads_here, SPAN, 2)
+    slot_stats = jnp.take(back_stats, place, axis=0).reshape(span_total, K, SPAN, heads_here, 2)
     live_k = live.reshape(span_total, K)[:, :, None, None]
     slot_top = jnp.where(live_k, slot_stats[..., 0], -jnp.inf)
     best = jnp.max(slot_top, axis=1, keepdims=True)
     scale = jnp.where(live_k, jnp.exp(slot_top - best) * slot_stats[..., 1], 0.0)
-    share = scale / jnp.sum(scale, axis=1, keepdims=True)
-    share = jnp.transpose(share, (0, 1, 3, 2))[..., None]
+    share = (scale / jnp.sum(scale, axis=1, keepdims=True))[..., None]
     slot_vals = jnp.where(live_k[..., None], slot_ctx.astype(jnp.float32), 0.0)
     context = jnp.sum(share * slot_vals, axis=1)
     context = context.astype(jnp.bfloat16).reshape(tok_rows, row_width)

time: 293 us -> 281 us (0.959)
  local copies, waits for them, and re-layouts: 77.2 us -> 44.8 us
  Pallas kernels: 93 us -> 121 us
  matrix products: 18.4 us -> 13.6 us
    gather x3 -> x0, local copies, waits for them, and re-layouts: 38.8 us -> none  [on_device(): blocks = jnp.take(neighbour_kv, recv_e, axis=0)]
    pallas_call x0 -> x1, Pallas kernels: none -> 27.8 us  [attend(): pl.pallas_call(functools.partial(attend_kernel, 1.0 / math.sqrt(HD), head...]
    gather x2, local copies, waits for them, and re-layouts: 3.25 us -> 8.68 us  [on_device(): jnp.take(back_stats, place, axis=0)]
    reshape x4 -> x3, local copies, waits for them, and re-layouts: 14.6 us -> 9.66 us  [the longest x1 6.33 us: on_device(): back_stats = back_stats.reshape(places_total, SPAN, heads_here, 2)]
    dot_general x2 -> x0, matrix products: 4.61 us -> none  [the longest x1 2.42 us: on_device(): jnp.einsum('pqhd,pnhd->phqn', recv_q, key_rows, preferred_element_type=jn...]
    select_n x2 -> x0, other arithmetic: 3.63 us -> none  [on_device(): blocks = jnp.take(neighbour_kv, recv_e, axis=0)]
where the time goes in v6:
time: 281 us; the launch traced here: 280 us
  Pallas kernels  121 us (43%)
  waiting for transfers between devices  79.6 us (28%)
  local copies, waits for them, and re-layouts  44.8 us (16%)
  matrix products  13.6 us (5%)
  between operations  13.5 us (5%)
  other arithmetic  8.07 us (3%)
    all_gather x1, waiting for transfers between devices, on_device(): contexts = lax.all_gather(context, 'db', axis=0, tiled=False)  79.6 us
    pallas_call x1, Pallas kernels, exchange_out(): pl.pallas_call(functools.partial(out_kernel, n_seq, n_db, features), out_...  49.5 us
    pallas_call x1, Pallas kernels, exchange_back(): pl.pallas_call(functools.partial(back_kernel, n_seq), out_shape=(jax.Shap...  43.4 us
    pallas_call x1, Pallas kernels, attend(): pl.pallas_call(functools.partial(attend_kernel, 1.0 / math.sqrt(HD), head...  27.8 us
    gather x2, local copies, waits for them, and re-layouts, on_device(): jnp.take(back_stats, place, axis=0)  8.68 us
    dot_general x1, matrix products, on_device(): jnp.einsum('str,srf->tf', contexts, weight_cols, preferred_element_type=j...  7.1 us
    dot_general x1, matrix products, on_device(): jnp.dot(decoder_states, query_weight, preferred_element_type=jnp.float32)  6.5 us
    reshape x1, local copies, waits for them, and re-layouts, on_device(): back_stats = back_stats.reshape(places_total, SPAN, heads_here, 2)  6.33 us
  transfers between devices with their start and end apart: 1, of which 1 were waited for; matrix products, arithmetic and copies ran while one was open for 0% of the time, Pallas kernels for 0%

profile of v6, /device:TPU:1, one launch (start us, length us, event | category | flops | bytes accessed | tf_op | source)
XLA Modules:
  0.0 280.3 jit_solution(4576483460008278340)
XLA Ops:
  6.5 0.9 iota_compare_fusion.1
  8.4 0.8 copy.44
  9.3 0.8 copy.47
  12.8 2.5 reshape.238.kv0.kv1.kv2
  15.4 6.5 %convolution_convert_fusion = bf16[1024,256]{1,0:T(8,128)(2,1)} fusion(bf16[1024,4096]{1,0:T(8,128)(2,1)} %param.7, bf16[4096,256]{1,0:T(8,128)(2,1)S(1)} %copy-done), kind=kOutput, calls=%fused_computation.9 | convolution fusion | flops 2147745792 | bytes 11010048 | tf_op jit(solution)/shard_map/dot_general | solution.py:239
  21.9 1.7 gather_fusion
  23.5 1.3 broadcast_in_dim.76
  24.9 4.5 %scatter_fusion = bf16[48,64,256]{2,1,0:T(8,128)(2,1)} fusion(bf16[48,64,256]{2,1,0:T(8,128)(2,1)} %broadcast_in_dim.76, s32[32]{0:T(128)S(1)} %get-tuple-element.20, bf16[32,64,256]{2,1,0:T(8,128)(2,1)S(1)} %gather_fusion), kind=kCustom, calls=%fused_computation.3 | custom fusion | bytes 3145856 | tf_op jit(solution)/shard_map/scatter | solution.py:248
  29.4 49.5 %shard_map.73 = (bf16[16,3,64,256]{3,2,1,0:T(8,128)(2,1)}, s32[16,128]{1,0:T(8,128)}, bf16[16,256,256]{2,1,0:T(8,128)(2,1)}) custom-call(bf16[16,3,64,256]{3,2,1,0:T(8,128)(2,1)} %bitcast.45, s32[16,128]{1,0:T(8,128)} %pad.4.send_e, bf16[256,4096]{1,0:T(8,128)(2,1)} %w_loc.1), custom_call_target="tpu_custom_call" | custom-call | tf_op jit(solution)/shard_map/pallas_call | solution.py:190
  79.0 1.3 reshape.237.e_ref
  80.2 27.8 %shard_map.74 = (bf16[16,3,64,256]{3,2,1,0:T(8,128)(2,1)}, f32[16,3,64,4]{3,2,1,0:T(8,128)}) custom-call(s32[48]{0:T(128)} %reshape.237.e_ref, bf16[16,3,64,256]{3,2,1,0:T(8,128)(2,1)} %get-tuple-element.13.q_ref, bf16[8,128,512]{2,1,0:T(8,128)(2,1)} %reshape.238.kv0.kv1.kv2, bf16[8,128,512]{2,1,0:T(8,128)(2,1)} %reshape.238.kv0.kv1.kv2, ...), custom_call_target="tpu_custom_call" | custom-call | tf_op jit(solution)/shard_map/pallas_call | solution.py:173
  108.1 2.7 copy.48
  110.7 0.8 copy.49.stats
  111.5 43.4 %shard_map.75 = (bf16[16,3,64,256]{3,2,1,0:T(8,128)(2,1)}, f32[16,6,128]{2,1,0:T(8,128)}) custom-call(bf16[16,3,64,256]{3,2,1,0:T(8,128)(2,1)} %get-tuple-element.14.ctx, f32[16,6,128]{2,1,0:T(8,128)} %copy.49.stats), custom_call_target="tpu_custom_call" | custom-call | tf_op jit(solution)/shard_map/pallas_call | solution.py:209
  155.0 3.5 %reshape.241 = bf16[48,64,2,128]{3,2,1,0:T(2,128)(2,1)} reshape(bf16[16,3,64,256]{3,2,1,0:T(8,128)(2,1)} %get-tuple-element.17) | data formatting | bytes 3145728 | tf_op jit(solution)/shard_map/reshape | solution.py:261
  158.5 6.3 %reshape.240 = f32[48,64,2,2]{3,2,1,0:T(2,128)} reshape(f32[16,6,128]{2,1,0:T(8,128)S(1)} %copy-done.1) | data formatting | bytes 98304 | tf_op jit(solution)/shard_map/reshape | solution.py:262
  164.8 4.1 %gather_fusion.2 = bf16[32,64,2,128]{3,2,1,0:T(2,128)(2,1)S(1)} fusion(bf16[48,64,2,128]{3,2,1,0:T(2,128)(2,1)} %reshape.241, s32[1024]{0:T(1024)S(1)} %pad_clamp_fusion), kind=kCustom, calls=%fused_computation.2 | custom fusion | bytes 2097280 | tf_op jit(solution)/shard_map/jit(_take)/gather | solution.py:264
  168.9 5.9 %gather_fusion.1 = f32[32,64,2,2]{3,2,1,0:T(2,128)} fusion(f32[48,64,2,2]{3,2,1,0:T(2,128)} %reshape.240, s32[1024]{0:T(1024)S(1)} %pad_clamp_fusion), kind=kCustom, calls=%fused_computation.1 | custom fusion | bytes 65664 | tf_op jit(solution)/shard_map/jit(_take)/gather | solution.py:265
  174.8 2.8 copy.50
  177.9 1.4 copy.52
  179.3 5.3 %multiply_reduce_fusion = bf16[16,64,2,128]{3,2,1,0:T(2,128)(2,1)} fusion(pred[16,2]{1,0:T(8,128)(4,1)S(1)} %iota_compare_fusion.1, pred[16,2]{1,0:T(8,128)(4,1)S(1)} %copy.53, f32[16,2,64,2]{3,2,1,0:T(8,128)} %copy.52, bf16[32,64,2,128]{3,2,1,0:T(2,128)(2,1)S(1)} %gather_fusion.2), kind=kLoop, calls=%fused_computation.5 | loop fusion | flops 2359296 | bytes 1589312 | tf_op jit(solution)/shard_map/reduce_sum | solution.py:272
  184.6 2.2 convert_element_type.29
  186.8 79.6 %all-gather.2.cloned.1.call-done = bf16[16,1024,256]{2,1,0:T(8,128)(2,1)} async-done(((bf16[1,1024,256]{2,1,0:T(8,128)(2,1)}), bf16[16,1024,256]{2,1,0:T(8,128)(2,1)}) %all-gather.2.cloned.1.call-update) | async-done | bytes 8388624 | tf_op jit(solution)/shard_map/all_gather | solution.py:275
  266.4 7.1 %fusion = bf16[1024,256]{1,0:T(8,128)(2,1)} fusion(bf16[16,1024,256]{2,1,0:T(8,128)(2,1)} %all-gather.2.cloned.1.call-done, bf16[16,256,256]{2,1,0:T(8,128)(2,1)} %get-tuple-element.18), kind=kOutput, calls=%fused_computation.8 | convolution fusion | flops 2147745792 | bytes 11010048 | tf_op jit(solution)/shard_map/str,srf->tf/dot_general | solution.py:276
  (31 shorter events, 4.2 us)
Async XLA Ops:
  6.5 8.8 %copy-start = (bf16[4096,256]{1,0:T(8,128)(2,1)S(1)}, bf16[4096,256]{1,0:T(8,128)(2,1)}, u32[]{:S(2)}) copy-start(bf16[4096,256]{1,0:T(8,128)(2,1)} %param.8) | copy-start | bytes 6291460
  6.5 259.9 %all-gather.2.cloned.1.call-start = ((), (), s32[]{:S(2)}) async-start(), calls=%async_computation | async-start | bytes 8912896 | tf_op jit(solution)/shard_map/all_gather | solution.py:275
  155.0 3.5 %copy-start.1 = (f32[16,6,128]{2,1,0:T(8,128)S(1)}, f32[16,6,128]{2,1,0:T(8,128)}, u32[]{:S(2)}) copy-start(f32[16,6,128]{2,1,0:T(8,128)} %get-tuple-element.16) | copy-start | bytes 147460
Sparse Core Ops, SparseCore 0:
  187.0 79.3 all-gather.1

commit v7 on v6

--- a/solution.py
+++ b/solution.py
@@ -178,6 +178,43 @@
             jax.ShapeDtypeStruct((n_src, cap, span, 2 * heads), jnp.float32),
         ),
     )(recv_e, recv_q, kv_flat, kv_flat, kv_flat)
+
+
+def combine_kernel(heads, place_ref, count_ref, c0, c1, s0, s1, out_ref):
+    live1 = count_ref[pl.program_id(0)] > 1
+    for h in range(heads):
+        cols = slice(h * HD, (h + 1) * HD)
+        m0 = s0[0, :, 2 * h:2 * h + 1]
+        l0 = s0[0, :, 2 * h + 1:2 * h + 2]
+        m1 = s1[0, :, 2 * h:2 * h + 1]
+        l1 = s1[0, :, 2 * h + 1:2 * h + 2]
+        best = jnp.where(live1, jnp.maximum(m0, m1), m0)
+        a0 = jnp.exp(m0 - best) * l0
+        a1 = jnp.where(live1, jnp.exp(m1 - best) * l1, 0.0)
+        v0 = c0[0, :, cols].astype(jnp.float32)
+        v1 = jnp.where(live1, c1[0, :, cols].astype(jnp.float32), 0.0)
+        out_ref[0, :, cols] = ((a0 * v0 + a1 * v1) / (a0 + a1)).astype(out_ref.dtype)
+
+
+def combine(back_ctx, back_stats, place, neighbour_count, heads):
+    places, span, width = back_ctx.shape
+    spans = neighbour_count.shape[0]
+
+    def by_place(k, shape):
+        return pl.BlockSpec((1,) + shape, lambda c, p, n: (p[c * K + k], 0, 0))
+
+    grid_spec = pltpu.PrefetchScalarGridSpec(
+        num_scalar_prefetch=2,
+        grid=(spans,),
+        in_specs=[by_place(0, (span, width)), by_place(1, (span, width)),
+                  by_place(0, (span, 2 * heads)), by_place(1, (span, 2 * heads))],
+        out_specs=pl.BlockSpec((1, span, width), lambda c, p, n: (c, 0, 0)),
+    )
+    return pl.pallas_call(
+        functools.partial(combine_kernel, heads),
+        grid_spec=grid_spec,
+        out_shape=jax.ShapeDtypeStruct((spans, span, width), jnp.bfloat16),
+    )(place, neighbour_count, back_ctx, back_ctx, back_stats, back_stats)
 
 
 def any_spec():
@@ -258,19 +295,10 @@
     back_ctx, back_stats = exchange_back(
         part, stats.reshape(n_seq, CAP * SPAN * 2 * heads_here // LANES, LANES), n_seq
     )
-    back_ctx = back_ctx.reshape(places_total, SPAN, heads_here, HD)
-    back_stats = back_stats.reshape(places_total, SPAN, heads_here, 2)
-
-    slot_ctx = jnp.take(back_ctx, place, axis=0).reshape(span_total, K, SPAN, heads_here, HD)
-    slot_stats = jnp.take(back_stats, place, axis=0).reshape(span_total, K, SPAN, heads_here, 2)
-    live_k = live.reshape(span_total, K)[:, :, None, None]
-    slot_top = jnp.where(live_k, slot_stats[..., 0], -jnp.inf)
-    best = jnp.max(slot_top, axis=1, keepdims=True)
-    scale = jnp.where(live_k, jnp.exp(slot_top - best) * slot_stats[..., 1], 0.0)
-    share = (scale / jnp.sum(scale, axis=1, keepdims=True))[..., None]
-    slot_vals = jnp.where(live_k[..., None], slot_ctx.astype(jnp.float32), 0.0)
-    context = jnp.sum(share * slot_vals, axis=1)
-    context = context.astype(jnp.bfloat16).reshape(tok_rows, row_width)
+    back_ctx = back_ctx.reshape(places_total, SPAN, row_width)
+    back_stats = back_stats.reshape(places_total, SPAN, 2 * heads_here)
+    context = combine(back_ctx, back_stats, place, neighbour_count, heads_here)
+    context = context.reshape(tok_rows, row_width)
 
     contexts = lax.all_gather(context, "db", axis=0, tiled=False)
     out = jnp.einsum(

time: 281 us -> 264 us (0.940)
  local copies, waits for them, and re-layouts: 44.8 us -> 22.1 us
  Pallas kernels: 121 us -> 131 us
  other arithmetic: 8.07 us -> 2.29 us
    gather x3 -> x0, local copies, waits for them, and re-layouts: 12.7 us -> none  [the longest x2 8.68 us: on_device(): jnp.take(back_stats, place, axis=0)]
    pallas_call x0 -> x1, Pallas kernels: none -> 10.5 us  [combine(): pl.pallas_call(functools.partial(combine_kernel, heads), grid_spec=grid_s...]
    reshape x2 -> x1, local copies, waits for them, and re-layouts: 9.86 us -> 3.61 us  [on_device(): back_stats = back_stats.reshape(places_total, SPAN, 2 * heads_here)]
    reduce_sum x2 -> x0, other arithmetic: 5.35 us -> none  [the longest x1 5.26 us: on_device(): context = jnp.sum(share * slot_vals, axis=1)]
where the time goes in v7:
time: 264 us; the launch traced here: 262 us
  Pallas kernels  131 us (50%)
  waiting for transfers between devices  80.1 us (30%)
  local copies, waits for them, and re-layouts  22.1 us (8%)
  matrix products  13.6 us (5%)
  between operations  13.4 us (5%)
    all_gather x1, waiting for transfers between devices, on_device(): contexts = lax.all_gather(context, 'db', axis=0, tiled=False)  80.1 us
    pallas_call x1, Pallas kernels, exchange_out(): pl.pallas_call(functools.partial(out_kernel, n_seq, n_db, features), out_...  49.4 us
    pallas_call x1, Pallas kernels, exchange_back(): pl.pallas_call(functools.partial(back_kernel, n_seq), out_shape=(jax.Shap...  43.2 us
    pallas_call x1, Pallas kernels, attend(): pl.pallas_call(functools.partial(attend_kernel, 1.0 / math.sqrt(HD), head...  27.8 us
    pallas_call x1, Pallas kernels, combine(): pl.pallas_call(functools.partial(combine_kernel, heads), grid_spec=grid_s...  10.5 us
    dot_general x1, matrix products, on_device(): jnp.einsum('str,srf->tf', contexts, weight_cols, preferred_element_type=j...  7.1 us
    dot_general x1, matrix products, on_device(): jnp.dot(decoder_states, query_weight, preferred_element_type=jnp.float32)  6.5 us
  transfers between devices with their start and end apart: 1, of which 1 were waited for; matrix products, arithmetic and copies ran while one was open for 0% of the time, Pallas kernels for 0%

profile of v7, /device:TPU:1, one launch (start us, length us, event | category | flops | bytes accessed | tf_op | source)
XLA Modules:
  0.0 262.5 jit_solution(17926359679967406099)
XLA Ops:
  6.5 0.9 iota_compare_fusion.1
  7.5 0.1 lt.68
  7.6 0.7 broadcast_multiply_fusion
  8.3 0.8 copy.21
  9.2 0.8 copy.23
  10.2 0.2 convert_reduce_fusion
  10.4 0.5 multiply_add_fusion.place_ref
  10.9 0.7 scatter_custom_fusion.1
  11.7 0.6 pad.4.send_e
  12.3 2.5 reshape.153.kv0.kv1.kv2
  14.8 6.5 %convolution_convert_fusion = bf16[1024,256]{1,0:T(8,128)(2,1)} fusion(bf16[1024,4096]{1,0:T(8,128)(2,1)} %param.7, bf16[4096,256]{1,0:T(8,128)(2,1)S(1)} %copy-done), kind=kOutput, calls=%fused_computation.5 | convolution fusion | flops 2147745792 | bytes 11010048 | tf_op jit(solution)/shard_map/dot_general | solution.py:276
  21.3 1.7 gather_fusion
  23.0 1.3 broadcast_in_dim.8
  24.3 4.8 %scatter_fusion = bf16[48,64,256]{2,1,0:T(8,128)(2,1)} fusion(bf16[48,64,256]{2,1,0:T(8,128)(2,1)} %broadcast_in_dim.8, s32[32]{0:T(128)S(1)} %fusion.3, bf16[32,64,256]{2,1,0:T(8,128)(2,1)S(1)} %gather_fusion), kind=kCustom, calls=%fused_computation.1 | custom fusion | bytes 3145856 | tf_op jit(solution)/shard_map/scatter | solution.py:285
  29.1 49.4 %shard_map.73 = (bf16[16,3,64,256]{3,2,1,0:T(8,128)(2,1)}, s32[16,128]{1,0:T(8,128)}, bf16[16,256,256]{2,1,0:T(8,128)(2,1)}) custom-call(bf16[16,3,64,256]{3,2,1,0:T(8,128)(2,1)} %bitcast.26, s32[16,128]{1,0:T(8,128)} %pad.4.send_e, bf16[256,4096]{1,0:T(8,128)(2,1)} %w_loc.1), custom_call_target="tpu_custom_call" | custom-call | tf_op jit(solution)/shard_map/pallas_call | solution.py:227
  78.5 1.3 reshape.152.e_ref
  79.8 27.8 %shard_map.74 = (bf16[16,3,64,256]{3,2,1,0:T(8,128)(2,1)}, f32[16,3,64,4]{3,2,1,0:T(8,128)}) custom-call(s32[48]{0:T(128)} %reshape.152.e_ref, bf16[16,3,64,256]{3,2,1,0:T(8,128)(2,1)} %get-tuple-element.13.q_ref, bf16[8,128,512]{2,1,0:T(8,128)(2,1)} %reshape.153.kv0.kv1.kv2, bf16[8,128,512]{2,1,0:T(8,128)(2,1)} %reshape.153.kv0.kv1.kv2, ...), custom_call_target="tpu_custom_call" | custom-call | tf_op jit(solution)/shard_map/pallas_call | solution.py:173
  107.6 2.7 %copy.24 = f32[16,3,64,4]{0,3,2,1:T(4,128)S(1)} copy(f32[16,3,64,4]{3,2,1,0:T(8,128)} %get-tuple-element.15) | data formatting | bytes 98304 | tf_op jit(solution)/shard_map/pallas_call | solution.py:173
  110.3 0.8 copy.25.stats
  111.1 43.2 %shard_map.75 = (bf16[16,3,64,256]{3,2,1,0:T(8,128)(2,1)}, f32[16,6,128]{2,1,0:T(8,128)}) custom-call(bf16[16,3,64,256]{3,2,1,0:T(8,128)(2,1)} %get-tuple-element.14.ctx, f32[16,6,128]{2,1,0:T(8,128)} %copy.25.stats), custom_call_target="tpu_custom_call" | custom-call | tf_op jit(solution)/shard_map/pallas_call | solution.py:246
  154.3 3.6 %reshape.156.s0.s1 = f32[48,64,4]{2,1,0:T(8,128)} reshape(f32[16,6,128]{2,1,0:T(8,128)} %get-tuple-element.17) | data formatting | bytes 98304 | tf_op jit(solution)/shard_map/reshape | solution.py:299
  157.9 10.5 %shard_map.76 = bf16[16,64,256]{2,1,0:T(8,128)(2,1)} custom-call(s32[32]{0:T(128)} %multiply_add_fusion.place_ref, s32[16]{0:T(128)} %count_ref.1, bf16[48,64,256]{2,1,0:T(8,128)(2,1)} %bitcast.27, bf16[48,64,256]{2,1,0:T(8,128)(2,1)} %bitcast.28, f32[48,64,4]{2,1,0:T(8,128)} %reshape.156.s0.s1, f32[48,64,4]{2,1,0:T(8,128)} %reshape.156.s0.s1), custom_call_target="tpu_custom_call" | custom-call | tf_op jit(solution)/shard_map/pallas_call | solution.py:213
  168.5 80.1 %all-gather.2.cloned.1.call-done = bf16[16,1024,256]{2,1,0:T(8,128)(2,1)} async-done(((bf16[1,1024,256]{2,1,0:T(8,128)(2,1)}), bf16[16,1024,256]{2,1,0:T(8,128)(2,1)}) %all-gather.2.cloned.1.call-update) | async-done | bytes 8388624 | tf_op jit(solution)/shard_map/all_gather | solution.py:303
  248.5 7.1 %fusion = bf16[1024,256]{1,0:T(8,128)(2,1)} fusion(bf16[16,1024,256]{2,1,0:T(8,128)(2,1)} %all-gather.2.cloned.1.call-done, bf16[16,256,256]{2,1,0:T(8,128)(2,1)} %get-tuple-element.18), kind=kOutput, calls=%fused_computation.4 | convolution fusion | flops 2147745792 | bytes 11010048 | tf_op jit(solution)/shard_map/str,srf->tf/dot_general | solution.py:304
  (13 shorter events, 0.6 us)
Async XLA Ops:
  6.5 8.3 %copy-start = (bf16[4096,256]{1,0:T(8,128)(2,1)S(1)}, bf16[4096,256]{1,0:T(8,128)(2,1)}, u32[]{:S(2)}) copy-start(bf16[4096,256]{1,0:T(8,128)(2,1)} %param.8) | copy-start | bytes 6291460
  6.5 242.0 %all-gather.2.cloned.1.call-start = ((), (), s32[]{:S(2)}) async-start(), calls=%async_computation | async-start | bytes 8912896 | tf_op jit(solution)/shard_map/all_gather | solution.py:303
Sparse Core Ops, SparseCore 0:
  168.6 79.8 all-gather.1

commit v8 on v7

--- a/solution.py
+++ b/solution.py
@@ -134,10 +134,10 @@
         peer_copy(ctx.at[me_s], back_ctx.at[s], cs.at[s], cr.at[s], (s, me_d)).wait_recv()
 
 
-def attend_kernel(scale, heads, e_ref, q_ref, kv0, kv1, kv2, ctx_ref, stats_ref):
+def attend_kernel(scale, heads, head, e_ref, q_ref, kv0, kv1, kv2, ctx_ref, stats_ref):
     for j, kv_ref in enumerate((kv0, kv1, kv2)):
         width = heads * HD
-        for h in range(heads):
+        for h in (head,):
             q = q_ref[0, j, :, h * HD:(h + 1) * HD]
             k = kv_ref[0, :, h * HD:(h + 1) * HD]
             v = kv_ref[0, :, width + h * HD:width + (h + 1) * HD]
@@ -148,12 +148,12 @@
             w = jnp.exp(s - top)
             total = jnp.sum(w, axis=1, keepdims=True)
             ctx = jnp.dot(w.astype(jnp.bfloat16), v, preferred_element_type=jnp.float32)
-            ctx_ref[0, j, :, h * HD:(h + 1) * HD] = (ctx / total).astype(ctx_ref.dtype)
-            stats_ref[0, j, :, 2 * h:2 * h + 1] = top
-            stats_ref[0, j, :, 2 * h + 1:2 * h + 2] = total
-
-
-def attend(recv_q, recv_e, kv_flat, heads):
+            ctx_ref[0, j] = (ctx / total).astype(ctx_ref.dtype)
+            stats_ref[0, j, :, 0:1] = top
+            stats_ref[0, j, :, 1:2] = total
+
+
+def attend(recv_q, recv_e, kv_flat, heads, head):
     n_src, cap, span, width = recv_q.shape
     key_len = kv_flat.shape[1]
 
@@ -166,16 +166,16 @@
         in_specs=[pl.BlockSpec((1, cap, span, width), lambda i, e: (i, 0, 0, 0))]
         + [kv_spec(j) for j in range(CAP)],
         out_specs=[
-            pl.BlockSpec((1, cap, span, width), lambda i, e: (i, 0, 0, 0)),
-            pl.BlockSpec((1, cap, span, 2 * heads), lambda i, e: (i, 0, 0, 0)),
+            pl.BlockSpec((1, cap, span, HD), lambda i, e: (i, 0, 0, 0)),
+            pl.BlockSpec((1, cap, span, 2), lambda i, e: (i, 0, 0, 0)),
         ],
     )
     return pl.pallas_call(
-        functools.partial(attend_kernel, 1.0 / math.sqrt(HD), heads),
+        functools.partial(attend_kernel, 1.0 / math.sqrt(HD), heads, head),
         grid_spec=grid_spec,
         out_shape=(
-            jax.ShapeDtypeStruct(recv_q.shape, jnp.bfloat16),
-            jax.ShapeDtypeStruct((n_src, cap, span, 2 * heads), jnp.float32),
+            jax.ShapeDtypeStruct((n_src, cap, span, HD), jnp.bfloat16),
+            jax.ShapeDtypeStruct((n_src, cap, span, 2), jnp.float32),
         ),
     )(recv_e, recv_q, kv_flat, kv_flat, kv_flat)
 
@@ -241,7 +241,7 @@
     )(send_q, send_e, w_loc)
 
 
-def exchange_back(ctx, stats, n_seq):
+def exchange_back(ctx, stats, n_seq, collective_id):
     dma = pltpu.SemaphoreType.DMA
     return pl.pallas_call(
         functools.partial(back_kernel, n_seq),
@@ -252,7 +252,7 @@
         in_specs=[any_spec()] * 2,
         out_specs=(any_spec(), any_spec()),
         scratch_shapes=[dma((n_seq,)), dma((n_seq,)), dma((n_seq,)), dma((n_seq,)), dma((2,))],
-        compiler_params=pltpu.CompilerParams(collective_id=1, has_side_effects=True),
+        compiler_params=pltpu.CompilerParams(collective_id=collective_id, has_side_effects=True),
     )(ctx, stats)
 
 
@@ -291,19 +291,22 @@
     )
     recv_e = recv_e[:, :CAP].reshape(-1)
     kv_flat = neighbour_kv.reshape(neighbour_kv.shape[0], key_len, 2 * row_width)
-    part, stats = attend(recv_q, recv_e, kv_flat, heads_here)
-    back_ctx, back_stats = exchange_back(
-        part, stats.reshape(n_seq, CAP * SPAN * 2 * heads_here // LANES, LANES), n_seq
-    )
-    back_ctx = back_ctx.reshape(places_total, SPAN, row_width)
-    back_stats = back_stats.reshape(places_total, SPAN, 2 * heads_here)
-    context = combine(back_ctx, back_stats, place, neighbour_count, heads_here)
-    context = context.reshape(tok_rows, row_width)
-
-    contexts = lax.all_gather(context, "db", axis=0, tiled=False)
-    out = jnp.einsum(
-        "str,srf->tf", contexts, weight_cols, preferred_element_type=jnp.float32
-    )
+    weight_cols = weight_cols.reshape(n_db, heads_here, HD, weight_cols.shape[2])
+    out = None
+    for head in range(heads_here):
+        part, stats = attend(recv_q, recv_e, kv_flat, heads_here, head)
+        back_ctx, back_stats = exchange_back(
+            part, stats.reshape(n_seq, CAP * SPAN * 2 // LANES, LANES), n_seq, 1 + head
+        )
+        back_ctx = back_ctx.reshape(places_total, SPAN, HD)
+        back_stats = back_stats.reshape(places_total, SPAN, 2)
+        context = combine(back_ctx, back_stats, place, neighbour_count, 1)
+        context = context.reshape(tok_rows, HD)
+        contexts = lax.all_gather(context, "db", axis=0, tiled=False)
+        term = jnp.einsum(
+            "str,srf->tf", contexts, weight_cols[:, head], preferred_element_type=jnp.float32
+        )
+        out = term if out is None else out + term
     return out.astype(jnp.bfloat16)
 
 

time: 264 us -> 281 us (1.064)
  Pallas kernels: 131 us -> 153 us
  waiting for transfers between devices: 80.1 us -> 66.2 us
  local copies, waits for them, and re-layouts: 22.1 us -> 27.9 us
    all_gather x1 -> x2, waiting for transfers between devices: 80.1 us -> 66.2 us  [on_device(): contexts = lax.all_gather(context, 'db', axis=0, tiled=False)]
    pallas_call x1 -> x2, Pallas kernels: 10.5 us -> 20.5 us  [combine(): pl.pallas_call(functools.partial(combine_kernel, heads), grid_spec=grid_s...]
    pallas_call x1 -> x2, Pallas kernels: 27.8 us -> 34.4 us  [attend(): pl.pallas_call(functools.partial(attend_kernel, 1.0 / math.sqrt(HD), head...]
    pallas_call x1 -> x2, Pallas kernels: 43.2 us -> 48.1 us  [exchange_back(): pl.pallas_call(functools.partial(back_kernel, n_seq), out_shape=(jax.Shap...]
    reshape x2 -> x4, local copies, waits for them, and re-layouts: 4.41 us -> 8.45 us  [the longest x2 7.02 us: on_device(): back_stats = back_stats.reshape(places_total, SPAN, 2)]
    dot_general x1 -> x2, matrix products: 7.1 us -> 8.26 us  [on_device(): jnp.einsum('str,srf->tf', contexts, weight_cols[:, head], preferred_eleme...]
  transfers between devices with their start and end apart: 1 -> 2, of which waited for: 1 -> 2; matrix products, arithmetic and copies ran while one was open for 0% -> 4% of each run, Pallas kernels for 0% -> 18%
where the time goes in v8:
time: 281 us; the launch traced here: 277 us
  Pallas kernels  153 us (54%)
  waiting for transfers between devices  66.2 us (24%)
  local copies, waits for them, and re-layouts  27.9 us (10%)
  matrix products  14.8 us (5%)
  between operations  13.5 us (5%)
    all_gather x2, waiting for transfers between devices, on_device(): contexts = lax.all_gather(context, 'db', axis=0, tiled=False)  66.2 us
    pallas_call x1, Pallas kernels, exchange_out(): pl.pallas_call(functools.partial(out_kernel, n_seq, n_db, features), out_...  49.7 us
    pallas_call x2, Pallas kernels, exchange_back(): pl.pallas_call(functools.partial(back_kernel, n_seq), out_shape=(jax.Shap...  48.1 us
    pallas_call x2, Pallas kernels, attend(): pl.pallas_call(functools.partial(attend_kernel, 1.0 / math.sqrt(HD), head...  34.4 us
    pallas_call x2, Pallas kernels, combine(): pl.pallas_call(functools.partial(combine_kernel, heads), grid_spec=grid_s...  20.5 us
    dot_general x2, matrix products, on_device(): jnp.einsum('str,srf->tf', contexts, weight_cols[:, head], preferred_eleme...  8.26 us
    reshape x2, local copies, waits for them, and re-layouts, on_device(): back_stats = back_stats.reshape(places_total, SPAN, 2)  7.02 us
    dot_general x1, matrix products, on_device(): jnp.dot(decoder_states, query_weight, preferred_element_type=jnp.float32)  6.5 us
  transfers between devices with their start and end apart: 2, of which 2 were waited for; matrix products, arithmetic and copies ran while one was open for 4% of the time, Pallas kernels for 18%

profile of v8, /device:TPU:1, one launch (start us, length us, event | category | flops | bytes accessed | tf_op | source)
XLA Modules:
  0.0 277.4 jit_solution(3825421795533558816)
XLA Ops:
  6.5 0.9 iota_compare_fusion.1
  7.6 0.8 copy.43
  10.1 0.8 copy.45
  12.3 6.5 %convolution_convert_fusion = bf16[1024,256]{1,0:T(8,128)(2,1)} fusion(bf16[1024,4096]{1,0:T(8,128)(2,1)} %param.7, bf16[4096,256]{1,0:T(8,128)(2,1)S(1)} %copy-done), kind=kOutput, calls=%fused_computation.7 | convolution fusion | flops 2147745792 | bytes 11010048 | tf_op jit(solution)/shard_map/dot_general | solution.py:276
  18.9 1.7 gather_fusion
  20.5 1.4 broadcast_in_dim.8
  21.9 4.8 %scatter_fusion = bf16[48,64,256]{2,1,0:T(8,128)(2,1)} fusion(bf16[48,64,256]{2,1,0:T(8,128)(2,1)} %broadcast_in_dim.8, s32[32]{0:T(128)S(1)} %fusion.4, bf16[32,64,256]{2,1,0:T(8,128)(2,1)S(1)} %gather_fusion), kind=kCustom, calls=%fused_computation.1 | custom fusion | bytes 3145856 | tf_op jit(solution)/shard_map/scatter | solution.py:285
  26.6 49.7 %shard_map.73 = (bf16[16,3,64,256]{3,2,1,0:T(8,128)(2,1)}, s32[16,128]{1,0:T(8,128)}, bf16[16,256,256]{2,1,0:T(8,128)(2,1)}) custom-call(bf16[16,3,64,256]{3,2,1,0:T(8,128)(2,1)} %bitcast.42, s32[16,128]{1,0:T(8,128)} %pad.4.send_e, bf16[256,4096]{1,0:T(8,128)(2,1)} %w_loc.1), custom_call_target="tpu_custom_call" | custom-call | tf_op jit(solution)/shard_map/pallas_call | solution.py:227
  76.4 1.4 reshape.164.e_ref
  77.7 1.5 reshape.165.kv0.kv1.kv2
  79.3 17.1 %shard_map.77 = (bf16[16,3,64,128]{3,2,1,0:T(8,128)(2,1)}, f32[16,3,64,2]{3,2,1,0:T(8,128)}) custom-call(s32[48]{0:T(128)} %reshape.164.e_ref, bf16[16,3,64,256]{3,2,1,0:T(8,128)(2,1)} %get-tuple-element.17.q_ref, bf16[8,128,512]{2,1,0:T(8,128)(2,1)} %reshape.165.kv0.kv1.kv2, bf16[8,128,512]{2,1,0:T(8,128)(2,1)} %reshape.165.kv0.kv1.kv2, ...), custom_call_target="tpu_custom_call" | custom-call | tf_op jit(solution)/shard_map/pallas_call | solution.py:173
  96.4 2.7 copy.52
  99.8 25.9 %shard_map.78 = (bf16[16,3,64,128]{3,2,1,0:T(8,128)(2,1)}, f32[16,3,128]{2,1,0:T(4,128)}) custom-call(bf16[16,3,64,128]{3,2,1,0:T(8,128)(2,1)} %get-tuple-element.23.ctx, f32[16,3,128]{2,1,0:T(4,128)} %copy.53.stats), custom_call_target="tpu_custom_call" | custom-call | tf_op jit(solution)/shard_map/pallas_call | solution.py:246
  125.7 3.5 %reshape.200.s0.s1 = f32[48,64,2]{2,1,0:T(8,128)} reshape(f32[16,3,128]{2,1,0:T(4,128)} %get-tuple-element.26) | data formatting | bytes 49152 | tf_op jit(solution)/shard_map/reshape | solution.py:302
  129.2 10.3 %shard_map.79 = bf16[16,64,128]{2,1,0:T(8,128)(2,1)} custom-call(s32[32]{0:T(128)} %multiply_add_fusion.place_ref, s32[16]{0:T(128)} %count_ref.3, bf16[48,64,128]{2,1,0:T(8,128)(2,1)} %bitcast.45, bf16[48,64,128]{2,1,0:T(8,128)(2,1)} %bitcast.46, f32[48,64,2]{2,1,0:T(8,128)} %reshape.200.s0.s1, f32[48,64,2]{2,1,0:T(8,128)} %reshape.200.s0.s1), custom_call_target="tpu_custom_call" | custom-call | tf_op jit(solution)/shard_map/pallas_call | solution.py:213
  139.5 17.2 %shard_map.74 = (bf16[16,3,64,128]{3,2,1,0:T(8,128)(2,1)}, f32[16,3,64,2]{3,2,1,0:T(8,128)}) custom-call(s32[48]{0:T(128)} %reshape.164.e_ref, bf16[16,3,64,256]{3,2,1,0:T(8,128)(2,1)} %get-tuple-element.17.q_ref, bf16[8,128,512]{2,1,0:T(8,128)(2,1)} %reshape.165.kv0.kv1.kv2, bf16[8,128,512]{2,1,0:T(8,128)(2,1)} %reshape.165.kv0.kv1.kv2, ...), custom_call_target="tpu_custom_call" | custom-call | tf_op jit(solution)/shard_map/pallas_call | solution.py:173
  156.7 2.7 copy.46
  160.1 22.2 %shard_map.75 = (bf16[16,3,64,128]{3,2,1,0:T(8,128)(2,1)}, f32[16,3,128]{2,1,0:T(4,128)}) custom-call(bf16[16,3,64,128]{3,2,1,0:T(8,128)(2,1)} %get-tuple-element.18.ctx, f32[16,3,128]{2,1,0:T(4,128)} %copy.47.stats), custom_call_target="tpu_custom_call" | custom-call | tf_op jit(solution)/shard_map/pallas_call | solution.py:246
  182.3 3.5 %reshape.199.s0.s1 = f32[48,64,2]{2,1,0:T(8,128)} reshape(f32[16,3,128]{2,1,0:T(4,128)} %get-tuple-element.21) | data formatting | bytes 49152 | tf_op jit(solution)/shard_map/reshape | solution.py:302
  185.8 10.2 %shard_map.76 = bf16[16,64,128]{2,1,0:T(8,128)(2,1)} custom-call(s32[32]{0:T(128)} %multiply_add_fusion.place_ref, s32[16]{0:T(128)} %count_ref.3, bf16[48,64,128]{2,1,0:T(8,128)(2,1)} %bitcast.43, bf16[48,64,128]{2,1,0:T(8,128)(2,1)} %bitcast.44, f32[48,64,2]{2,1,0:T(8,128)} %reshape.199.s0.s1, f32[48,64,2]{2,1,0:T(8,128)} %reshape.199.s0.s1), custom_call_target="tpu_custom_call" | custom-call | tf_op jit(solution)/shard_map/pallas_call | solution.py:213
  196.1 11.0 %all-gather.5.cloned.1.call-done = bf16[16,1024,128]{2,1,0:T(8,128)(2,1)} async-done(((bf16[1,1024,128]{2,1,0:T(8,128)(2,1)}), bf16[16,1024,128]{2,1,0:T(8,128)(2,1)}) %all-gather.5.cloned.1.call-update) | async-done | bytes 4194320 | tf_op jit(solution)/shard_map/all_gather | solution.py:305
  207.1 3.7 %convolution_bitcast_fusion = f32[1024,256]{1,0:T(8,128)S(1)} fusion(bf16[16,1024,128]{2,1,0:T(8,128)(2,1)} %all-gather.5.cloned.1.call-done, bf16[16,2,128,256]{3,2,1,0:T(8,128)(2,1)} %bitcast.53), kind=kOutput, calls=%fused_computation.3 | convolution fusion | flops 1073741824 | bytes 6291456 | tf_op jit(solution)/shard_map/str,srf->tf/dot_general | solution.py:306
  210.9 55.1 %all-gather.3.cloned.1.call-done = bf16[16,1024,128]{2,1,0:T(8,128)(2,1)} async-done(((bf16[1,1024,128]{2,1,0:T(8,128)(2,1)}), bf16[16,1024,128]{2,1,0:T(8,128)(2,1)}) %all-gather.3.cloned.1.call-update) | async-done | bytes 4194320 | tf_op jit(solution)/shard_map/all_gather | solution.py:305
  266.0 4.5 %fusion.1 = bf16[1024,256]{1,0:T(8,128)(2,1)} fusion(f32[1024,256]{1,0:T(8,128)S(1)} %convolution_bitcast_fusion, bf16[16,1024,128]{2,1,0:T(8,128)(2,1)} %all-gather.3.cloned.1.call-done, bf16[16,2,128,256]{3,2,1,0:T(8,128)(2,1)} %bitcast.54), kind=kOutput, calls=%fused_computation.6 | convolution fusion | flops 1074266112 | bytes 6815744 | tf_op jit(solution)/shard_map/str,srf->tf/dot_general | solution.py:306
  (25 shorter events, 4.9 us)
Async XLA Ops:
  6.5 5.8 %copy-start = (bf16[4096,256]{1,0:T(8,128)(2,1)S(1)}, bf16[4096,256]{1,0:T(8,128)(2,1)}, u32[]{:S(2)}) copy-start(bf16[4096,256]{1,0:T(8,128)(2,1)} %param.8) | copy-start | bytes 6291460
  6.5 200.6 %all-gather.5.cloned.1.call-start = ((), (), s32[]{:S(2)}) async-start(), calls=%async_computation.1 | async-start | bytes 4456448 | tf_op jit(solution)/shard_map/all_gather | solution.py:305
  26.6 51.1 %copy-start.1 = (bf16[8,128,2,256]{3,2,1,0:T(2,128)(2,1)S(1)}, bf16[8,128,2,256]{3,2,1,0:T(2,128)(2,1)}, u32[]{:S(2)}) copy-start(bf16[8,128,2,256]{3,2,1,0:T(2,128)(2,1)} %param.10) | copy-start | bytes 3145732
  139.5 126.5 %all-gather.3.cloned.1.call-start = ((), (), s32[]{:S(2)}) async-start(), calls=%async_computation | async-start | bytes 4456448 | tf_op jit(solution)/shard_map/all_gather | solution.py:305
Sparse Core Ops, SparseCore 0:
  139.6 67.4 all-gather.4
  209.9 56.0 all-gather.2

commit v9 on v7

--- a/solution.py
+++ b/solution.py
@@ -134,87 +134,91 @@
         peer_copy(ctx.at[me_s], back_ctx.at[s], cs.at[s], cr.at[s], (s, me_d)).wait_recv()
 
 
-def attend_kernel(scale, heads, e_ref, q_ref, kv0, kv1, kv2, ctx_ref, stats_ref):
-    for j, kv_ref in enumerate((kv0, kv1, kv2)):
-        width = heads * HD
-        for h in range(heads):
-            q = q_ref[0, j, :, h * HD:(h + 1) * HD]
-            k = kv_ref[0, :, h * HD:(h + 1) * HD]
-            v = kv_ref[0, :, width + h * HD:width + (h + 1) * HD]
-            s = lax.dot_general(
-                q, k, (((1,), (1,)), ((), ())), preferred_element_type=jnp.float32
-            ) * scale
-            top = jnp.max(s, axis=1, keepdims=True)
-            w = jnp.exp(s - top)
-            total = jnp.sum(w, axis=1, keepdims=True)
-            ctx = jnp.dot(w.astype(jnp.bfloat16), v, preferred_element_type=jnp.float32)
-            ctx_ref[0, j, :, h * HD:(h + 1) * HD] = (ctx / total).astype(ctx_ref.dtype)
-            stats_ref[0, j, :, 2 * h:2 * h + 1] = top
-            stats_ref[0, j, :, 2 * h + 1:2 * h + 2] = total
+def attend_kernel(scale, heads, e_ref, q_ref, kv_ref, ctx_ref, stats_ref):
+    n_src, cap = q_ref.shape[0], q_ref.shape[1]
+    width = heads * HD
+
+    def one_source(i, carry):
+        for j in range(cap):
+            kv = kv_ref.at[e_ref[i * cap + j]]
+            for h in range(heads):
+                q = q_ref[i, j, :, h * HD:(h + 1) * HD]
+                k = kv[:, h * HD:(h + 1) * HD]
+                v = kv[:, width + h * HD:width + (h + 1) * HD]
+                s = lax.dot_general(
+                    q, k, (((1,), (1,)), ((), ())), preferred_element_type=jnp.float32
+                ) * scale
+                top = jnp.max(s, axis=1, keepdims=True)
+                w = jnp.exp(s - top)
+                total = jnp.sum(w, axis=1, keepdims=True)
+                ctx = jnp.dot(w.astype(jnp.bfloat16), v, preferred_element_type=jnp.float32)
+                ctx_ref[i, j, :, h * HD:(h + 1) * HD] = (ctx / total).astype(ctx_ref.dtype)
+                stats_ref[i, j, :, 2 * h:2 * h + 1] = top
+                stats_ref[i, j, :, 2 * h + 1:2 * h + 2] = total
+        return carry
+
+    lax.fori_loop(0, n_src, one_source, 0)
+
+
+def vmem_whole(shape):
+    return pl.BlockSpec(shape, lambda *_: (0,) * len(shape))
 
 
 def attend(recv_q, recv_e, kv_flat, heads):
     n_src, cap, span, width = recv_q.shape
-    key_len = kv_flat.shape[1]
-
-    def kv_spec(j):
-        return pl.BlockSpec((1, key_len, kv_flat.shape[2]), lambda i, e: (e[i * CAP + j], 0, 0))
-
+    stats_shape = (n_src, cap, span, 2 * heads)
     grid_spec = pltpu.PrefetchScalarGridSpec(
         num_scalar_prefetch=1,
-        grid=(n_src,),
-        in_specs=[pl.BlockSpec((1, cap, span, width), lambda i, e: (i, 0, 0, 0))]
-        + [kv_spec(j) for j in range(CAP)],
-        out_specs=[
-            pl.BlockSpec((1, cap, span, width), lambda i, e: (i, 0, 0, 0)),
-            pl.BlockSpec((1, cap, span, 2 * heads), lambda i, e: (i, 0, 0, 0)),
-        ],
+        grid=(1,),
+        in_specs=[vmem_whole(recv_q.shape), vmem_whole(kv_flat.shape)],
+        out_specs=[vmem_whole(recv_q.shape), vmem_whole(stats_shape)],
     )
     return pl.pallas_call(
         functools.partial(attend_kernel, 1.0 / math.sqrt(HD), heads),
         grid_spec=grid_spec,
         out_shape=(
             jax.ShapeDtypeStruct(recv_q.shape, jnp.bfloat16),
-            jax.ShapeDtypeStruct((n_src, cap, span, 2 * heads), jnp.float32),
+            jax.ShapeDtypeStruct(stats_shape, jnp.float32),
         ),
-    )(recv_e, recv_q, kv_flat, kv_flat, kv_flat)
-
-
-def combine_kernel(heads, place_ref, count_ref, c0, c1, s0, s1, out_ref):
-    live1 = count_ref[pl.program_id(0)] > 1
-    for h in range(heads):
-        cols = slice(h * HD, (h + 1) * HD)
-        m0 = s0[0, :, 2 * h:2 * h + 1]
-        l0 = s0[0, :, 2 * h + 1:2 * h + 2]
-        m1 = s1[0, :, 2 * h:2 * h + 1]
-        l1 = s1[0, :, 2 * h + 1:2 * h + 2]
-        best = jnp.where(live1, jnp.maximum(m0, m1), m0)
-        a0 = jnp.exp(m0 - best) * l0
-        a1 = jnp.where(live1, jnp.exp(m1 - best) * l1, 0.0)
-        v0 = c0[0, :, cols].astype(jnp.float32)
-        v1 = jnp.where(live1, c1[0, :, cols].astype(jnp.float32), 0.0)
-        out_ref[0, :, cols] = ((a0 * v0 + a1 * v1) / (a0 + a1)).astype(out_ref.dtype)
+    )(recv_e, recv_q, kv_flat)
+
+
+def combine_kernel(heads, place_ref, count_ref, ctx_ref, stats_ref, out_ref):
+    def one_span(c, carry):
+        p0 = place_ref[c * K]
+        p1 = place_ref[c * K + 1]
+        live1 = count_ref[c] > 1
+        for h in range(heads):
+            cols = slice(h * HD, (h + 1) * HD)
+            m0 = stats_ref[p0, :, 2 * h:2 * h + 1]
+            l0 = stats_ref[p0, :, 2 * h + 1:2 * h + 2]
+            m1 = stats_ref[p1, :, 2 * h:2 * h + 1]
+            l1 = stats_ref[p1, :, 2 * h + 1:2 * h + 2]
+            best = jnp.where(live1, jnp.maximum(m0, m1), m0)
+            a0 = jnp.exp(m0 - best) * l0
+            a1 = jnp.where(live1, jnp.exp(m1 - best) * l1, 0.0)
+            v0 = ctx_ref[p0, :, cols].astype(jnp.float32)
+            v1 = jnp.where(live1, ctx_ref[p1, :, cols].astype(jnp.float32), 0.0)
+            out_ref[c, :, cols] = ((a0 * v0 + a1 * v1) / (a0 + a1)).astype(out_ref.dtype)
+        return carry
+
+    lax.fori_loop(0, out_ref.shape[0], one_span, 0)
 
 
 def combine(back_ctx, back_stats, place, neighbour_count, heads):
     places, span, width = back_ctx.shape
     spans = neighbour_count.shape[0]
-
-    def by_place(k, shape):
-        return pl.BlockSpec((1,) + shape, lambda c, p, n: (p[c * K + k], 0, 0))
-
     grid_spec = pltpu.PrefetchScalarGridSpec(
         num_scalar_prefetch=2,
-        grid=(spans,),
-        in_specs=[by_place(0, (span, width)), by_place(1, (span, width)),
-                  by_place(0, (span, 2 * heads)), by_place(1, (span, 2 * heads))],
-        out_specs=pl.BlockSpec((1, span, width), lambda c, p, n: (c, 0, 0)),
+        grid=(1,),
+        in_specs=[vmem_whole(back_ctx.shape), vmem_whole(back_stats.shape)],
+        out_specs=vmem_whole((spans, span, width)),
     )
     return pl.pallas_call(
         functools.partial(combine_kernel, heads),
         grid_spec=grid_spec,
         out_shape=jax.ShapeDtypeStruct((spans, span, width), jnp.bfloat16),
-    )(place, neighbour_count, back_ctx, back_ctx, back_stats, back_stats)
+    )(place, neighbour_count, back_ctx, back_stats)
 
 
 def any_spec():

time: 264 us -> 259 us (0.981)
  Pallas kernels: 131 us -> 128 us
    pallas_call x1, Pallas kernels: 10.5 us -> 6.71 us  [combine(): pl.pallas_call(functools.partial(combine_kernel, heads), grid_spec=grid_s...]
where the time goes in v9:
time: 259 us
  Pallas kernels  128 us (49%)
  waiting for transfers between devices  79.4 us (31%)
  local copies, waits for them, and re-layouts  22 us (8%)
  matrix products  13.6 us (5%)
  between operations  13.4 us (5%)
    all_gather x1, waiting for transfers between devices, on_device(): contexts = lax.all_gather(context, 'db', axis=0, tiled=False)  79.4 us
    pallas_call x1, Pallas kernels, exchange_out(): pl.pallas_call(functools.partial(out_kernel, n_seq, n_db, features), out_...  49.5 us
    pallas_call x1, Pallas kernels, exchange_back(): pl.pallas_call(functools.partial(back_kernel, n_seq), out_shape=(jax.Shap...  43.3 us
    pallas_call x1, Pallas kernels, attend(): pl.pallas_call(functools.partial(attend_kernel, 1.0 / math.sqrt(HD), head...  28.5 us
    dot_general x1, matrix products, on_device(): jnp.einsum('str,srf->tf', contexts, weight_cols, preferred_element_type=j...  7.1 us
    pallas_call x1, Pallas kernels, combine(): pl.pallas_call(functools.partial(combine_kernel, heads), grid_spec=grid_s...  6.71 us
    dot_general x1, matrix products, on_device(): jnp.dot(decoder_states, query_weight, preferred_element_type=jnp.float32)  6.5 us
  transfers between devices with their start and end apart: 1, of which 1 were waited for; matrix products, arithmetic and copies ran while one was open for 0% of the time, Pallas kernels for 0%

profile of v9, /device:TPU:1, one launch (start us, length us, event | category | flops | bytes accessed | tf_op | source)
XLA Modules:
  0.0 258.8 jit_solution(9218702065110379387)
XLA Ops:
  6.5 0.9 iota_compare_fusion.1
  7.5 0.1 lt.68
  7.6 0.7 broadcast_multiply_fusion
  8.3 0.8 copy.21
  9.2 0.8 copy.23
  10.2 0.2 convert_reduce_fusion
  10.4 0.5 multiply_add_fusion.place_ref
  10.9 0.7 scatter_custom_fusion.1
  11.7 0.6 pad.4.send_e
  12.3 2.5 reshape.153.kv_ref
  14.8 6.5 %convolution_convert_fusion = bf16[1024,256]{1,0:T(8,128)(2,1)} fusion(bf16[1024,4096]{1,0:T(8,128)(2,1)} %param.7, bf16[4096,256]{1,0:T(8,128)(2,1)S(1)} %copy-done), kind=kOutput, calls=%fused_computation.5 | convolution fusion | flops 2147745792 | bytes 11010048 | tf_op jit(solution)/shard_map/dot_general | solution.py:280
  21.3 1.7 gather_fusion
  23.0 1.3 broadcast_in_dim.8
  24.3 4.7 %scatter_fusion = bf16[48,64,256]{2,1,0:T(8,128)(2,1)} fusion(bf16[48,64,256]{2,1,0:T(8,128)(2,1)} %broadcast_in_dim.8, s32[32]{0:T(128)S(1)} %fusion.3, bf16[32,64,256]{2,1,0:T(8,128)(2,1)S(1)} %gather_fusion), kind=kCustom, calls=%fused_computation.1 | custom fusion | bytes 3145856 | tf_op jit(solution)/shard_map/scatter | solution.py:289
  29.0 49.5 %shard_map.73 = (bf16[16,3,64,256]{3,2,1,0:T(8,128)(2,1)}, s32[16,128]{1,0:T(8,128)}, bf16[16,256,256]{2,1,0:T(8,128)(2,1)}) custom-call(bf16[16,3,64,256]{3,2,1,0:T(8,128)(2,1)} %bitcast.26, s32[16,128]{1,0:T(8,128)} %pad.4.send_e, bf16[256,4096]{1,0:T(8,128)(2,1)} %w_loc.1), custom_call_target="tpu_custom_call" | custom-call | tf_op jit(solution)/shard_map/pallas_call | solution.py:231
  78.5 1.3 reshape.152.e_ref
  79.8 28.5 %shard_map.74 = (bf16[16,3,64,256]{3,2,1,0:T(8,128)(2,1)}, f32[16,3,64,4]{3,2,1,0:T(8,128)}) custom-call(s32[48]{0:T(128)} %reshape.152.e_ref, bf16[16,3,64,256]{3,2,1,0:T(8,128)(2,1)} %get-tuple-element.13.q_ref, bf16[8,128,512]{2,1,0:T(8,128)(2,1)} %reshape.153.kv_ref), custom_call_target="tpu_custom_call" | custom-call | tf_op jit(solution)/shard_map/pallas_call | solution.py:176
  108.4 2.7 %copy.24 = f32[16,3,64,4]{0,3,2,1:T(4,128)S(1)} copy(f32[16,3,64,4]{3,2,1,0:T(8,128)} %get-tuple-element.15) | data formatting | bytes 98304 | tf_op jit(solution)/shard_map/pallas_call | solution.py:176
  111.0 0.8 copy.25.stats
  111.8 43.3 %shard_map.75 = (bf16[16,3,64,256]{3,2,1,0:T(8,128)(2,1)}, f32[16,6,128]{2,1,0:T(8,128)}) custom-call(bf16[16,3,64,256]{3,2,1,0:T(8,128)(2,1)} %get-tuple-element.14.ctx, f32[16,6,128]{2,1,0:T(8,128)} %copy.25.stats), custom_call_target="tpu_custom_call" | custom-call | tf_op jit(solution)/shard_map/pallas_call | solution.py:250
  155.1 3.6 %reshape.156.stats_ref = f32[48,64,4]{2,1,0:T(8,128)} reshape(f32[16,6,128]{2,1,0:T(8,128)} %get-tuple-element.17) | data formatting | bytes 98304 | tf_op jit(solution)/shard_map/reshape | solution.py:303
  158.7 6.7 %shard_map.76 = bf16[16,64,256]{2,1,0:T(8,128)(2,1)} custom-call(s32[32]{0:T(128)} %multiply_add_fusion.place_ref, s32[16]{0:T(128)} %count_ref.1, bf16[48,64,256]{2,1,0:T(8,128)(2,1)} %bitcast.29, f32[48,64,4]{2,1,0:T(8,128)} %reshape.156.stats_ref), custom_call_target="tpu_custom_call" | custom-call | tf_op jit(solution)/shard_map/pallas_call | solution.py:217
  165.5 79.4 %all-gather.2.cloned.1.call-done = bf16[16,1024,256]{2,1,0:T(8,128)(2,1)} async-done(((bf16[1,1024,256]{2,1,0:T(8,128)(2,1)}), bf16[16,1024,256]{2,1,0:T(8,128)(2,1)}) %all-gather.2.cloned.1.call-update) | async-done | bytes 8388624 | tf_op jit(solution)/shard_map/all_gather | solution.py:307
  244.9 7.1 %fusion = bf16[1024,256]{1,0:T(8,128)(2,1)} fusion(bf16[16,1024,256]{2,1,0:T(8,128)(2,1)} %all-gather.2.cloned.1.call-done, bf16[16,256,256]{2,1,0:T(8,128)(2,1)} %get-tuple-element.18), kind=kOutput, calls=%fused_computation.4 | convolution fusion | flops 2147745792 | bytes 11010048 | tf_op jit(solution)/shard_map/str,srf->tf/dot_general | solution.py:308
  (13 shorter events, 0.6 us)
Async XLA Ops:
  6.5 8.3 %copy-start = (bf16[4096,256]{1,0:T(8,128)(2,1)S(1)}, bf16[4096,256]{1,0:T(8,128)(2,1)}, u32[]{:S(2)}) copy-start(bf16[4096,256]{1,0:T(8,128)(2,1)} %param.8) | copy-start | bytes 6291460
  6.5 238.4 %all-gather.2.cloned.1.call-start = ((), (), s32[]{:S(2)}) async-start(), calls=%async_computation | async-start | bytes 8912896 | tf_op jit(solution)/shard_map/all_gather | solution.py:307
Sparse Core Ops, SparseCore 0:
  165.6 79.2 all-gather.1

commit v10 on v9

--- a/solution.py
+++ b/solution.py
@@ -134,30 +134,37 @@
         peer_copy(ctx.at[me_s], back_ctx.at[s], cs.at[s], cr.at[s], (s, me_d)).wait_recv()
 
 
-def attend_kernel(scale, heads, e_ref, q_ref, kv_ref, ctx_ref, stats_ref):
-    n_src, cap = q_ref.shape[0], q_ref.shape[1]
-    width = heads * HD
-
-    def one_source(i, carry):
-        for j in range(cap):
-            kv = kv_ref.at[e_ref[i * cap + j]]
-            for h in range(heads):
-                q = q_ref[i, j, :, h * HD:(h + 1) * HD]
-                k = kv[:, h * HD:(h + 1) * HD]
-                v = kv[:, width + h * HD:width + (h + 1) * HD]
-                s = lax.dot_general(
-                    q, k, (((1,), (1,)), ((), ())), preferred_element_type=jnp.float32
-                ) * scale
-                top = jnp.max(s, axis=1, keepdims=True)
-                w = jnp.exp(s - top)
-                total = jnp.sum(w, axis=1, keepdims=True)
-                ctx = jnp.dot(w.astype(jnp.bfloat16), v, preferred_element_type=jnp.float32)
-                ctx_ref[i, j, :, h * HD:(h + 1) * HD] = (ctx / total).astype(ctx_ref.dtype)
-                stats_ref[i, j, :, 2 * h:2 * h + 1] = top
-                stats_ref[i, j, :, 2 * h + 1:2 * h + 2] = total
+def attend_kernel(scale, heads, rows, e_ref, q_ref, kv_ref, ctx_ref, stats_ref):
+    key_len = SPAN * 2
+    keys_total, width = kv_ref.shape[0], heads * HD
+    per_tile = rows // SPAN
+    col_block = lax.broadcasted_iota(jnp.int32, (1, keys_total), 1) // key_len
+    row_block = lax.broadcasted_iota(jnp.int32, (rows, 1), 0) // SPAN
+
+    def one_tile(t, carry):
+        start = pl.multiple_of(t * rows, rows)
+        row_entry = jnp.zeros((rows, 1), jnp.int32)
+        for j in range(per_tile):
+            row_entry = jnp.where(row_block == j, e_ref[t * per_tile + j], row_entry)
+        named = col_block == row_entry
+        for h in range(heads):
+            q = q_ref[pl.ds(start, rows), h * HD:(h + 1) * HD]
+            k = kv_ref[:, h * HD:(h + 1) * HD]
+            v = kv_ref[:, width + h * HD:width + (h + 1) * HD]
+            s = lax.dot_general(
+                q, k, (((1,), (1,)), ((), ())), preferred_element_type=jnp.float32
+            ) * scale
+            s = jnp.where(named, s, -jnp.inf)
+            top = jnp.max(s, axis=1, keepdims=True)
+            w = jnp.exp(s - top)
+            total = jnp.sum(w, axis=1, keepdims=True)
+            ctx = jnp.dot(w.astype(jnp.bfloat16), v, preferred_element_type=jnp.float32)
+            ctx_ref[pl.ds(start, rows), h * HD:(h + 1) * HD] = (ctx / total).astype(ctx_ref.dtype)
+            stats_ref[pl.ds(start, rows), 2 * h:2 * h + 1] = top
+            stats_ref[pl.ds(start, rows), 2 * h + 1:2 * h + 2] = total
         return carry
 
-    lax.fori_loop(0, n_src, one_source, 0)
+    lax.fori_loop(0, q_ref.shape[0] // rows, one_tile, 0)
 
 
 def vmem_whole(shape):
@@ -166,21 +173,24 @@
 
 def attend(recv_q, recv_e, kv_flat, heads):
     n_src, cap, span, width = recv_q.shape
-    stats_shape = (n_src, cap, span, 2 * heads)
+    q_rows = recv_q.reshape(n_src * cap * span, width)
+    kv_rows = kv_flat.reshape(-1, kv_flat.shape[2])
+    stats_shape = (q_rows.shape[0], 2 * heads)
     grid_spec = pltpu.PrefetchScalarGridSpec(
         num_scalar_prefetch=1,
         grid=(1,),
-        in_specs=[vmem_whole(recv_q.shape), vmem_whole(kv_flat.shape)],
-        out_specs=[vmem_whole(recv_q.shape), vmem_whole(stats_shape)],
-    )
-    return pl.pallas_call(
-        functools.partial(attend_kernel, 1.0 / math.sqrt(HD), heads),
+        in_specs=[vmem_whole(q_rows.shape), vmem_whole(kv_rows.shape)],
+        out_specs=[vmem_whole(q_rows.shape), vmem_whole(stats_shape)],
+    )
+    ctx, stats = pl.pallas_call(
+        functools.partial(attend_kernel, 1.0 / math.sqrt(HD), heads, 4 * span),
         grid_spec=grid_spec,
         out_shape=(
-            jax.ShapeDtypeStruct(recv_q.shape, jnp.bfloat16),
+            jax.ShapeDtypeStruct(q_rows.shape, jnp.bfloat16),
             jax.ShapeDtypeStruct(stats_shape, jnp.float32),
         ),
-    )(recv_e, recv_q, kv_flat)
+    )(recv_e, q_rows, kv_rows)
+    return ctx.reshape(recv_q.shape), stats.reshape(n_src, cap, span, 2 * heads)
 
 
 def combine_kernel(heads, place_ref, count_ref, ctx_ref, stats_ref, out_ref):

time: 259 us -> 249 us (0.961)
  Pallas kernels: 128 us -> 117 us
    pallas_call x1, Pallas kernels: 28.5 us -> 17.7 us  [attend(): pl.pallas_call(functools.partial(attend_kernel, 1.0 / math.sqrt(HD), head...]
    reshape x2 -> x0, local copies, waits for them, and re-layouts: 3.32 us -> none  [the longest x1 2.52 us: on_device(): neighbour_kv.reshape(neighbour_kv.shape[0], key_len, 2 * row_width)]
    another operation x0 -> x1, local copies, waits for them, and re-layouts: none -> 3.15 us  [on_device(): stats.reshape(n_seq, CAP * SPAN * 2 * heads_here // LANES, LANES)]
    pallas_call x1 -> x0, local copies, waits for them, and re-layouts: 2.66 us -> none  [attend(): pl.pallas_call(functools.partial(attend_kernel, 1.0 / math.sqrt(HD), head...]
where the time goes in v10:
time: 249 us; the launch traced here: 248 us
  Pallas kernels  117 us (47%)
  waiting for transfers between devices  79.7 us (32%)
  local copies, waits for them, and re-layouts  21.7 us (9%)
  matrix products  13.6 us (5%)
  between operations  13.4 us (5%)
    all_gather x1, waiting for transfers between devices, on_device(): contexts = lax.all_gather(context, 'db', axis=0, tiled=False)  79.7 us
    pallas_call x1, Pallas kernels, exchange_out(): pl.pallas_call(functools.partial(out_kernel, n_seq, n_db, features), out_...  49.7 us
    pallas_call x1, Pallas kernels, exchange_back(): pl.pallas_call(functools.partial(back_kernel, n_seq), out_shape=(jax.Shap...  43.3 us
    pallas_call x1, Pallas kernels, attend(): pl.pallas_call(functools.partial(attend_kernel, 1.0 / math.sqrt(HD), head...  17.7 us
    dot_general x1, matrix products, on_device(): jnp.einsum('str,srf->tf', contexts, weight_cols, preferred_element_type=j...  7.1 us
    pallas_call x1, Pallas kernels, combine(): pl.pallas_call(functools.partial(combine_kernel, heads), grid_spec=grid_s...  6.71 us
    dot_general x1, matrix products, on_device(): jnp.dot(decoder_states, query_weight, preferred_element_type=jnp.float32)  6.51 us
  transfers between devices with their start and end apart: 1, of which 1 were waited for; matrix products, arithmetic and copies ran while one was open for 0% of the time, Pallas kernels for 0%

profile of v10, /device:TPU:1, one launch (start us, length us, event | category | flops | bytes accessed | tf_op | source)
XLA Modules:
  0.0 248.2 jit_solution(3040681702499474883)
XLA Ops:
  6.5 0.9 iota_compare_fusion.1
  7.4 0.1 lt.72
  7.5 0.1 lt.68
  7.6 0.7 broadcast_multiply_fusion
  8.3 0.8 copy.17
  9.2 0.8 copy.19
  10.2 0.2 convert_reduce_fusion
  10.4 0.5 multiply_add_fusion.place_ref
  10.9 0.7 scatter_custom_fusion.1
  11.7 0.6 pad.4.send_e
  12.3 2.5 copy.20
  14.7 6.5 %convolution_convert_fusion = bf16[1024,256]{1,0:T(8,128)(2,1)} fusion(bf16[1024,4096]{1,0:T(8,128)(2,1)} %param.7, bf16[4096,256]{1,0:T(8,128)(2,1)S(1)} %copy-done), kind=kOutput, calls=%fused_computation.5 | convolution fusion | flops 2147745792 | bytes 11010048 | tf_op jit(solution)/shard_map/dot_general | solution.py:290
  21.2 1.7 gather_fusion
  22.9 1.3 broadcast_in_dim.8
  24.2 4.8 %scatter_fusion = bf16[48,64,256]{2,1,0:T(8,128)(2,1)} fusion(bf16[48,64,256]{2,1,0:T(8,128)(2,1)} %broadcast_in_dim.8, s32[32]{0:T(128)S(1)} %fusion.3, bf16[32,64,256]{2,1,0:T(8,128)(2,1)S(1)} %gather_fusion), kind=kCustom, calls=%fused_computation.1 | custom fusion | bytes 3145856 | tf_op jit(solution)/shard_map/scatter | solution.py:299
  29.0 49.7 %shard_map.73 = (bf16[16,3,64,256]{3,2,1,0:T(8,128)(2,1)}, s32[16,128]{1,0:T(8,128)}, bf16[16,256,256]{2,1,0:T(8,128)(2,1)}) custom-call(bf16[16,3,64,256]{3,2,1,0:T(8,128)(2,1)} %bitcast.30, s32[16,128]{1,0:T(8,128)} %pad.4.send_e, bf16[256,4096]{1,0:T(8,128)(2,1)} %w_loc.1), custom_call_target="tpu_custom_call" | custom-call | tf_op jit(solution)/shard_map/pallas_call | solution.py:241
  78.7 1.3 reshape.152.e_ref
  80.0 17.7 %shard_map.74 = (bf16[3072,256]{1,0:T(8,128)(2,1)}, f32[3072,4]{1,0:T(8,128)}) custom-call(s32[48]{0:T(128)} %reshape.152.e_ref, bf16[3072,256]{1,0:T(8,128)(2,1)} %bitcast.34, bf16[1024,512]{1,0:T(8,128)(2,1)} %bitcast.31), custom_call_target="tpu_custom_call" | custom-call | tf_op jit(solution)/shard_map/pallas_call | solution.py:185
  97.8 3.1 %reshape_reshape.7.stats = f32[16,6,128]{2,1,0:T(8,128)} reshape(f32[3072,4]{1,0:T(8,128)} %get-tuple-element.15) | data formatting | bytes 98304 | tf_op jit(solution)/shard_map/reshape;reshape | solution.py:310
  100.9 43.3 %shard_map.75 = (bf16[16,3,64,256]{3,2,1,0:T(8,128)(2,1)}, f32[16,6,128]{2,1,0:T(8,128)}) custom-call(bf16[16,3,64,256]{3,2,1,0:T(8,128)(2,1)} %bitcast.35, f32[16,6,128]{2,1,0:T(8,128)} %reshape_reshape.7.stats), custom_call_target="tpu_custom_call" | custom-call | tf_op jit(solution)/shard_map/pallas_call | solution.py:260
  144.2 3.6 %reshape.156.stats_ref = f32[48,64,4]{2,1,0:T(8,128)} reshape(f32[16,6,128]{2,1,0:T(8,128)} %get-tuple-element.17) | data formatting | bytes 98304 | tf_op jit(solution)/shard_map/reshape | solution.py:313
  147.8 6.7 %shard_map.76 = bf16[16,64,256]{2,1,0:T(8,128)(2,1)} custom-call(s32[32]{0:T(128)} %multiply_add_fusion.place_ref, s32[16]{0:T(128)} %count_ref.1, bf16[48,64,256]{2,1,0:T(8,128)(2,1)} %bitcast.36, f32[48,64,4]{2,1,0:T(8,128)} %reshape.156.stats_ref), custom_call_target="tpu_custom_call" | custom-call | tf_op jit(solution)/shard_map/pallas_call | solution.py:227
  154.5 79.7 %all-gather.2.cloned.1.call-done = bf16[16,1024,256]{2,1,0:T(8,128)(2,1)} async-done(((bf16[1,1024,256]{2,1,0:T(8,128)(2,1)}), bf16[16,1024,256]{2,1,0:T(8,128)(2,1)}) %all-gather.2.cloned.1.call-update) | async-done | bytes 8388624 | tf_op jit(solution)/shard_map/all_gather | solution.py:317
  234.2 7.1 %fusion = bf16[1024,256]{1,0:T(8,128)(2,1)} fusion(bf16[16,1024,256]{2,1,0:T(8,128)(2,1)} %all-gather.2.cloned.1.call-done, bf16[16,256,256]{2,1,0:T(8,128)(2,1)} %get-tuple-element.18), kind=kOutput, calls=%fused_computation.4 | convolution fusion | flops 2147745792 | bytes 11010048 | tf_op jit(solution)/shard_map/str,srf->tf/dot_general | solution.py:318
  (12 shorter events, 0.5 us)
Async XLA Ops:
  6.5 8.2 %copy-start = (bf16[4096,256]{1,0:T(8,128)(2,1)S(1)}, bf16[4096,256]{1,0:T(8,128)(2,1)}, u32[]{:S(2)}) copy-start(bf16[4096,256]{1,0:T(8,128)(2,1)} %param.8) | copy-start | bytes 6291460
  6.5 227.7 %all-gather.2.cloned.1.call-start = ((), (), s32[]{:S(2)}) async-start(), calls=%async_computation | async-start | bytes 8912896 | tf_op jit(solution)/shard_map/all_gather | solution.py:317
Sparse Core Ops, SparseCore 0:
  154.6 79.5 all-gather.1

commit v11 on v10

--- a/solution.py
+++ b/solution.py
@@ -6,7 +6,7 @@
 from jax import lax
 from jax.experimental import pallas as pl
 from jax.experimental.pallas import tpu as pltpu
-from jax.sharding import PartitionSpec as P
+from jax.sharding import Mesh, PartitionSpec as P
 
 HD = 128
 SPAN = 64
@@ -14,6 +14,17 @@
 CAP = 3
 LANES = 128
 MESH = pl.DeviceIdType.MESH
+DB = ("xh", "yy", "cc")
+
+
+def db_coords(d, n_y, n_core):
+    return (d // (n_y * n_core), lax.rem(d // n_core, n_y), lax.rem(d, n_core))
+
+
+def my_db():
+    n_y, n_core = lax.psum(1, "yy"), lax.psum(1, "cc")
+    xh, yy, cc = lax.axis_index("xh"), lax.axis_index("yy"), lax.axis_index("cc")
+    return (xh * n_y + yy) * n_core + cc, (xh, yy, cc), n_y, n_core
 
 
 def slot_places(neighbour_shard, neighbour_count):
@@ -38,7 +49,13 @@
 def out_kernel(n_seq, n_db, features, send_q, send_e, w_loc, recv_q, recv_e, w_cols,
                qs, qr, es, er, ws, wr, ls):
     me_s = lax.axis_index("seq")
-    me_d = lax.axis_index("db")
+    me_d, mine, n_y, n_core = my_db()
+
+    def seq_peer(d):
+        return (d,) + mine
+
+    def db_peer(d):
+        return (me_s,) + db_coords(d, n_y, n_core)
 
     def w_src(d):
         return w_loc.at[:, pl.ds(pl.multiple_of(d * features, features), features)]
@@ -47,12 +64,12 @@
 
     @pl.loop(1, n_seq)
     def _(o):
-        pl.semaphore_signal(barrier, inc=1, device_id=(lax.rem(me_s + o, n_seq), me_d),
+        pl.semaphore_signal(barrier, inc=1, device_id=seq_peer(lax.rem(me_s + o, n_seq)),
                             device_id_type=MESH)
 
     @pl.loop(1, n_db)
     def _(o):
-        pl.semaphore_signal(barrier, inc=1, device_id=(me_s, lax.rem(me_d + o, n_db)),
+        pl.semaphore_signal(barrier, inc=1, device_id=db_peer(lax.rem(me_d + o, n_db)),
                             device_id_type=MESH)
 
     pl.semaphore_wait(barrier, (n_seq - 1) + (n_db - 1))
@@ -68,13 +85,13 @@
     @pl.loop(1, n_db)
     def _(o):
         d = lax.rem(me_d + o, n_db)
-        peer_copy(w_src(d), w_cols.at[me_d], ws.at[d], wr.at[me_d], (me_s, d)).start()
+        peer_copy(w_src(d), w_cols.at[me_d], ws.at[d], wr.at[me_d], db_peer(d)).start()
 
     @pl.loop(1, n_seq)
     def _(o):
         d = lax.rem(me_s + o, n_seq)
-        peer_copy(send_e.at[d], recv_e.at[me_s], es.at[d], er.at[me_s], (d, me_d)).start()
-        peer_copy(send_q.at[d], recv_q.at[me_s], qs.at[d], qr.at[me_s], (d, me_d)).start()
+        peer_copy(send_e.at[d], recv_e.at[me_s], es.at[d], er.at[me_s], seq_peer(d)).start()
+        peer_copy(send_q.at[d], recv_q.at[me_s], qs.at[d], qr.at[me_s], seq_peer(d)).start()
 
     for c in own:
         c.wait()
@@ -83,27 +100,31 @@
     def _(o):
         d = lax.rem(me_s + o, n_seq)
         s = lax.rem(me_s + n_seq - o, n_seq)
-        peer_copy(send_e.at[d], recv_e.at[me_s], es.at[d], er.at[me_s], (d, me_d)).wait_send()
-        peer_copy(send_q.at[d], recv_q.at[me_s], qs.at[d], qr.at[me_s], (d, me_d)).wait_send()
-        peer_copy(send_e.at[me_s], recv_e.at[s], es.at[s], er.at[s], (s, me_d)).wait_recv()
-        peer_copy(send_q.at[me_s], recv_q.at[s], qs.at[s], qr.at[s], (s, me_d)).wait_recv()
+        peer_copy(send_e.at[d], recv_e.at[me_s], es.at[d], er.at[me_s], seq_peer(d)).wait_send()
+        peer_copy(send_q.at[d], recv_q.at[me_s], qs.at[d], qr.at[me_s], seq_peer(d)).wait_send()
+        peer_copy(send_e.at[me_s], recv_e.at[s], es.at[s], er.at[s], seq_peer(s)).wait_recv()
+        peer_copy(send_q.at[me_s], recv_q.at[s], qs.at[s], qr.at[s], seq_peer(s)).wait_recv()
 
     @pl.loop(1, n_db)
     def _(o):
         d = lax.rem(me_d + o, n_db)
         s = lax.rem(me_d + n_db - o, n_db)
-        peer_copy(w_src(d), w_cols.at[me_d], ws.at[d], wr.at[me_d], (me_s, d)).wait_send()
-        peer_copy(w_src(me_d), w_cols.at[s], ws.at[s], wr.at[s], (me_s, s)).wait_recv()
+        peer_copy(w_src(d), w_cols.at[me_d], ws.at[d], wr.at[me_d], db_peer(d)).wait_send()
+        peer_copy(w_src(me_d), w_cols.at[s], ws.at[s], wr.at[s], db_peer(s)).wait_recv()
 
 
 def back_kernel(n_seq, ctx, stats, back_ctx, back_stats, cs, cr, ss, sr, ls):
     me_s = lax.axis_index("seq")
-    me_d = lax.axis_index("db")
+    _, mine, _, _ = my_db()
+
+    def seq_peer(d):
+        return (d,) + mine
+
     barrier = pltpu.get_barrier_semaphore()
 
     @pl.loop(1, n_seq)
     def _(o):
-        pl.semaphore_signal(barrier, inc=1, device_id=(lax.rem(me_s + o, n_seq), me_d),
+        pl.semaphore_signal(barrier, inc=1, device_id=seq_peer(lax.rem(me_s + o, n_seq)),
                             device_id_type=MESH)
 
     pl.semaphore_wait(barrier, n_seq - 1)
@@ -118,8 +139,8 @@
     @pl.loop(1, n_seq)
     def _(o):
         d = lax.rem(me_s + o, n_seq)
-        peer_copy(stats.at[d], back_stats.at[me_s], ss.at[d], sr.at[me_s], (d, me_d)).start()
-        peer_copy(ctx.at[d], back_ctx.at[me_s], cs.at[d], cr.at[me_s], (d, me_d)).start()
+        peer_copy(stats.at[d], back_stats.at[me_s], ss.at[d], sr.at[me_s], seq_peer(d)).start()
+        peer_copy(ctx.at[d], back_ctx.at[me_s], cs.at[d], cr.at[me_s], seq_peer(d)).start()
 
     for c in own:
         c.wait()
@@ -128,10 +149,10 @@
     def _(o):
         d = lax.rem(me_s + o, n_seq)
         s = lax.rem(me_s + n_seq - o, n_seq)
-        peer_copy(stats.at[d], back_stats.at[me_s], ss.at[d], sr.at[me_s], (d, me_d)).wait_send()
-        peer_copy(ctx.at[d], back_ctx.at[me_s], cs.at[d], cr.at[me_s], (d, me_d)).wait_send()
-        peer_copy(stats.at[me_s], back_stats.at[s], ss.at[s], sr.at[s], (s, me_d)).wait_recv()
-        peer_copy(ctx.at[me_s], back_ctx.at[s], cs.at[s], cr.at[s], (s, me_d)).wait_recv()
+        peer_copy(stats.at[d], back_stats.at[me_s], ss.at[d], sr.at[me_s], seq_peer(d)).wait_send()
+        peer_copy(ctx.at[d], back_ctx.at[me_s], cs.at[d], cr.at[me_s], seq_peer(d)).wait_send()
+        peer_copy(stats.at[me_s], back_stats.at[s], ss.at[s], sr.at[s], seq_peer(s)).wait_recv()
+        peer_copy(ctx.at[me_s], back_ctx.at[s], cs.at[s], cr.at[s], seq_peer(s)).wait_recv()
 
 
 def attend_kernel(scale, heads, rows, e_ref, q_ref, kv_ref, ctx_ref, stats_ref):
@@ -285,7 +306,7 @@
     heads_here = row_width // HD
     key_len = neighbour_kv.shape[1]
     n_seq = lax.psum(1, "seq")
-    n_db = lax.psum(1, "db")
+    n_db = lax.psum(1, DB)
     places_total = n_seq * CAP
     queries = jnp.dot(decoder_states, query_weight, preferred_element_type=jnp.float32).astype(
         jnp.bfloat16
@@ -314,24 +335,30 @@
     context = combine(back_ctx, back_stats, place, neighbour_count, heads_here)
     context = context.reshape(tok_rows, row_width)
 
-    contexts = lax.all_gather(context, "db", axis=0, tiled=False)
+    n_core = lax.psum(1, "cc")
+    contexts = lax.all_gather(context, ("xh", "yy"), axis=0, tiled=False)
+    contexts = lax.all_gather(contexts, "cc", axis=0, tiled=False)
+    weight_cols = weight_cols.reshape(n_db // n_core, n_core, row_width, weight_cols.shape[2])
     out = jnp.einsum(
-        "str,srf->tf", contexts, weight_cols, preferred_element_type=jnp.float32
+        "cgtr,gcrf->tf", contexts, weight_cols, preferred_element_type=jnp.float32
     )
     return out.astype(jnp.bfloat16)
 
 
 def solution(mesh):
+    n_core, n_xh = 2, 2
+    n_y = mesh.shape["db"] // (n_core * n_xh)
+    fine = Mesh(mesh.devices.reshape(mesh.shape["seq"], n_xh, n_y, n_core), ("seq",) + DB)
     in_specs = (
         P("seq", None),
-        P(None, "db"),
-        P("db", None),
-        P("seq", None, None, "db"),
+        P(None, DB),
+        P(DB, None),
+        P("seq", None, None, DB),
         P("seq", None),
         P("seq", None),
         P("seq"),
     )
-    out_specs = P("seq", "db")
+    out_specs = P("seq", DB)
     return jax.shard_map(
-        on_device, mesh=mesh, in_specs=in_specs, out_specs=out_specs, check_vma=False
-    )
+        on_device, mesh=fine, in_specs=in_specs, out_specs=out_specs, check_vma=False
+    )

time: 249 us -> 272 us (1.092)
  waiting for transfers between devices: 79.7 us -> 103 us
    all_gather x1 -> x2, waiting for transfers between devices: 79.7 us -> 103 us  [the longest x1 77.3 us: on_device(): contexts = lax.all_gather(context, ('xh', 'yy'), axis=0, tiled=False)]
  transfers between devices with their start and end apart: 1 -> 2, of which waited for: 1 -> 2; matrix products, arithmetic and copies ran while one was open for 0% -> 0% of each run, Pallas kernels for 0% -> 0%
where the time goes in v11:
time: 272 us
  Pallas kernels  117 us (43%)
  waiting for transfers between devices  103 us (38%)
  local copies, waits for them, and re-layouts  21.5 us (8%)
  matrix products  13.6 us (5%)
  between operations  13.5 us (5%)
    all_gather x1, waiting for transfers between devices, on_device(): contexts = lax.all_gather(context, ('xh', 'yy'), axis=0, tiled=False)  77.3 us
    pallas_call x1, Pallas kernels, exchange_out(): pl.pallas_call(functools.partial(out_kernel, n_seq, n_db, features), out_...  49.5 us
    pallas_call x1, Pallas kernels, exchange_back(): pl.pallas_call(functools.partial(back_kernel, n_seq), out_shape=(jax.Shap...  43.5 us
    all_gather x1, waiting for transfers between devices, on_device(): contexts = lax.all_gather(contexts, 'cc', axis=0, tiled=False)  26.1 us
    pallas_call x1, Pallas kernels, attend(): pl.pallas_call(functools.partial(attend_kernel, 1.0 / math.sqrt(HD), head...  17.7 us
    dot_general x1, matrix products, on_device(): jnp.einsum('cgtr,gcrf->tf', contexts, weight_cols, preferred_element_type...  7.1 us
    pallas_call x1, Pallas kernels, combine(): pl.pallas_call(functools.partial(combine_kernel, heads), grid_spec=grid_s...  6.71 us
    dot_general x1, matrix products, on_device(): jnp.dot(decoder_states, query_weight, preferred_element_type=jnp.float32)  6.5 us
  transfers between devices with their start and end apart: 2, of which 2 were waited for; matrix products, arithmetic and copies ran while one was open for 0% of the time, Pallas kernels for 0%

profile of v11, /device:TPU:1, one launch (start us, length us, event | category | flops | bytes accessed | tf_op | source)
XLA Modules:
  0.0 271.8 jit_solution(6351714334647020404)
XLA Ops:
  6.5 0.9 iota_compare_fusion.1
  7.5 0.1 lt.68
  7.6 0.7 broadcast_multiply_fusion
  8.3 0.8 copy.20
  9.2 0.8 copy.22
  10.2 0.2 convert_reduce_fusion
  10.4 0.6 multiply_add_fusion.place_ref
  11.0 0.7 scatter_custom_fusion.1
  11.7 0.6 pad.4.send_e
  12.3 2.5 copy.25
  14.8 6.5 %convolution_convert_fusion = bf16[1024,256]{1,0:T(8,128)(2,1)} fusion(bf16[1024,4096]{1,0:T(8,128)(2,1)} %param.7, bf16[4096,256]{1,0:T(8,128)(2,1)S(1)} %copy-done), kind=kOutput, calls=%fused_computation.7 | convolution fusion | flops 2147745792 | bytes 11010048 | tf_op jit(solution)/shard_map/dot_general | solution.py:311
  21.3 1.7 gather_fusion
  23.0 1.3 broadcast_in_dim.8
  24.3 4.6 %scatter_fusion = bf16[48,64,256]{2,1,0:T(8,128)(2,1)} fusion(bf16[48,64,256]{2,1,0:T(8,128)(2,1)} %broadcast_in_dim.8, s32[32]{0:T(128)S(1)} %fusion.10, bf16[32,64,256]{2,1,0:T(8,128)(2,1)S(1)} %gather_fusion), kind=kCustom, calls=%fused_computation.1 | custom fusion | bytes 3145856 | tf_op jit(solution)/shard_map/scatter | solution.py:320
  28.9 49.5 %shard_map.73 = (bf16[16,3,64,256]{3,2,1,0:T(8,128)(2,1)}, s32[16,128]{1,0:T(8,128)}, bf16[16,256,256]{2,1,0:T(8,128)(2,1)}) custom-call(bf16[16,3,64,256]{3,2,1,0:T(8,128)(2,1)} %bitcast.33, s32[16,128]{1,0:T(8,128)} %pad.4.send_e, bf16[256,4096]{1,0:T(8,128)(2,1)} %w_loc.1), custom_call_target="tpu_custom_call" | custom-call | tf_op jit(solution)/shard_map/pallas_call | solution.py:262
  78.4 1.3 reshape.155.e_ref
  79.7 17.7 %shard_map.74 = (bf16[3072,256]{1,0:T(8,128)(2,1)}, f32[3072,4]{1,0:T(8,128)}) custom-call(s32[48]{0:T(128)} %reshape.155.e_ref, bf16[3072,256]{1,0:T(8,128)(2,1)} %bitcast.37, bf16[1024,512]{1,0:T(8,128)(2,1)} %bitcast.34), custom_call_target="tpu_custom_call" | custom-call | tf_op jit(solution)/shard_map/pallas_call | solution.py:206
  97.4 3.1 %reshape_reshape.7.stats = f32[16,6,128]{2,1,0:T(8,128)} reshape(f32[3072,4]{1,0:T(8,128)} %get-tuple-element.15) | data formatting | bytes 98304 | tf_op jit(solution)/shard_map/reshape;reshape | solution.py:331
  100.5 43.5 %shard_map.75 = (bf16[16,3,64,256]{3,2,1,0:T(8,128)(2,1)}, f32[16,6,128]{2,1,0:T(8,128)}) custom-call(bf16[16,3,64,256]{3,2,1,0:T(8,128)(2,1)} %bitcast.38, f32[16,6,128]{2,1,0:T(8,128)} %reshape_reshape.7.stats), custom_call_target="tpu_custom_call" | custom-call | tf_op jit(solution)/shard_map/pallas_call | solution.py:281
  144.1 3.6 %reshape.159.stats_ref = f32[48,64,4]{2,1,0:T(8,128)} reshape(f32[16,6,128]{2,1,0:T(8,128)} %get-tuple-element.17) | data formatting | bytes 98304 | tf_op jit(solution)/shard_map/reshape | solution.py:334
  147.7 6.7 %shard_map.76 = bf16[16,64,256]{2,1,0:T(8,128)(2,1)} custom-call(s32[32]{0:T(128)} %multiply_add_fusion.place_ref, s32[16]{0:T(128)} %count_ref.1, bf16[48,64,256]{2,1,0:T(8,128)(2,1)} %bitcast.39, f32[48,64,4]{2,1,0:T(8,128)} %reshape.159.stats_ref), custom_call_target="tpu_custom_call" | custom-call | tf_op jit(solution)/shard_map/pallas_call | solution.py:248
  154.5 77.3 %all-gather.4.cloned.1.call-done = bf16[8,1024,256]{2,1,0:T(8,128)(2,1)} async-done(((bf16[1,1024,256]{2,1,0:T(8,128)(2,1)}), bf16[8,1024,256]{2,1,0:T(8,128)(2,1)}) %all-gather.4.cloned.1.call-update) | async-done | bytes 4194320 | tf_op jit(solution)/shard_map/all_gather | solution.py:339
  231.8 26.1 %all-gather.6.cloned.1.call-done = bf16[16,1024,256]{2,1,0:T(8,128)(2,1)} async-done(((bf16[8,1024,256]{2,1,0:T(8,128)(2,1)}), bf16[16,1024,256]{2,1,0:T(8,128)(2,1)}) %all-gather.6.cloned.1.call-update) | async-done | bytes 8388624 | tf_op jit(solution)/shard_map/all_gather | solution.py:340
  257.9 7.1 %fusion.5 = bf16[1024,256]{1,0:T(8,128)(2,1)} fusion(bf16[2,8,1024,256]{3,2,1,0:T(8,128)(2,1)} %bitcast.42, bf16[8,2,256,256]{3,2,1,0:T(8,128)(2,1)} %bitcast.43), kind=kOutput, calls=%fused_computation.6 | convolution fusion | flops 2147745792 | bytes 11010048 | tf_op jit(solution)/shard_map/cgtr,gcrf->tf/dot_general | solution.py:342
  (15 shorter events, 0.6 us)
Async XLA Ops:
  6.5 8.3 %copy-start = (bf16[4096,256]{1,0:T(8,128)(2,1)S(1)}, bf16[4096,256]{1,0:T(8,128)(2,1)}, u32[]{:S(2)}) copy-start(bf16[4096,256]{1,0:T(8,128)(2,1)} %param.8) | copy-start | bytes 6291460
  6.5 225.2 %all-gather.4.cloned.1.call-start = ((), (), s32[]{:S(2)}) async-start(), calls=%async_computation | async-start | bytes 4718592 | tf_op jit(solution)/shard_map/all_gather | solution.py:339
  154.4 103.4 %all-gather.6.cloned.1.call-start = ((), (), s32[]{:S(2)}) async-start(), calls=%async_computation.1 | async-start | bytes 12582912 | tf_op jit(solution)/shard_map/all_gather | solution.py:340
Sparse Core Ops, SparseCore 0:
  154.5 77.1 all-gather.3
  233.6 24.2 all-gather.5

commit v12 on v10

--- a/solution.py
+++ b/solution.py
@@ -193,23 +193,144 @@
     return ctx.reshape(recv_q.shape), stats.reshape(n_src, cap, span, 2 * heads)
 
 
-def combine_kernel(heads, place_ref, count_ref, ctx_ref, stats_ref, out_ref):
+def attend_back_kernel(n_seq, heads, scale, e_ref, q_ref, kv_ref, back_ctx, back_stats,
+                       stage_ctx, stage_stats, ctx_v, stats_v, cs, cr, ss, sr, ls):
+    me_s = lax.axis_index("seq")
+    me_d = lax.axis_index("db")
+    rows = stage_ctx.shape[1]
+    keys_total = kv_ref.shape[0]
+    width = heads * HD
+    cap = rows // SPAN
+    key_block = lax.broadcasted_iota(jnp.int32, (keys_total, 1), 0) // (2 * SPAN)
+    lane_place = lax.broadcasted_iota(jnp.int32, (1, rows), 1) // SPAN
+
+    barrier = pltpu.get_barrier_semaphore()
+
+    @pl.loop(1, n_seq)
+    def _(o):
+        pl.semaphore_signal(barrier, inc=1, device_id=(lax.rem(me_s + o, n_seq), me_d),
+                            device_id_type=MESH)
+
+    pl.semaphore_wait(barrier, n_seq - 1)
+
+    def compute(d):
+        entry = jnp.zeros((1, rows), jnp.int32)
+        for j in range(cap):
+            entry = jnp.where(lane_place == j, e_ref[d, j], entry)
+        named = key_block == entry
+        start = pl.multiple_of(d * rows, rows)
+        stats_v[...] = jnp.zeros_like(stats_v)
+        for h in range(heads):
+            q = q_ref[pl.ds(start, rows), h * HD:(h + 1) * HD]
+            k = kv_ref[:, h * HD:(h + 1) * HD]
+            v = kv_ref[:, width + h * HD:width + (h + 1) * HD]
+            st = lax.dot_general(
+                k, q, (((1,), (1,)), ((), ())), preferred_element_type=jnp.float32
+            ) * scale
+            st = jnp.where(named, st, -jnp.inf)
+            top = jnp.max(st, axis=0, keepdims=True)
+            w = jnp.exp(st - top)
+            total = jnp.sum(w, axis=0, keepdims=True)
+            u = lax.dot_general(
+                w.astype(jnp.bfloat16), v, (((0,), (0,)), ((), ())),
+                preferred_element_type=jnp.float32,
+            )
+            ctx_v[:, h * HD:(h + 1) * HD] = u.astype(ctx_v.dtype)
+            stats_v[2 * h:2 * h + 1, 0:rows] = top
+            stats_v[2 * h + 1:2 * h + 2, 0:rows] = total
+        staged = [
+            pltpu.make_async_copy(ctx_v, stage_ctx.at[d], ls.at[0]),
+            pltpu.make_async_copy(stats_v, stage_stats.at[d], ls.at[1]),
+        ]
+        for c in staged:
+            c.start()
+        for c in staged:
+            c.wait()
+
+    compute(me_s)
+    own = [
+        pltpu.make_async_copy(stage_ctx.at[me_s], back_ctx.at[me_s], ls.at[2]),
+        pltpu.make_async_copy(stage_stats.at[me_s], back_stats.at[me_s], ls.at[3]),
+    ]
+    for c in own:
+        c.start()
+
+    @pl.loop(1, n_seq)
+    def _(o):
+        d = lax.rem(me_s + o, n_seq)
+        compute(d)
+        peer_copy(stage_stats.at[d], back_stats.at[me_s], ss.at[d], sr.at[me_s], (d, me_d)).start()
+        peer_copy(stage_ctx.at[d], back_ctx.at[me_s], cs.at[d], cr.at[me_s], (d, me_d)).start()
+
+    for c in own:
+        c.wait()
+
+    @pl.loop(1, n_seq)
+    def _(o):
+        d = lax.rem(me_s + o, n_seq)
+        s = lax.rem(me_s + n_seq - o, n_seq)
+        peer_copy(stage_stats.at[d], back_stats.at[me_s], ss.at[d], sr.at[me_s], (d, me_d)).wait_send()
+        peer_copy(stage_ctx.at[d], back_ctx.at[me_s], cs.at[d], cr.at[me_s], (d, me_d)).wait_send()
+        peer_copy(stage_stats.at[me_s], back_stats.at[s], ss.at[s], sr.at[s], (s, me_d)).wait_recv()
+        peer_copy(stage_ctx.at[me_s], back_ctx.at[s], cs.at[s], cr.at[s], (s, me_d)).wait_recv()
+
+
+def attend_back(recv_q, recv_e, kv_flat, heads, n_seq):
+    n_src, cap, span, width = recv_q.shape
+    rows = cap * span
+    q_rows = recv_q.reshape(n_src * rows, width)
+    kv_rows = kv_flat.reshape(-1, kv_flat.shape[2])
+    stats_shape = (n_src, 8, 2 * LANES)
+    ctx_shape = (n_src, rows, width)
+    dma = pltpu.SemaphoreType.DMA
+    outs = pl.pallas_call(
+        functools.partial(attend_back_kernel, n_seq, heads, 1.0 / math.sqrt(HD)),
+        out_shape=(
+            jax.ShapeDtypeStruct(ctx_shape, jnp.bfloat16),
+            jax.ShapeDtypeStruct(stats_shape, jnp.float32),
+            jax.ShapeDtypeStruct(ctx_shape, jnp.bfloat16),
+            jax.ShapeDtypeStruct(stats_shape, jnp.float32),
+        ),
+        in_specs=[
+            pl.BlockSpec(memory_space=pltpu.SMEM),
+            pl.BlockSpec(memory_space=pltpu.VMEM),
+            pl.BlockSpec(memory_space=pltpu.VMEM),
+        ],
+        out_specs=(any_spec(), any_spec(), any_spec(), any_spec()),
+        scratch_shapes=[
+            pltpu.VMEM((rows, width), jnp.bfloat16),
+            pltpu.VMEM(stats_shape[1:], jnp.float32),
+            dma((n_seq,)), dma((n_seq,)), dma((n_seq,)), dma((n_seq,)), dma((4,)),
+        ],
+        compiler_params=pltpu.CompilerParams(collective_id=1, has_side_effects=True),
+    )(recv_e, q_rows, kv_rows)
+    return outs[0], outs[1]
+
+
+def combine_kernel(heads, place_ref, count_ref, ctx_ref, stats_ref, out_ref, stats_t):
+    for s in range(stats_ref.shape[0]):
+        stats_t[s] = jnp.transpose(stats_ref[s])
+
     def one_span(c, carry):
         p0 = place_ref[c * K]
         p1 = place_ref[c * K + 1]
+        r0 = pl.multiple_of(lax.rem(p0, CAP) * SPAN, SPAN)
+        r1 = pl.multiple_of(lax.rem(p1, CAP) * SPAN, SPAN)
+        st0 = stats_t[p0 // CAP, pl.ds(r0, SPAN), :]
+        st1 = stats_t[p1 // CAP, pl.ds(r1, SPAN), :]
         live1 = count_ref[c] > 1
         for h in range(heads):
             cols = slice(h * HD, (h + 1) * HD)
-            m0 = stats_ref[p0, :, 2 * h:2 * h + 1]
-            l0 = stats_ref[p0, :, 2 * h + 1:2 * h + 2]
-            m1 = stats_ref[p1, :, 2 * h:2 * h + 1]
-            l1 = stats_ref[p1, :, 2 * h + 1:2 * h + 2]
+            m0, l0 = st0[:, 2 * h:2 * h + 1], st0[:, 2 * h + 1:2 * h + 2]
+            m1, l1 = st1[:, 2 * h:2 * h + 1], st1[:, 2 * h + 1:2 * h + 2]
             best = jnp.where(live1, jnp.maximum(m0, m1), m0)
-            a0 = jnp.exp(m0 - best) * l0
-            a1 = jnp.where(live1, jnp.exp(m1 - best) * l1, 0.0)
-            v0 = ctx_ref[p0, :, cols].astype(jnp.float32)
-            v1 = jnp.where(live1, ctx_ref[p1, :, cols].astype(jnp.float32), 0.0)
-            out_ref[c, :, cols] = ((a0 * v0 + a1 * v1) / (a0 + a1)).astype(out_ref.dtype)
+            a0 = jnp.exp(m0 - best)
+            a1 = jnp.where(live1, jnp.exp(m1 - best), 0.0)
+            u0 = ctx_ref[p0, :, cols].astype(jnp.float32)
+            u1 = jnp.where(live1, ctx_ref[p1, :, cols].astype(jnp.float32), 0.0)
+            out_ref[c, :, cols] = (
+                (a0 * u0 + a1 * u1) / (a0 * l0 + a1 * l1)
+            ).astype(out_ref.dtype)
         return carry
 
     lax.fori_loop(0, out_ref.shape[0], one_span, 0)
@@ -218,11 +339,13 @@
 def combine(back_ctx, back_stats, place, neighbour_count, heads):
     places, span, width = back_ctx.shape
     spans = neighbour_count.shape[0]
+    n_src, st_rows, st_cols = back_stats.shape
     grid_spec = pltpu.PrefetchScalarGridSpec(
         num_scalar_prefetch=2,
         grid=(1,),
         in_specs=[vmem_whole(back_ctx.shape), vmem_whole(back_stats.shape)],
         out_specs=vmem_whole((spans, span, width)),
+        scratch_shapes=[pltpu.VMEM((n_src, st_cols, st_rows), jnp.float32)],
     )
     return pl.pallas_call(
         functools.partial(combine_kernel, heads),
@@ -303,14 +426,9 @@
     recv_q, recv_e, weight_cols = exchange_out(
         send_q.reshape(n_seq, CAP, SPAN, row_width), send_e, output_weight, n_seq, n_db
     )
-    recv_e = recv_e[:, :CAP].reshape(-1)
     kv_flat = neighbour_kv.reshape(neighbour_kv.shape[0], key_len, 2 * row_width)
-    part, stats = attend(recv_q, recv_e, kv_flat, heads_here)
-    back_ctx, back_stats = exchange_back(
-        part, stats.reshape(n_seq, CAP * SPAN * 2 * heads_here // LANES, LANES), n_seq
-    )
+    back_ctx, back_stats = attend_back(recv_q, recv_e, kv_flat, heads_here, n_seq)
     back_ctx = back_ctx.reshape(places_total, SPAN, row_width)
-    back_stats = back_stats.reshape(places_total, SPAN, 2 * heads_here)
     context = combine(back_ctx, back_stats, place, neighbour_count, heads_here)
     context = context.reshape(tok_rows, row_width)
 

time: 249 us -> 247 us (level)
  Pallas kernels: 117 us -> 126 us
  local copies, waits for them, and re-layouts: 21.7 us -> 13.4 us
    pallas_call x2 -> x1, Pallas kernels: 61 us -> 70.1 us  [attend_back(): pl.pallas_call(functools.partial(attend_back_kernel, n_seq, heads, 1.0 /...]
    reshape x2 -> x0, local copies, waits for them, and re-layouts: 4.91 us -> none  [the longest x1 3.61 us: on_device(): back_stats = back_stats.reshape(places_total, SPAN, 2 * heads_here)]
    another operation x1 -> x0, local copies, waits for them, and re-layouts: 3.15 us -> none  [on_device(): stats.reshape(n_seq, CAP * SPAN * 2 * heads_here // LANES, LANES)]
where the time goes in v12:
time: 247 us
  Pallas kernels  126 us (51%)
  waiting for transfers between devices  77.5 us (31%)
  matrix products  13.6 us (6%)
  local copies, waits for them, and re-layouts  13.4 us (5%)
  between operations  13.4 us (5%)
    all_gather x1, waiting for transfers between devices, on_device(): contexts = lax.all_gather(context, 'db', axis=0, tiled=False)  77.5 us
    pallas_call x1, Pallas kernels, attend_back(): pl.pallas_call(functools.partial(attend_back_kernel, n_seq, heads, 1.0 /...  70.1 us
    pallas_call x1, Pallas kernels, exchange_out(): pl.pallas_call(functools.partial(out_kernel, n_seq, n_db, features), out_...  49.5 us
    dot_general x1, matrix products, on_device(): jnp.einsum('str,srf->tf', contexts, weight_cols, preferred_element_type=j...  7.1 us
    pallas_call x1, Pallas kernels, combine(): pl.pallas_call(functools.partial(combine_kernel, heads), grid_spec=grid_s...  6.67 us
    dot_general x1, matrix products, on_device(): jnp.dot(decoder_states, query_weight, preferred_element_type=jnp.float32)  6.5 us
  transfers between devices with their start and end apart: 1, of which 1 were waited for; matrix products, arithmetic and copies ran while one was open for 0% of the time, Pallas kernels for 0%

profile of v12, /device:TPU:1, one launch (start us, length us, event | category | flops | bytes accessed | tf_op | source)
XLA Modules:
  0.0 246.6 jit_solution(9002432959492708453)
XLA Ops:
  6.5 0.9 iota_compare_fusion.1
  7.4 0.1 lt.72
  7.5 0.1 lt.68
  7.6 0.7 broadcast_multiply_fusion
  8.3 0.8 copy.17
  9.1 0.1 copy.18
  9.2 0.1 mul.24
  9.2 0.8 copy.19
  10.0 0.1 reshape.165
  10.1 0.1 reshape.138
  10.2 0.2 convert_reduce_fusion
  10.4 0.6 multiply_add_fusion.place_ref
  10.9 0.7 scatter_custom_fusion.1
  11.7 0.6 pad.4.send_e
  12.3 2.5 %copy.20 = bf16[128,8,2,256]{3,1,2,0:T(8,128)(2,1)} copy(bf16[128,8,2,256]{3,2,1,0:T(2,128)(2,1)} %bitcast.34) | data formatting | bytes 2097152
  14.8 6.5 %convolution_convert_fusion = bf16[1024,256]{1,0:T(8,128)(2,1)} fusion(bf16[1024,4096]{1,0:T(8,128)(2,1)} %param.7, bf16[4096,256]{1,0:T(8,128)(2,1)S(1)} %copy-done), kind=kOutput, calls=%fused_computation.5 | convolution fusion | flops 2147745792 | bytes 11010048 | tf_op jit(solution)/shard_map/dot_general | solution.py:413
  21.3 1.7 gather_fusion
  22.9 1.3 broadcast_in_dim.8
  24.3 4.6 %scatter_fusion = bf16[48,64,256]{2,1,0:T(8,128)(2,1)} fusion(bf16[48,64,256]{2,1,0:T(8,128)(2,1)} %broadcast_in_dim.8, s32[32]{0:T(128)S(1)} %fusion.3, bf16[32,64,256]{2,1,0:T(8,128)(2,1)S(1)} %gather_fusion), kind=kCustom, calls=%fused_computation.1 | custom fusion | bytes 3145856 | tf_op jit(solution)/shard_map/scatter | solution.py:422
  28.8 49.5 %shard_map.73 = (bf16[16,3,64,256]{3,2,1,0:T(8,128)(2,1)}, s32[16,128]{1,0:T(8,128)}, bf16[16,256,256]{2,1,0:T(8,128)(2,1)}) custom-call(bf16[16,3,64,256]{3,2,1,0:T(8,128)(2,1)} %bitcast.28, s32[16,128]{1,0:T(8,128)} %pad.4.send_e, bf16[256,4096]{1,0:T(8,128)(2,1)} %w_loc.1), custom_call_target="tpu_custom_call" | custom-call | tf_op jit(solution)/shard_map/pallas_call | solution.py:364
  78.3 70.1 %shard_map.74 = (bf16[16,192,256]{2,1,0:T(8,128)(2,1)}, f32[16,8,256]{2,1,0:T(8,128)}, bf16[16,192,256]{2,1,0:T(8,128)(2,1)}, f32[16,8,256]{2,1,0:T(8,128)}) custom-call(s32[16,128]{1,0:T(8,128)} %get-tuple-element.10.e_ref, bf16[3072,256]{1,0:T(8,128)(2,1)} %bitcast.32, bf16[1024,512]{1,0:T(8,128)(2,1)} %bitcast.29), custom_call_target="tpu_custom_call" | custom-call | tf_op jit(solution)/shard_map/pallas_call | solution.py:286
  148.4 6.7 %shard_map.75 = bf16[16,64,256]{2,1,0:T(8,128)(2,1)} custom-call(s32[32]{0:T(128)} %multiply_add_fusion.place_ref, s32[16]{0:T(128)} %count_ref.1, bf16[48,64,256]{2,1,0:T(8,128)(2,1)} %bitcast.33, f32[16,8,256]{2,1,0:T(8,128)} %get-tuple-element.13.stats_ref), custom_call_target="tpu_custom_call" | custom-call | tf_op jit(solution)/shard_map/pallas_call | solution.py:350
  155.1 77.5 %all-gather.2.cloned.1.call-done = bf16[16,1024,256]{2,1,0:T(8,128)(2,1)} async-done(((bf16[1,1024,256]{2,1,0:T(8,128)(2,1)}), bf16[16,1024,256]{2,1,0:T(8,128)(2,1)}) %all-gather.2.cloned.1.call-update) | async-done | bytes 8388624 | tf_op jit(solution)/shard_map/all_gather | solution.py:435
  232.6 7.1 %fusion = bf16[1024,256]{1,0:T(8,128)(2,1)} fusion(bf16[16,1024,256]{2,1,0:T(8,128)(2,1)} %all-gather.2.cloned.1.call-done, bf16[16,256,256]{2,1,0:T(8,128)(2,1)} %get-tuple-element.14), kind=kOutput, calls=%fused_computation.4 | convolution fusion | flops 2147745792 | bytes 11010048 | tf_op jit(solution)/shard_map/str,srf->tf/dot_general | solution.py:436
  (8 shorter events, 0.1 us)
Async XLA Ops:
  6.5 8.2 %copy-start = (bf16[4096,256]{1,0:T(8,128)(2,1)S(1)}, bf16[4096,256]{1,0:T(8,128)(2,1)}, u32[]{:S(2)}) copy-start(bf16[4096,256]{1,0:T(8,128)(2,1)} %param.8) | copy-start | bytes 6291460
  6.5 226.1 %all-gather.2.cloned.1.call-start = ((), (), s32[]{:S(2)}) async-start(), calls=%async_computation | async-start | bytes 8912896 | tf_op jit(solution)/shard_map/all_gather | solution.py:435
Sparse Core Ops, SparseCore 0:
  155.2 77.3 all-gather.1

commit v13 on v12

--- a/solution.py
+++ b/solution.py
@@ -35,14 +35,10 @@
     )
 
 
-def out_kernel(n_seq, n_db, features, send_q, send_e, w_loc, recv_q, recv_e, w_cols,
-               qs, qr, es, er, ws, wr, ls):
+def out_kernel(n_seq, send_q, send_e, recv_q, recv_e, qs, qr, es, er, ls):
     me_s = lax.axis_index("seq")
     me_d = lax.axis_index("db")
 
-    def w_src(d):
-        return w_loc.at[:, pl.ds(pl.multiple_of(d * features, features), features)]
-
     barrier = pltpu.get_barrier_semaphore()
 
     @pl.loop(1, n_seq)
@@ -50,25 +46,14 @@
         pl.semaphore_signal(barrier, inc=1, device_id=(lax.rem(me_s + o, n_seq), me_d),
                             device_id_type=MESH)
 
-    @pl.loop(1, n_db)
-    def _(o):
-        pl.semaphore_signal(barrier, inc=1, device_id=(me_s, lax.rem(me_d + o, n_db)),
-                            device_id_type=MESH)
-
-    pl.semaphore_wait(barrier, (n_seq - 1) + (n_db - 1))
+    pl.semaphore_wait(barrier, n_seq - 1)
 
     own = [
         pltpu.make_async_copy(send_q.at[me_s], recv_q.at[me_s], ls.at[0]),
         pltpu.make_async_copy(send_e.at[me_s], recv_e.at[me_s], ls.at[1]),
-        pltpu.make_async_copy(w_src(me_d), w_cols.at[me_d], ls.at[2]),
     ]
     for c in own:
         c.start()
-
-    @pl.loop(1, n_db)
-    def _(o):
-        d = lax.rem(me_d + o, n_db)
-        peer_copy(w_src(d), w_cols.at[me_d], ws.at[d], wr.at[me_d], (me_s, d)).start()
 
     @pl.loop(1, n_seq)
     def _(o):
@@ -87,13 +72,6 @@
         peer_copy(send_q.at[d], recv_q.at[me_s], qs.at[d], qr.at[me_s], (d, me_d)).wait_send()
         peer_copy(send_e.at[me_s], recv_e.at[s], es.at[s], er.at[s], (s, me_d)).wait_recv()
         peer_copy(send_q.at[me_s], recv_q.at[s], qs.at[s], qr.at[s], (s, me_d)).wait_recv()
-
-    @pl.loop(1, n_db)
-    def _(o):
-        d = lax.rem(me_d + o, n_db)
-        s = lax.rem(me_d + n_db - o, n_db)
-        peer_copy(w_src(d), w_cols.at[me_d], ws.at[d], wr.at[me_d], (me_s, d)).wait_send()
-        peer_copy(w_src(me_d), w_cols.at[s], ws.at[s], wr.at[s], (me_s, s)).wait_recv()
 
 
 def back_kernel(n_seq, ctx, stats, back_ctx, back_stats, cs, cr, ss, sr, ls):
@@ -193,8 +171,9 @@
     return ctx.reshape(recv_q.shape), stats.reshape(n_src, cap, span, 2 * heads)
 
 
-def attend_back_kernel(n_seq, heads, scale, e_ref, q_ref, kv_ref, back_ctx, back_stats,
-                       stage_ctx, stage_stats, ctx_v, stats_v, cs, cr, ss, sr, ls):
+def attend_back_kernel(n_seq, n_db, heads, scale, e_ref, q_ref, kv_ref, w_loc, back_ctx,
+                       back_stats, stage_ctx, stage_stats, w_cols, ctx_v, stats_v, cs, cr,
+                       ss, sr, ws, wr, ls):
     me_s = lax.axis_index("seq")
     me_d = lax.axis_index("db")
     rows = stage_ctx.shape[1]
@@ -211,7 +190,25 @@
         pl.semaphore_signal(barrier, inc=1, device_id=(lax.rem(me_s + o, n_seq), me_d),
                             device_id_type=MESH)
 
-    pl.semaphore_wait(barrier, n_seq - 1)
+    @pl.loop(1, n_db)
+    def _(o):
+        pl.semaphore_signal(barrier, inc=1, device_id=(me_s, lax.rem(me_d + o, n_db)),
+                            device_id_type=MESH)
+
+    pl.semaphore_wait(barrier, (n_seq - 1) + (n_db - 1))
+
+    features = w_cols.shape[2]
+
+    def w_src(d):
+        return w_loc.at[:, pl.ds(pl.multiple_of(d * features, features), features)]
+
+    own_w = pltpu.make_async_copy(w_src(me_d), w_cols.at[me_d], ls.at[4])
+    own_w.start()
+
+    @pl.loop(1, n_db)
+    def _(o):
+        d = lax.rem(me_d + o, n_db)
+        peer_copy(w_src(d), w_cols.at[me_d], ws.at[d], wr.at[me_d], (me_s, d)).start()
 
     def compute(d):
         entry = jnp.zeros((1, rows), jnp.int32)
@@ -274,8 +271,17 @@
         peer_copy(stage_stats.at[me_s], back_stats.at[s], ss.at[s], sr.at[s], (s, me_d)).wait_recv()
         peer_copy(stage_ctx.at[me_s], back_ctx.at[s], cs.at[s], cr.at[s], (s, me_d)).wait_recv()
 
-
-def attend_back(recv_q, recv_e, kv_flat, heads, n_seq):
+    own_w.wait()
+
+    @pl.loop(1, n_db)
+    def _(o):
+        d = lax.rem(me_d + o, n_db)
+        s = lax.rem(me_d + n_db - o, n_db)
+        peer_copy(w_src(d), w_cols.at[me_d], ws.at[d], wr.at[me_d], (me_s, d)).wait_send()
+        peer_copy(w_src(me_d), w_cols.at[s], ws.at[s], wr.at[s], (me_s, s)).wait_recv()
+
+
+def attend_back(recv_q, recv_e, kv_flat, w_loc, heads, n_seq, n_db):
     n_src, cap, span, width = recv_q.shape
     rows = cap * span
     q_rows = recv_q.reshape(n_src * rows, width)
@@ -284,27 +290,30 @@
     ctx_shape = (n_src, rows, width)
     dma = pltpu.SemaphoreType.DMA
     outs = pl.pallas_call(
-        functools.partial(attend_back_kernel, n_seq, heads, 1.0 / math.sqrt(HD)),
+        functools.partial(attend_back_kernel, n_seq, n_db, heads, 1.0 / math.sqrt(HD)),
         out_shape=(
             jax.ShapeDtypeStruct(ctx_shape, jnp.bfloat16),
             jax.ShapeDtypeStruct(stats_shape, jnp.float32),
             jax.ShapeDtypeStruct(ctx_shape, jnp.bfloat16),
             jax.ShapeDtypeStruct(stats_shape, jnp.float32),
+            jax.ShapeDtypeStruct((n_db, w_loc.shape[0], w_loc.shape[1] // n_db), w_loc.dtype),
         ),
         in_specs=[
             pl.BlockSpec(memory_space=pltpu.SMEM),
             pl.BlockSpec(memory_space=pltpu.VMEM),
             pl.BlockSpec(memory_space=pltpu.VMEM),
+            any_spec(),
         ],
-        out_specs=(any_spec(), any_spec(), any_spec(), any_spec()),
+        out_specs=(any_spec(), any_spec(), any_spec(), any_spec(), any_spec()),
         scratch_shapes=[
             pltpu.VMEM((rows, width), jnp.bfloat16),
             pltpu.VMEM(stats_shape[1:], jnp.float32),
-            dma((n_seq,)), dma((n_seq,)), dma((n_seq,)), dma((n_seq,)), dma((4,)),
+            dma((n_seq,)), dma((n_seq,)), dma((n_seq,)), dma((n_seq,)),
+            dma((n_db,)), dma((n_db,)), dma((5,)),
         ],
         compiler_params=pltpu.CompilerParams(collective_id=1, has_side_effects=True),
-    )(recv_e, q_rows, kv_rows)
-    return outs[0], outs[1]
+    )(recv_e, q_rows, kv_rows, w_loc)
+    return outs[0], outs[1], outs[4]
 
 
 def combine_kernel(heads, place_ref, count_ref, ctx_ref, stats_ref, out_ref, stats_t):
@@ -358,24 +367,19 @@
     return pl.BlockSpec(memory_space=pl.ANY)
 
 
-def exchange_out(send_q, send_e, w_loc, n_seq, n_db):
-    features = w_loc.shape[1] // n_db
+def exchange_out(send_q, send_e, n_seq):
     dma = pltpu.SemaphoreType.DMA
     return pl.pallas_call(
-        functools.partial(out_kernel, n_seq, n_db, features),
+        functools.partial(out_kernel, n_seq),
         out_shape=(
             jax.ShapeDtypeStruct(send_q.shape, send_q.dtype),
             jax.ShapeDtypeStruct(send_e.shape, send_e.dtype),
-            jax.ShapeDtypeStruct((n_db, w_loc.shape[0], features), w_loc.dtype),
         ),
-        in_specs=[any_spec()] * 3,
-        out_specs=(any_spec(), any_spec(), any_spec()),
-        scratch_shapes=[
-            dma((n_seq,)), dma((n_seq,)), dma((n_seq,)), dma((n_seq,)),
-            dma((n_db,)), dma((n_db,)), dma((3,)),
-        ],
+        in_specs=[any_spec()] * 2,
+        out_specs=(any_spec(), any_spec()),
+        scratch_shapes=[dma((n_seq,)), dma((n_seq,)), dma((n_seq,)), dma((n_seq,)), dma((2,))],
         compiler_params=pltpu.CompilerParams(collective_id=0, has_side_effects=True),
-    )(send_q, send_e, w_loc)
+    )(send_q, send_e)
 
 
 def exchange_back(ctx, stats, n_seq):
@@ -423,11 +427,11 @@
     send_e = jnp.zeros((places_total,), jnp.int32)
     send_e = send_e.at[target].set(neighbour_entry.reshape(-1), mode="drop")
     send_e = jnp.pad(send_e.reshape(n_seq, CAP), ((0, 0), (0, LANES - CAP)))
-    recv_q, recv_e, weight_cols = exchange_out(
-        send_q.reshape(n_seq, CAP, SPAN, row_width), send_e, output_weight, n_seq, n_db
-    )
+    recv_q, recv_e = exchange_out(send_q.reshape(n_seq, CAP, SPAN, row_width), send_e, n_seq)
     kv_flat = neighbour_kv.reshape(neighbour_kv.shape[0], key_len, 2 * row_width)
-    back_ctx, back_stats = attend_back(recv_q, recv_e, kv_flat, heads_here, n_seq)
+    back_ctx, back_stats, weight_cols = attend_back(
+        recv_q, recv_e, kv_flat, output_weight, heads_here, n_seq, n_db
+    )
     back_ctx = back_ctx.reshape(places_total, SPAN, row_width)
     context = combine(back_ctx, back_stats, place, neighbour_count, heads_here)
     context = context.reshape(tok_rows, row_width)

time: 247 us -> 239 us (0.968)
  Pallas kernels: 126 us -> 119 us
    pallas_call x2, Pallas kernels: 120 us -> 112 us  [the longest x1 68.9 us: attend_back(): pl.pallas_call(functools.partial(attend_back_kernel, n_seq, n_db, heads,...]
where the time goes in v13:
time: 239 us
  Pallas kernels  119 us (50%)
  waiting for transfers between devices  77.1 us (32%)
  matrix products  13.6 us (6%)
  local copies, waits for them, and re-layouts  13.4 us (6%)
  between operations  13.4 us (6%)
    all_gather x1, waiting for transfers between devices, on_device(): contexts = lax.all_gather(context, 'db', axis=0, tiled=False)  77 us
    pallas_call x1, Pallas kernels, attend_back(): pl.pallas_call(functools.partial(attend_back_kernel, n_seq, n_db, heads,...  68.9 us
    pallas_call x1, Pallas kernels, exchange_out(): pl.pallas_call(functools.partial(out_kernel, n_seq), out_shape=(jax.Shape...  43.5 us
    dot_general x1, matrix products, on_device(): jnp.einsum('str,srf->tf', contexts, weight_cols, preferred_element_type=j...  7.1 us
    pallas_call x1, Pallas kernels, combine(): pl.pallas_call(functools.partial(combine_kernel, heads), grid_spec=grid_s...  6.67 us
    dot_general x1, matrix products, on_device(): jnp.dot(decoder_states, query_weight, preferred_element_type=jnp.float32)  6.5 us
  transfers between devices with their start and end apart: 1, of which 1 were waited for; matrix products, arithmetic and copies ran while one was open for 0% of the time, Pallas kernels for 0%

profile of v13, /device:TPU:1, one launch (start us, length us, event | category | flops | bytes accessed | tf_op | source)
XLA Modules:
  0.0 238.9 jit_solution(7050291026294006136)
XLA Ops:
  6.5 0.9 iota_compare_fusion.1
  7.4 0.1 lt.72
  7.5 0.1 lt.68
  7.6 0.7 broadcast_multiply_fusion
  8.3 0.8 copy.17
  9.1 0.1 copy.18
  9.2 0.1 mul.24
  9.2 0.8 copy.19
  10.0 0.1 reshape.165
  10.1 0.1 reshape.138
  10.2 0.2 convert_reduce_fusion
  10.4 0.6 multiply_add_fusion.place_ref
  10.9 0.7 scatter_custom_fusion.1
  11.7 0.6 pad.4.send_e
  12.3 2.5 %copy.20 = bf16[128,8,2,256]{3,1,2,0:T(8,128)(2,1)} copy(bf16[128,8,2,256]{3,2,1,0:T(2,128)(2,1)} %bitcast.34) | data formatting | bytes 2097152
  14.8 6.5 %convolution_convert_fusion = bf16[1024,256]{1,0:T(8,128)(2,1)} fusion(bf16[1024,4096]{1,0:T(8,128)(2,1)} %param.7, bf16[4096,256]{1,0:T(8,128)(2,1)S(1)} %copy-done), kind=kOutput, calls=%fused_computation.5 | convolution fusion | flops 2147745792 | bytes 11010048 | tf_op jit(solution)/shard_map/dot_general | solution.py:417
  21.3 1.7 gather_fusion
  22.9 1.3 broadcast_in_dim.8
  24.3 4.6 %scatter_fusion = bf16[48,64,256]{2,1,0:T(8,128)(2,1)} fusion(bf16[48,64,256]{2,1,0:T(8,128)(2,1)} %broadcast_in_dim.8, s32[32]{0:T(128)S(1)} %fusion.3, bf16[32,64,256]{2,1,0:T(8,128)(2,1)S(1)} %gather_fusion), kind=kCustom, calls=%fused_computation.1 | custom fusion | bytes 3145856 | tf_op jit(solution)/shard_map/scatter | solution.py:426
  28.8 43.5 %shard_map.73 = (bf16[16,3,64,256]{3,2,1,0:T(8,128)(2,1)}, s32[16,128]{1,0:T(8,128)}) custom-call(bf16[16,3,64,256]{3,2,1,0:T(8,128)(2,1)} %bitcast.28, s32[16,128]{1,0:T(8,128)} %pad.4.send_e), custom_call_target="tpu_custom_call" | custom-call | tf_op jit(solution)/shard_map/pallas_call | solution.py:372
  72.3 68.9 %shard_map.74 = (bf16[16,192,256]{2,1,0:T(8,128)(2,1)}, f32[16,8,256]{2,1,0:T(8,128)}, bf16[16,192,256]{2,1,0:T(8,128)(2,1)}, f32[16,8,256]{2,1,0:T(8,128)}, bf16[16,256,256]{2,1,0:T(8,128)(2,1)}) custom-call(s32[16,128]{1,0:T(8,128)} %get-tuple-element.10.e_ref, bf16[3072,256]{1,0:T(8,128)(2,1)} %bitcast.32, bf16[1024,512]{1,0:T(8,128)(2,1)} %bitcast.29, ...), custom_call_target="tpu_custom_call" | custom-call | tf_op jit(solution)/shard_map/pallas_call | solution.py:292
  141.2 6.7 %shard_map.75 = bf16[16,64,256]{2,1,0:T(8,128)(2,1)} custom-call(s32[32]{0:T(128)} %multiply_add_fusion.place_ref, s32[16]{0:T(128)} %count_ref.1, bf16[48,64,256]{2,1,0:T(8,128)(2,1)} %bitcast.33, f32[16,8,256]{2,1,0:T(8,128)} %get-tuple-element.13.stats_ref), custom_call_target="tpu_custom_call" | custom-call | tf_op jit(solution)/shard_map/pallas_call | solution.py:359
  147.9 77.0 %all-gather.2.cloned.1.call-done = bf16[16,1024,256]{2,1,0:T(8,128)(2,1)} async-done(((bf16[1,1024,256]{2,1,0:T(8,128)(2,1)}), bf16[16,1024,256]{2,1,0:T(8,128)(2,1)}) %all-gather.2.cloned.1.call-update) | async-done | bytes 8388624 | tf_op jit(solution)/shard_map/all_gather | solution.py:439
  224.9 7.1 %fusion = bf16[1024,256]{1,0:T(8,128)(2,1)} fusion(bf16[16,1024,256]{2,1,0:T(8,128)(2,1)} %all-gather.2.cloned.1.call-done, bf16[16,256,256]{2,1,0:T(8,128)(2,1)} %get-tuple-element.14), kind=kOutput, calls=%fused_computation.4 | convolution fusion | flops 2147745792 | bytes 11010048 | tf_op jit(solution)/shard_map/str,srf->tf/dot_general | solution.py:440
  (8 shorter events, 0.1 us)
Async XLA Ops:
  6.5 8.2 %copy-start = (bf16[4096,256]{1,0:T(8,128)(2,1)S(1)}, bf16[4096,256]{1,0:T(8,128)(2,1)}, u32[]{:S(2)}) copy-start(bf16[4096,256]{1,0:T(8,128)(2,1)} %param.8) | copy-start | bytes 6291460
  6.5 218.4 %all-gather.2.cloned.1.call-start = ((), (), s32[]{:S(2)}) async-start(), calls=%async_computation | async-start | bytes 8912896 | tf_op jit(solution)/shard_map/all_gather | solution.py:439
Sparse Core Ops, SparseCore 0:
  148.0 76.8 all-gather.1

commit v14 on v13

--- a/solution.py
+++ b/solution.py
@@ -363,6 +363,30 @@
     )(place, neighbour_count, back_ctx, back_stats)
 
 
+def pack_kernel(src_ref, q_ref, out_ref):
+    def one_place(p, carry):
+        span = src_ref[p]
+        rows = q_ref[jnp.maximum(span, 0)]
+        out_ref[p] = jnp.where(span >= 0, rows, jnp.zeros_like(rows))
+        return carry
+
+    lax.fori_loop(0, out_ref.shape[0], one_place, 0)
+
+
+def pack(queries, src_span, places):
+    grid_spec = pltpu.PrefetchScalarGridSpec(
+        num_scalar_prefetch=1,
+        grid=(1,),
+        in_specs=[vmem_whole(queries.shape)],
+        out_specs=vmem_whole((places,) + queries.shape[1:]),
+    )
+    return pl.pallas_call(
+        pack_kernel,
+        grid_spec=grid_spec,
+        out_shape=jax.ShapeDtypeStruct((places,) + queries.shape[1:], queries.dtype),
+    )(src_span, queries)
+
+
 def any_spec():
     return pl.BlockSpec(memory_space=pl.ANY)
 
@@ -422,8 +446,9 @@
     live, place = slot_places(neighbour_shard, neighbour_count)
     target = jnp.where(live, place, places_total)
     span_of_slot = jnp.arange(span_total * K, dtype=jnp.int32) // K
-    send_q = jnp.zeros((places_total, SPAN, row_width), jnp.bfloat16)
-    send_q = send_q.at[target].set(queries[span_of_slot], mode="drop")
+    src_span = jnp.full((places_total,), -1, jnp.int32)
+    src_span = src_span.at[target].set(span_of_slot, mode="drop")
+    send_q = pack(queries, src_span, places_total)
     send_e = jnp.zeros((places_total,), jnp.int32)
     send_e = send_e.at[target].set(neighbour_entry.reshape(-1), mode="drop")
     send_e = jnp.pad(send_e.reshape(n_seq, CAP), ((0, 0), (0, LANES - CAP)))

time: 239 us -> 236 us (0.987)
  local copies, waits for them, and re-layouts: 13.4 us -> 7.05 us
  Pallas kernels: 119 us -> 122 us
    scatter x1, local copies, waits for them, and re-layouts: 4.58 us -> 1.17 us  [on_device(): src_span = src_span.at[target].set(span_of_slot, mode='drop')]
    pallas_call x0 -> x1, Pallas kernels: none -> 3.33 us  [pack(): pl.pallas_call(pack_kernel, grid_spec=grid_spec, out_shape=jax.ShapeDtype...]
where the time goes in v14:
time: 236 us
  Pallas kernels  122 us (52%)
  waiting for transfers between devices  77 us (33%)
  matrix products  13.6 us (6%)
  between operations  13.4 us (6%)
  local copies, waits for them, and re-layouts  7.05 us (3%)
    all_gather x1, waiting for transfers between devices, on_device(): contexts = lax.all_gather(context, 'db', axis=0, tiled=False)  77 us
    pallas_call x1, Pallas kernels, attend_back(): pl.pallas_call(functools.partial(attend_back_kernel, n_seq, n_db, heads,...  69 us
    pallas_call x1, Pallas kernels, exchange_out(): pl.pallas_call(functools.partial(out_kernel, n_seq), out_shape=(jax.Shape...  43.5 us
    dot_general x1, matrix products, on_device(): jnp.einsum('str,srf->tf', contexts, weight_cols, preferred_element_type=j...  7.1 us
    pallas_call x1, Pallas kernels, combine(): pl.pallas_call(functools.partial(combine_kernel, heads), grid_spec=grid_s...  6.67 us
    dot_general x1, matrix products, on_device(): jnp.dot(decoder_states, query_weight, preferred_element_type=jnp.float32)  6.5 us
  transfers between devices with their start and end apart: 1, of which 1 were waited for; matrix products, arithmetic and copies ran while one was open for 0% of the time, Pallas kernels for 0%

profile of v14, /device:TPU:1, one launch (start us, length us, event | category | flops | bytes accessed | tf_op | source)
XLA Modules:
  0.0 235.9 jit_solution(17119195217777108575)
XLA Ops:
  6.5 0.9 iota_compare_fusion.1
  7.4 0.1 lt.62
  7.5 0.1 lt.58
  7.6 0.7 broadcast_multiply_fusion
  8.3 0.8 copy.17
  9.1 0.1 copy.18
  9.1 0.1 mul.24
  9.2 0.8 copy.19
  10.0 0.1 reshape.114
  10.1 0.1 reshape.95
  10.2 0.2 convert_reduce_fusion
  10.4 0.6 multiply_add_fusion.place_ref
  10.9 0.7 scatter_custom_fusion.1
  11.6 0.1 reshape.99
  11.7 0.6 pad.4.send_e
  12.3 2.5 %copy.20 = bf16[128,8,2,256]{3,1,2,0:T(8,128)(2,1)} copy(bf16[128,8,2,256]{3,2,1,0:T(2,128)(2,1)} %bitcast.31) | data formatting | bytes 2097152
  14.7 1.2 scatter_custom_fusion.src_ref
  15.9 6.5 %convolution_convert_fusion = bf16[1024,256]{1,0:T(8,128)(2,1)} fusion(bf16[1024,4096]{1,0:T(8,128)(2,1)} %param.7, bf16[4096,256]{1,0:T(8,128)(2,1)S(1)} %copy-done), kind=kOutput, calls=%fused_computation.4 | convolution fusion | flops 2147745792 | bytes 11010048 | tf_op jit(solution)/shard_map/dot_general | solution.py:441
  22.4 3.3 %shard_map.73 = bf16[48,64,256]{2,1,0:T(8,128)(2,1)} custom-call(s32[48]{0:T(128)} %scatter_custom_fusion.src_ref, bf16[16,64,256]{2,1,0:T(8,128)(2,1)} %bitcast.32), custom_call_target="tpu_custom_call" | custom-call | tf_op jit(solution)/shard_map/pallas_call | solution.py:383
  25.8 43.5 %shard_map.74 = (bf16[16,3,64,256]{3,2,1,0:T(8,128)(2,1)}, s32[16,128]{1,0:T(8,128)}) custom-call(bf16[16,3,64,256]{3,2,1,0:T(8,128)(2,1)} %bitcast.26, s32[16,128]{1,0:T(8,128)} %pad.4.send_e), custom_call_target="tpu_custom_call" | custom-call | tf_op jit(solution)/shard_map/pallas_call | solution.py:396
  69.2 69.0 %shard_map.75 = (bf16[16,192,256]{2,1,0:T(8,128)(2,1)}, f32[16,8,256]{2,1,0:T(8,128)}, bf16[16,192,256]{2,1,0:T(8,128)(2,1)}, f32[16,8,256]{2,1,0:T(8,128)}, bf16[16,256,256]{2,1,0:T(8,128)(2,1)}) custom-call(s32[16,128]{1,0:T(8,128)} %get-tuple-element.10.e_ref, bf16[3072,256]{1,0:T(8,128)(2,1)} %bitcast.29, bf16[1024,512]{1,0:T(8,128)(2,1)} %bitcast.27, ...), custom_call_target="tpu_custom_call" | custom-call | tf_op jit(solution)/shard_map/pallas_call | solution.py:292
  138.3 6.7 %shard_map.76 = bf16[16,64,256]{2,1,0:T(8,128)(2,1)} custom-call(s32[32]{0:T(128)} %multiply_add_fusion.place_ref, s32[16]{0:T(128)} %count_ref.1, bf16[48,64,256]{2,1,0:T(8,128)(2,1)} %bitcast.30, f32[16,8,256]{2,1,0:T(8,128)} %get-tuple-element.13.stats_ref), custom_call_target="tpu_custom_call" | custom-call | tf_op jit(solution)/shard_map/pallas_call | solution.py:359
  144.9 77.0 %all-gather.2.cloned.1.call-done = bf16[16,1024,256]{2,1,0:T(8,128)(2,1)} async-done(((bf16[1,1024,256]{2,1,0:T(8,128)(2,1)}), bf16[16,1024,256]{2,1,0:T(8,128)(2,1)}) %all-gather.2.cloned.1.call-update) | async-done | bytes 8388624 | tf_op jit(solution)/shard_map/all_gather | solution.py:464
  221.9 7.1 %fusion = bf16[1024,256]{1,0:T(8,128)(2,1)} fusion(bf16[16,1024,256]{2,1,0:T(8,128)(2,1)} %all-gather.2.cloned.1.call-done, bf16[16,256,256]{2,1,0:T(8,128)(2,1)} %get-tuple-element.14), kind=kOutput, calls=%fused_computation.3 | convolution fusion | flops 2147745792 | bytes 11010048 | tf_op jit(solution)/shard_map/str,srf->tf/dot_general | solution.py:465
  (6 shorter events, 0.0 us)
Async XLA Ops:
  6.5 9.4 %copy-start = (bf16[4096,256]{1,0:T(8,128)(2,1)S(1)}, bf16[4096,256]{1,0:T(8,128)(2,1)}, u32[]{:S(2)}) copy-start(bf16[4096,256]{1,0:T(8,128)(2,1)} %param.8) | copy-start | bytes 6291460
  6.5 215.4 %all-gather.2.cloned.1.call-start = ((), (), s32[]{:S(2)}) async-start(), calls=%async_computation | async-start | bytes 8912896 | tf_op jit(solution)/shard_map/all_gather | solution.py:464
Sparse Core Ops, SparseCore 0:
  145.1 76.8 all-gather.1

commit v15 on v14

--- a/solution.py
+++ b/solution.py
@@ -173,7 +173,7 @@
 
 def attend_back_kernel(n_seq, n_db, heads, scale, e_ref, q_ref, kv_ref, w_loc, back_ctx,
                        back_stats, stage_ctx, stage_stats, w_cols, ctx_v, stats_v, cs, cr,
-                       ss, sr, ws, wr, ls):
+                       ss, sr, ws, wr, ls, stg):
     me_s = lax.axis_index("seq")
     me_d = lax.axis_index("db")
     rows = stage_ctx.shape[1]
@@ -210,13 +210,13 @@
         d = lax.rem(me_d + o, n_db)
         peer_copy(w_src(d), w_cols.at[me_d], ws.at[d], wr.at[me_d], (me_s, d)).start()
 
-    def compute(d):
+    def compute(d, slot):
         entry = jnp.zeros((1, rows), jnp.int32)
         for j in range(cap):
             entry = jnp.where(lane_place == j, e_ref[d, j], entry)
         named = key_block == entry
         start = pl.multiple_of(d * rows, rows)
-        stats_v[...] = jnp.zeros_like(stats_v)
+        stats_v[slot] = jnp.zeros(stats_v.shape[1:], stats_v.dtype)
         for h in range(heads):
             q = q_ref[pl.ds(start, rows), h * HD:(h + 1) * HD]
             k = kv_ref[:, h * HD:(h + 1) * HD]
@@ -232,19 +232,25 @@
                 w.astype(jnp.bfloat16), v, (((0,), (0,)), ((), ())),
                 preferred_element_type=jnp.float32,
             )
-            ctx_v[:, h * HD:(h + 1) * HD] = u.astype(ctx_v.dtype)
-            stats_v[2 * h:2 * h + 1, 0:rows] = top
-            stats_v[2 * h + 1:2 * h + 2, 0:rows] = total
-        staged = [
-            pltpu.make_async_copy(ctx_v, stage_ctx.at[d], ls.at[0]),
-            pltpu.make_async_copy(stats_v, stage_stats.at[d], ls.at[1]),
+            ctx_v[slot, :, h * HD:(h + 1) * HD] = u.astype(ctx_v.dtype)
+            stats_v[slot, 2 * h:2 * h + 1, 0:rows] = top
+            stats_v[slot, 2 * h + 1:2 * h + 2, 0:rows] = total
+
+    def staged(d, slot):
+        return [
+            pltpu.make_async_copy(ctx_v.at[slot], stage_ctx.at[d], stg.at[0, slot]),
+            pltpu.make_async_copy(stats_v.at[slot], stage_stats.at[d], stg.at[1, slot]),
         ]
-        for c in staged:
-            c.start()
-        for c in staged:
-            c.wait()
-
-    compute(me_s)
+
+    def send(d):
+        peer_copy(stage_stats.at[d], back_stats.at[me_s], ss.at[d], sr.at[me_s], (d, me_d)).start()
+        peer_copy(stage_ctx.at[d], back_ctx.at[me_s], cs.at[d], cr.at[me_s], (d, me_d)).start()
+
+    compute(me_s, 0)
+    for c in staged(me_s, 0):
+        c.start()
+    for c in staged(me_s, 0):
+        c.wait()
     own = [
         pltpu.make_async_copy(stage_ctx.at[me_s], back_ctx.at[me_s], ls.at[2]),
         pltpu.make_async_copy(stage_stats.at[me_s], back_stats.at[me_s], ls.at[3]),
@@ -255,9 +261,22 @@
     @pl.loop(1, n_seq)
     def _(o):
         d = lax.rem(me_s + o, n_seq)
-        compute(d)
-        peer_copy(stage_stats.at[d], back_stats.at[me_s], ss.at[d], sr.at[me_s], (d, me_d)).start()
-        peer_copy(stage_ctx.at[d], back_ctx.at[me_s], cs.at[d], cr.at[me_s], (d, me_d)).start()
+        slot = lax.rem(o, 2)
+        compute(d, slot)
+        for c in staged(d, slot):
+            c.start()
+
+        @pl.when(o > 1)
+        def _():
+            prev = lax.rem(me_s + o - 1, n_seq)
+            for c in staged(prev, 1 - slot):
+                c.wait()
+            send(prev)
+
+    last = lax.rem(me_s + n_seq - 1, n_seq)
+    for c in staged(last, (n_seq - 1) % 2):
+        c.wait()
+    send(last)
 
     for c in own:
         c.wait()
@@ -306,10 +325,10 @@
         ],
         out_specs=(any_spec(), any_spec(), any_spec(), any_spec(), any_spec()),
         scratch_shapes=[
-            pltpu.VMEM((rows, width), jnp.bfloat16),
-            pltpu.VMEM(stats_shape[1:], jnp.float32),
+            pltpu.VMEM((2, rows, width), jnp.bfloat16),
+            pltpu.VMEM((2,) + stats_shape[1:], jnp.float32),
             dma((n_seq,)), dma((n_seq,)), dma((n_seq,)), dma((n_seq,)),
-            dma((n_db,)), dma((n_db,)), dma((5,)),
+            dma((n_db,)), dma((n_db,)), dma((5,)), dma((2, 2)),
         ],
         compiler_params=pltpu.CompilerParams(collective_id=1, has_side_effects=True),
     )(recv_e, q_rows, kv_rows, w_loc)

time: 236 us -> 233 us (0.987)
  Pallas kernels: 122 us -> 119 us
    pallas_call x1, Pallas kernels: 69 us -> 65.9 us  [attend_back(): pl.pallas_call(functools.partial(attend_back_kernel, n_seq, n_db, heads,...]
where the time goes in v15:
time: 233 us
  Pallas kernels  119 us (51%)
  waiting for transfers between devices  77 us (33%)
  matrix products  13.6 us (6%)
  between operations  13.4 us (6%)
  local copies, waits for them, and re-layouts  7.05 us (3%)
    all_gather x1, waiting for transfers between devices, on_device(): contexts = lax.all_gather(context, 'db', axis=0, tiled=False)  77 us
    pallas_call x1, Pallas kernels, attend_back(): pl.pallas_call(functools.partial(attend_back_kernel, n_seq, n_db, heads,...  65.9 us
    pallas_call x1, Pallas kernels, exchange_out(): pl.pallas_call(functools.partial(out_kernel, n_seq), out_shape=(jax.Shape...  43.5 us
    dot_general x1, matrix products, on_device(): jnp.einsum('str,srf->tf', contexts, weight_cols, preferred_element_type=j...  7.1 us
    pallas_call x1, Pallas kernels, combine(): pl.pallas_call(functools.partial(combine_kernel, heads), grid_spec=grid_s...  6.67 us
    dot_general x1, matrix products, on_device(): jnp.dot(decoder_states, query_weight, preferred_element_type=jnp.float32)  6.5 us
  transfers between devices with their start and end apart: 1, of which 1 were waited for; matrix products, arithmetic and copies ran while one was open for 0% of the time, Pallas kernels for 0%

profile of v15, /device:TPU:1, one launch (start us, length us, event | category | flops | bytes accessed | tf_op | source)
XLA Modules:
  0.0 232.8 jit_solution(5160833582315672574)
XLA Ops:
  6.5 0.9 iota_compare_fusion.1
  7.4 0.1 lt.62
  7.5 0.1 lt.58
  7.6 0.7 broadcast_multiply_fusion
  8.3 0.8 copy.17
  9.1 0.1 copy.18
  9.1 0.1 mul.24
  9.2 0.8 copy.19
  10.0 0.1 reshape.114
  10.1 0.1 reshape.95
  10.2 0.2 convert_reduce_fusion
  10.4 0.6 multiply_add_fusion.place_ref
  10.9 0.7 scatter_custom_fusion.1
  11.6 0.1 reshape.99
  11.7 0.6 pad.4.send_e
  12.3 2.5 %copy.20 = bf16[128,8,2,256]{3,1,2,0:T(8,128)(2,1)} copy(bf16[128,8,2,256]{3,2,1,0:T(2,128)(2,1)} %bitcast.31) | data formatting | bytes 2097152
  14.7 1.2 scatter_custom_fusion.src_ref
  15.9 6.5 %convolution_convert_fusion = bf16[1024,256]{1,0:T(8,128)(2,1)} fusion(bf16[1024,4096]{1,0:T(8,128)(2,1)} %param.7, bf16[4096,256]{1,0:T(8,128)(2,1)S(1)} %copy-done), kind=kOutput, calls=%fused_computation.4 | convolution fusion | flops 2147745792 | bytes 11010048 | tf_op jit(solution)/shard_map/dot_general | solution.py:460
  22.4 3.3 %shard_map.73 = bf16[48,64,256]{2,1,0:T(8,128)(2,1)} custom-call(s32[48]{0:T(128)} %scatter_custom_fusion.src_ref, bf16[16,64,256]{2,1,0:T(8,128)(2,1)} %bitcast.32), custom_call_target="tpu_custom_call" | custom-call | tf_op jit(solution)/shard_map/pallas_call | solution.py:402
  25.8 43.5 %shard_map.74 = (bf16[16,3,64,256]{3,2,1,0:T(8,128)(2,1)}, s32[16,128]{1,0:T(8,128)}) custom-call(bf16[16,3,64,256]{3,2,1,0:T(8,128)(2,1)} %bitcast.26, s32[16,128]{1,0:T(8,128)} %pad.4.send_e), custom_call_target="tpu_custom_call" | custom-call | tf_op jit(solution)/shard_map/pallas_call | solution.py:415
  69.2 65.9 %shard_map.75 = (bf16[16,192,256]{2,1,0:T(8,128)(2,1)}, f32[16,8,256]{2,1,0:T(8,128)}, bf16[16,192,256]{2,1,0:T(8,128)(2,1)}, f32[16,8,256]{2,1,0:T(8,128)}, bf16[16,256,256]{2,1,0:T(8,128)(2,1)}) custom-call(s32[16,128]{1,0:T(8,128)} %get-tuple-element.10.e_ref, bf16[3072,256]{1,0:T(8,128)(2,1)} %bitcast.29, bf16[1024,512]{1,0:T(8,128)(2,1)} %bitcast.27, ...), custom_call_target="tpu_custom_call" | custom-call | tf_op jit(solution)/shard_map/pallas_call | solution.py:311
  135.2 6.7 %shard_map.76 = bf16[16,64,256]{2,1,0:T(8,128)(2,1)} custom-call(s32[32]{0:T(128)} %multiply_add_fusion.place_ref, s32[16]{0:T(128)} %count_ref.1, bf16[48,64,256]{2,1,0:T(8,128)(2,1)} %bitcast.30, f32[16,8,256]{2,1,0:T(8,128)} %get-tuple-element.13.stats_ref), custom_call_target="tpu_custom_call" | custom-call | tf_op jit(solution)/shard_map/pallas_call | solution.py:378
  141.9 77.0 %all-gather.2.cloned.1.call-done = bf16[16,1024,256]{2,1,0:T(8,128)(2,1)} async-done(((bf16[1,1024,256]{2,1,0:T(8,128)(2,1)}), bf16[16,1024,256]{2,1,0:T(8,128)(2,1)}) %all-gather.2.cloned.1.call-update) | async-done | bytes 8388624 | tf_op jit(solution)/shard_map/all_gather | solution.py:483
  218.9 7.1 %fusion = bf16[1024,256]{1,0:T(8,128)(2,1)} fusion(bf16[16,1024,256]{2,1,0:T(8,128)(2,1)} %all-gather.2.cloned.1.call-done, bf16[16,256,256]{2,1,0:T(8,128)(2,1)} %get-tuple-element.14), kind=kOutput, calls=%fused_computation.3 | convolution fusion | flops 2147745792 | bytes 11010048 | tf_op jit(solution)/shard_map/str,srf->tf/dot_general | solution.py:484
  (6 shorter events, 0.0 us)
Async XLA Ops:
  6.5 9.4 %copy-start = (bf16[4096,256]{1,0:T(8,128)(2,1)S(1)}, bf16[4096,256]{1,0:T(8,128)(2,1)}, u32[]{:S(2)}) copy-start(bf16[4096,256]{1,0:T(8,128)(2,1)} %param.8) | copy-start | bytes 6291460
  6.5 212.3 %all-gather.2.cloned.1.call-start = ((), (), s32[]{:S(2)}) async-start(), calls=%async_computation | async-start | bytes 8912896 | tf_op jit(solution)/shard_map/all_gather | solution.py:483
Sparse Core Ops, SparseCore 0:
  142.0 76.8 all-gather.1

commit v16 on v15

--- a/solution.py
+++ b/solution.py
@@ -171,9 +171,9 @@
     return ctx.reshape(recv_q.shape), stats.reshape(n_src, cap, span, 2 * heads)
 
 
-def attend_back_kernel(n_seq, n_db, heads, scale, e_ref, q_ref, kv_ref, w_loc, back_ctx,
-                       back_stats, stage_ctx, stage_stats, w_cols, ctx_v, stats_v, cs, cr,
-                       ss, sr, ws, wr, ls, stg):
+def attend_back_kernel(n_seq, n_db, heads, scale, send_e, send_q, kv_ref, w_loc, back_ctx,
+                       back_stats, stage_ctx, stage_stats, w_cols, ctx_v, stats_v, recv_q,
+                       recv_e, cs, cr, ss, sr, ws, wr, ls, stg, qs, qr, es, er):
     me_s = lax.axis_index("seq")
     me_d = lax.axis_index("db")
     rows = stage_ctx.shape[1]
@@ -205,20 +205,36 @@
     own_w = pltpu.make_async_copy(w_src(me_d), w_cols.at[me_d], ls.at[4])
     own_w.start()
 
+    own_in = [
+        pltpu.make_async_copy(send_q.at[me_s], recv_q.at[me_s], ls.at[0]),
+        pltpu.make_async_copy(send_e.at[me_s], recv_e.at[me_s], ls.at[1]),
+    ]
+    for c in own_in:
+        c.start()
+
+    def q_in(d, s):
+        return peer_copy(send_q.at[d], recv_q.at[s], qs.at[d], qr.at[s], (d, me_d))
+
+    def e_in(d, s):
+        return peer_copy(send_e.at[d], recv_e.at[s], es.at[d], er.at[s], (d, me_d))
+
+    @pl.loop(1, n_seq)
+    def _(o):
+        d = lax.rem(me_s + o, n_seq)
+        e_in(d, me_s).start()
+        q_in(d, me_s).start()
+
     @pl.loop(1, n_db)
     def _(o):
         d = lax.rem(me_d + o, n_db)
         peer_copy(w_src(d), w_cols.at[me_d], ws.at[d], wr.at[me_d], (me_s, d)).start()
 
     def compute(d, slot):
-        entry = jnp.zeros((1, rows), jnp.int32)
-        for j in range(cap):
-            entry = jnp.where(lane_place == j, e_ref[d, j], entry)
+        entry = recv_e[pl.ds(d, 1), 0:rows]
         named = key_block == entry
-        start = pl.multiple_of(d * rows, rows)
         stats_v[slot] = jnp.zeros(stats_v.shape[1:], stats_v.dtype)
         for h in range(heads):
-            q = q_ref[pl.ds(start, rows), h * HD:(h + 1) * HD]
+            q = recv_q[d, :, h * HD:(h + 1) * HD]
             k = kv_ref[:, h * HD:(h + 1) * HD]
             v = kv_ref[:, width + h * HD:width + (h + 1) * HD]
             st = lax.dot_general(
@@ -246,6 +262,8 @@
         peer_copy(stage_stats.at[d], back_stats.at[me_s], ss.at[d], sr.at[me_s], (d, me_d)).start()
         peer_copy(stage_ctx.at[d], back_ctx.at[me_s], cs.at[d], cr.at[me_s], (d, me_d)).start()
 
+    for c in own_in:
+        c.wait()
     compute(me_s, 0)
     for c in staged(me_s, 0):
         c.start()
@@ -262,6 +280,8 @@
     def _(o):
         d = lax.rem(me_s + o, n_seq)
         slot = lax.rem(o, 2)
+        e_in(me_s, d).wait_recv()
+        q_in(me_s, d).wait_recv()
         compute(d, slot)
         for c in staged(d, slot):
             c.start()
@@ -284,6 +304,12 @@
     @pl.loop(1, n_seq)
     def _(o):
         d = lax.rem(me_s + o, n_seq)
+        e_in(d, me_s).wait_send()
+        q_in(d, me_s).wait_send()
+
+    @pl.loop(1, n_seq)
+    def _(o):
+        d = lax.rem(me_s + o, n_seq)
         s = lax.rem(me_s + n_seq - o, n_seq)
         peer_copy(stage_stats.at[d], back_stats.at[me_s], ss.at[d], sr.at[me_s], (d, me_d)).wait_send()
         peer_copy(stage_ctx.at[d], back_ctx.at[me_s], cs.at[d], cr.at[me_s], (d, me_d)).wait_send()
@@ -300,10 +326,8 @@
         peer_copy(w_src(me_d), w_cols.at[s], ws.at[s], wr.at[s], (me_s, s)).wait_recv()
 
 
-def attend_back(recv_q, recv_e, kv_flat, w_loc, heads, n_seq, n_db):
-    n_src, cap, span, width = recv_q.shape
-    rows = cap * span
-    q_rows = recv_q.reshape(n_src * rows, width)
+def attend_back(send_q, send_e, kv_flat, w_loc, heads, n_seq, n_db):
+    n_src, rows, width = send_q.shape
     kv_rows = kv_flat.reshape(-1, kv_flat.shape[2])
     stats_shape = (n_src, 8, 2 * LANES)
     ctx_shape = (n_src, rows, width)
@@ -318,8 +342,8 @@
             jax.ShapeDtypeStruct((n_db, w_loc.shape[0], w_loc.shape[1] // n_db), w_loc.dtype),
         ),
         in_specs=[
-            pl.BlockSpec(memory_space=pltpu.SMEM),
-            pl.BlockSpec(memory_space=pltpu.VMEM),
+            any_spec(),
+            any_spec(),
             pl.BlockSpec(memory_space=pltpu.VMEM),
             any_spec(),
         ],
@@ -327,11 +351,14 @@
         scratch_shapes=[
             pltpu.VMEM((2, rows, width), jnp.bfloat16),
             pltpu.VMEM((2,) + stats_shape[1:], jnp.float32),
+            pltpu.VMEM(send_q.shape, send_q.dtype),
+            pltpu.VMEM(send_e.shape, send_e.dtype),
             dma((n_seq,)), dma((n_seq,)), dma((n_seq,)), dma((n_seq,)),
             dma((n_db,)), dma((n_db,)), dma((5,)), dma((2, 2)),
+            dma((n_seq,)), dma((n_seq,)), dma((n_seq,)), dma((n_seq,)),
         ],
         compiler_params=pltpu.CompilerParams(collective_id=1, has_side_effects=True),
-    )(recv_e, q_rows, kv_rows, w_loc)
+    )(send_e, send_q, kv_rows, w_loc)
     return outs[0], outs[1], outs[4]
 
 
@@ -470,11 +497,12 @@
     send_q = pack(queries, src_span, places_total)
     send_e = jnp.zeros((places_total,), jnp.int32)
     send_e = send_e.at[target].set(neighbour_entry.reshape(-1), mode="drop")
-    send_e = jnp.pad(send_e.reshape(n_seq, CAP), ((0, 0), (0, LANES - CAP)))
-    recv_q, recv_e = exchange_out(send_q.reshape(n_seq, CAP, SPAN, row_width), send_e, n_seq)
+    send_e = jnp.repeat(send_e.reshape(n_seq, CAP), SPAN, axis=1)
+    send_e = jnp.pad(send_e, ((0, 0), (0, 2 * LANES - CAP * SPAN)))
     kv_flat = neighbour_kv.reshape(neighbour_kv.shape[0], key_len, 2 * row_width)
     back_ctx, back_stats, weight_cols = attend_back(
-        recv_q, recv_e, kv_flat, output_weight, heads_here, n_seq, n_db
+        send_q.reshape(n_seq, CAP * SPAN, row_width), send_e, kv_flat, output_weight,
+        heads_here, n_seq, n_db
     )
     back_ctx = back_ctx.reshape(places_total, SPAN, row_width)
     context = combine(back_ctx, back_stats, place, neighbour_count, heads_here)

time: 233 us -> 225 us (0.966)
  Pallas kernels: 119 us -> 108 us
  waiting for transfers between devices: 77 us -> 79.8 us
    pallas_call x1 -> x0, Pallas kernels: 43.5 us -> none  [exchange_out(): pl.pallas_call(functools.partial(out_kernel, n_seq), out_shape=(jax.Shape...]
    pallas_call x1, Pallas kernels: 65.9 us -> 98.4 us  [attend_back(): pl.pallas_call(functools.partial(attend_back_kernel, n_seq, n_db, heads,...]
    all_gather x1, waiting for transfers between devices: 77 us -> 79.8 us  [on_device(): contexts = lax.all_gather(context, 'db', axis=0, tiled=False)]
where the time goes in v16:
time: 225 us
  Pallas kernels  108 us (48%)
  waiting for transfers between devices  79.8 us (35%)
  matrix products  13.6 us (6%)
  between operations  13.4 us (6%)
  local copies, waits for them, and re-layouts  7.31 us (3%)
  other arithmetic  2.3 us (1%)
    pallas_call x1, Pallas kernels, attend_back(): pl.pallas_call(functools.partial(attend_back_kernel, n_seq, n_db, heads,...  98.4 us
    all_gather x1, waiting for transfers between devices, on_device(): contexts = lax.all_gather(context, 'db', axis=0, tiled=False)  79.8 us
    dot_general x1, matrix products, on_device(): jnp.einsum('str,srf->tf', contexts, weight_cols, preferred_element_type=j...  7.1 us
    pallas_call x1, Pallas kernels, combine(): pl.pallas_call(functools.partial(combine_kernel, heads), grid_spec=grid_s...  6.67 us
    dot_general x1, matrix products, on_device(): jnp.dot(decoder_states, query_weight, preferred_element_type=jnp.float32)  6.5 us
  transfers between devices with their start and end apart: 1, of which 1 were waited for; matrix products, arithmetic and copies ran while one was open for 0% of the time, Pallas kernels for 0%

profile of v16, /device:TPU:1, one launch (start us, length us, event | category | flops | bytes accessed | tf_op | source)
XLA Modules:
  0.0 224.9 jit_solution(12448778635185174832)
XLA Ops:
  6.5 0.9 iota_compare_fusion.1
  7.4 0.1 lt.62
  7.5 0.1 lt.58
  7.6 0.7 broadcast_multiply_fusion
  8.3 0.8 copy.17
  9.1 0.1 copy.18
  9.1 0.1 mul.24
  9.2 0.8 copy.19
  10.0 0.1 reshape.106
  10.1 0.1 reshape.95
  10.2 0.2 convert_reduce_fusion
  10.4 0.6 multiply_add_fusion.place_ref
  10.9 0.7 scatter_custom_fusion
  11.6 0.1 reshape.97
  11.8 0.1 reshape.98
  11.8 0.6 pad.4.send_e
  12.5 2.5 %copy.20 = bf16[128,8,2,256]{3,1,2,0:T(8,128)(2,1)} copy(bf16[128,8,2,256]{3,2,1,0:T(2,128)(2,1)} %bitcast.29) | data formatting | bytes 2097152
  14.9 1.2 scatter_custom_fusion.1.src_ref
  16.2 6.5 %convolution_convert_fusion = bf16[1024,256]{1,0:T(8,128)(2,1)} fusion(bf16[1024,4096]{1,0:T(8,128)(2,1)} %param.7, bf16[4096,256]{1,0:T(8,128)(2,1)S(1)} %copy-done), kind=kOutput, calls=%fused_computation.4 | convolution fusion | flops 2147745792 | bytes 11010048 | tf_op jit(solution)/shard_map/dot_general | solution.py:487
  22.7 3.3 %shard_map.73 = bf16[48,64,256]{2,1,0:T(8,128)(2,1)} custom-call(s32[48]{0:T(128)} %scatter_custom_fusion.1.src_ref, bf16[16,64,256]{2,1,0:T(8,128)(2,1)} %bitcast.30), custom_call_target="tpu_custom_call" | custom-call | tf_op jit(solution)/shard_map/pallas_call | solution.py:429
  26.0 98.4 %shard_map.74 = (bf16[16,192,256]{2,1,0:T(8,128)(2,1)}, f32[16,8,256]{2,1,0:T(8,128)}, bf16[16,192,256]{2,1,0:T(8,128)(2,1)}, f32[16,8,256]{2,1,0:T(8,128)}, bf16[16,256,256]{2,1,0:T(8,128)(2,1)}) custom-call(s32[16,256]{1,0:T(8,128)} %pad.4.send_e, bf16[16,192,256]{2,1,0:T(8,128)(2,1)} %bitcast.25, bf16[1024,512]{1,0:T(8,128)(2,1)} %bitcast.26, ...), custom_call_target="tpu_custom_call" | custom-call | tf_op jit(solution)/shard_map/pallas_call | solution.py:335
  124.4 6.7 %shard_map.75 = bf16[16,64,256]{2,1,0:T(8,128)(2,1)} custom-call(s32[32]{0:T(128)} %multiply_add_fusion.place_ref, s32[16]{0:T(128)} %count_ref.1, bf16[48,64,256]{2,1,0:T(8,128)(2,1)} %bitcast.28, f32[16,8,256]{2,1,0:T(8,128)} %get-tuple-element.9.stats_ref), custom_call_target="tpu_custom_call" | custom-call | tf_op jit(solution)/shard_map/pallas_call | solution.py:405
  131.1 79.8 %all-gather.2.cloned.1.call-done = bf16[16,1024,256]{2,1,0:T(8,128)(2,1)} async-done(((bf16[1,1024,256]{2,1,0:T(8,128)(2,1)}), bf16[16,1024,256]{2,1,0:T(8,128)(2,1)}) %all-gather.2.cloned.1.call-update) | async-done | bytes 8388624 | tf_op jit(solution)/shard_map/all_gather | solution.py:511
  210.9 7.1 %fusion = bf16[1024,256]{1,0:T(8,128)(2,1)} fusion(bf16[16,1024,256]{2,1,0:T(8,128)(2,1)} %all-gather.2.cloned.1.call-done, bf16[16,256,256]{2,1,0:T(8,128)(2,1)} %get-tuple-element.10), kind=kOutput, calls=%fused_computation.3 | convolution fusion | flops 2147745792 | bytes 11010048 | tf_op jit(solution)/shard_map/str,srf->tf/dot_general | solution.py:512
  (7 shorter events, 0.1 us)
Async XLA Ops:
  6.5 9.6 %copy-start = (bf16[4096,256]{1,0:T(8,128)(2,1)S(1)}, bf16[4096,256]{1,0:T(8,128)(2,1)}, u32[]{:S(2)}) copy-start(bf16[4096,256]{1,0:T(8,128)(2,1)} %param.8) | copy-start | bytes 6291460
  6.5 204.4 %all-gather.2.cloned.1.call-start = ((), (), s32[]{:S(2)}) async-start(), calls=%async_computation | async-start | bytes 8912896 | tf_op jit(solution)/shard_map/all_gather | solution.py:511
Sparse Core Ops, SparseCore 0:
  131.2 79.6 all-gather.1

commit v17 on v16

--- a/solution.py
+++ b/solution.py
@@ -202,9 +202,6 @@
     def w_src(d):
         return w_loc.at[:, pl.ds(pl.multiple_of(d * features, features), features)]
 
-    own_w = pltpu.make_async_copy(w_src(me_d), w_cols.at[me_d], ls.at[4])
-    own_w.start()
-
     own_in = [
         pltpu.make_async_copy(send_q.at[me_s], recv_q.at[me_s], ls.at[0]),
         pltpu.make_async_copy(send_e.at[me_s], recv_e.at[me_s], ls.at[1]),
@@ -223,6 +220,9 @@
         d = lax.rem(me_s + o, n_seq)
         e_in(d, me_s).start()
         q_in(d, me_s).start()
+
+    own_w = pltpu.make_async_copy(w_src(me_d), w_cols.at[me_d], ls.at[4])
+    own_w.start()
 
     @pl.loop(1, n_db)
     def _(o):

time: 225 us -> 225 us (level)
  no operation moved by 1% of the time
where the time goes in v17:
time: 225 us
  Pallas kernels  108 us (48%)
  waiting for transfers between devices  79.9 us (36%)
  matrix products  13.6 us (6%)
  between operations  13.4 us (6%)
  local copies, waits for them, and re-layouts  7.31 us (3%)
  other arithmetic  2.3 us (1%)
    pallas_call x1, Pallas kernels, attend_back(): pl.pallas_call(functools.partial(attend_back_kernel, n_seq, n_db, heads,...  98.4 us
    all_gather x1, waiting for transfers between devices, on_device(): contexts = lax.all_gather(context, 'db', axis=0, tiled=False)  79.8 us
    dot_general x1, matrix products, on_device(): jnp.einsum('str,srf->tf', contexts, weight_cols, preferred_element_type=j...  7.1 us
    pallas_call x1, Pallas kernels, combine(): pl.pallas_call(functools.partial(combine_kernel, heads), grid_spec=grid_s...  6.67 us
    dot_general x1, matrix products, on_device(): jnp.dot(decoder_states, query_weight, preferred_element_type=jnp.float32)  6.5 us
  transfers between devices with their start and end apart: 1, of which 1 were waited for; matrix products, arithmetic and copies ran while one was open for 0% of the time, Pallas kernels for 0%

profile of v17, /device:TPU:1, one launch (start us, length us, event | category | flops | bytes accessed | tf_op | source)
XLA Modules:
  0.0 224.9 jit_solution(3675982576198171607)
XLA Ops:
  6.5 0.9 iota_compare_fusion.1
  7.4 0.1 lt.62
  7.5 0.1 lt.58
  7.6 0.7 broadcast_multiply_fusion
  8.3 0.8 copy.17
  9.1 0.1 copy.18
  9.1 0.1 mul.24
  9.2 0.8 copy.19
  10.0 0.1 reshape.106
  10.1 0.1 reshape.95
  10.2 0.2 convert_reduce_fusion
  10.4 0.6 multiply_add_fusion.place_ref
  10.9 0.7 scatter_custom_fusion
  11.6 0.1 reshape.97
  11.8 0.1 reshape.98
  11.8 0.6 pad.4.send_e
  12.5 2.5 %copy.20 = bf16[128,8,2,256]{3,1,2,0:T(8,128)(2,1)} copy(bf16[128,8,2,256]{3,2,1,0:T(2,128)(2,1)} %bitcast.29) | data formatting | bytes 2097152
  14.9 1.2 scatter_custom_fusion.1.src_ref
  16.2 6.5 %convolution_convert_fusion = bf16[1024,256]{1,0:T(8,128)(2,1)} fusion(bf16[1024,4096]{1,0:T(8,128)(2,1)} %param.7, bf16[4096,256]{1,0:T(8,128)(2,1)S(1)} %copy-done), kind=kOutput, calls=%fused_computation.4 | convolution fusion | flops 2147745792 | bytes 11010048 | tf_op jit(solution)/shard_map/dot_general | solution.py:487
  22.7 3.3 %shard_map.73 = bf16[48,64,256]{2,1,0:T(8,128)(2,1)} custom-call(s32[48]{0:T(128)} %scatter_custom_fusion.1.src_ref, bf16[16,64,256]{2,1,0:T(8,128)(2,1)} %bitcast.30), custom_call_target="tpu_custom_call" | custom-call | tf_op jit(solution)/shard_map/pallas_call | solution.py:429
  26.0 98.4 %shard_map.74 = (bf16[16,192,256]{2,1,0:T(8,128)(2,1)}, f32[16,8,256]{2,1,0:T(8,128)}, bf16[16,192,256]{2,1,0:T(8,128)(2,1)}, f32[16,8,256]{2,1,0:T(8,128)}, bf16[16,256,256]{2,1,0:T(8,128)(2,1)}) custom-call(s32[16,256]{1,0:T(8,128)} %pad.4.send_e, bf16[16,192,256]{2,1,0:T(8,128)(2,1)} %bitcast.25, bf16[1024,512]{1,0:T(8,128)(2,1)} %bitcast.26, ...), custom_call_target="tpu_custom_call" | custom-call | tf_op jit(solution)/shard_map/pallas_call | solution.py:335
  124.4 6.7 %shard_map.75 = bf16[16,64,256]{2,1,0:T(8,128)(2,1)} custom-call(s32[32]{0:T(128)} %multiply_add_fusion.place_ref, s32[16]{0:T(128)} %count_ref.1, bf16[48,64,256]{2,1,0:T(8,128)(2,1)} %bitcast.28, f32[16,8,256]{2,1,0:T(8,128)} %get-tuple-element.9.stats_ref), custom_call_target="tpu_custom_call" | custom-call | tf_op jit(solution)/shard_map/pallas_call | solution.py:405
  131.1 79.8 %all-gather.2.cloned.1.call-done = bf16[16,1024,256]{2,1,0:T(8,128)(2,1)} async-done(((bf16[1,1024,256]{2,1,0:T(8,128)(2,1)}), bf16[16,1024,256]{2,1,0:T(8,128)(2,1)}) %all-gather.2.cloned.1.call-update) | async-done | bytes 8388624 | tf_op jit(solution)/shard_map/all_gather | solution.py:511
  210.9 7.1 %fusion = bf16[1024,256]{1,0:T(8,128)(2,1)} fusion(bf16[16,1024,256]{2,1,0:T(8,128)(2,1)} %all-gather.2.cloned.1.call-done, bf16[16,256,256]{2,1,0:T(8,128)(2,1)} %get-tuple-element.10), kind=kOutput, calls=%fused_computation.3 | convolution fusion | flops 2147745792 | bytes 11010048 | tf_op jit(solution)/shard_map/str,srf->tf/dot_general | solution.py:512
  (7 shorter events, 0.1 us)
Async XLA Ops:
  6.5 9.6 %copy-start = (bf16[4096,256]{1,0:T(8,128)(2,1)S(1)}, bf16[4096,256]{1,0:T(8,128)(2,1)}, u32[]{:S(2)}) copy-start(bf16[4096,256]{1,0:T(8,128)(2,1)} %param.8) | copy-start | bytes 6291460
  6.5 204.4 %all-gather.2.cloned.1.call-start = ((), (), s32[]{:S(2)}) async-start(), calls=%async_computation | async-start | bytes 8912896 | tf_op jit(solution)/shard_map/all_gather | solution.py:511
Sparse Core Ops, SparseCore 0:
  131.2 79.6 all-gather.1

commit v18 on v16

--- a/solution.py
+++ b/solution.py
@@ -388,7 +388,7 @@
             ).astype(out_ref.dtype)
         return carry
 
-    lax.fori_loop(0, out_ref.shape[0], one_span, 0)
+    lax.fori_loop(0, out_ref.shape[0], one_span, 0, unroll=True)
 
 
 def combine(back_ctx, back_stats, place, neighbour_count, heads):

time: 225 us -> 224 us (level)
  no operation moved by 1% of the time
where the time goes in v18:
time: 224 us
  Pallas kernels  107 us (48%)
  waiting for transfers between devices  79.8 us (36%)
  matrix products  13.6 us (6%)
  between operations  13.4 us (6%)
  local copies, waits for them, and re-layouts  7.31 us (3%)
  other arithmetic  2.3 us (1%)
    pallas_call x1, Pallas kernels, attend_back(): pl.pallas_call(functools.partial(attend_back_kernel, n_seq, n_db, heads,...  98.4 us
    all_gather x1, waiting for transfers between devices, on_device(): contexts = lax.all_gather(context, 'db', axis=0, tiled=False)  79.8 us
    dot_general x1, matrix products, on_device(): jnp.einsum('str,srf->tf', contexts, weight_cols, preferred_element_type=j...  7.1 us
    dot_general x1, matrix products, on_device(): jnp.dot(decoder_states, query_weight, preferred_element_type=jnp.float32)  6.5 us
    pallas_call x1, Pallas kernels, combine(): pl.pallas_call(functools.partial(combine_kernel, heads), grid_spec=grid_s...  5.71 us
  transfers between devices with their start and end apart: 1, of which 1 were waited for; matrix products, arithmetic and copies ran while one was open for 0% of the time, Pallas kernels for 0%

profile of v18, /device:TPU:1, one launch (start us, length us, event | category | flops | bytes accessed | tf_op | source)
XLA Modules:
  0.0 223.9 jit_solution(12809480337914110770)
XLA Ops:
  6.5 0.9 iota_compare_fusion.1
  7.4 0.1 lt.62
  7.5 0.1 lt.58
  7.6 0.7 broadcast_multiply_fusion
  8.3 0.8 copy.17
  9.1 0.1 copy.18
  9.1 0.1 mul.24
  9.2 0.8 copy.19
  10.0 0.1 reshape.106
  10.1 0.1 reshape.95
  10.2 0.2 convert_reduce_fusion
  10.4 0.6 multiply_add_fusion.place_ref
  10.9 0.7 scatter_custom_fusion
  11.6 0.1 reshape.97
  11.8 0.1 reshape.98
  11.8 0.6 pad.4.send_e
  12.5 2.5 %copy.20 = bf16[128,8,2,256]{3,1,2,0:T(8,128)(2,1)} copy(bf16[128,8,2,256]{3,2,1,0:T(2,128)(2,1)} %bitcast.29) | data formatting | bytes 2097152
  14.9 1.2 scatter_custom_fusion.1.src_ref
  16.2 6.5 %convolution_convert_fusion = bf16[1024,256]{1,0:T(8,128)(2,1)} fusion(bf16[1024,4096]{1,0:T(8,128)(2,1)} %param.7, bf16[4096,256]{1,0:T(8,128)(2,1)S(1)} %copy-done), kind=kOutput, calls=%fused_computation.4 | convolution fusion | flops 2147745792 | bytes 11010048 | tf_op jit(solution)/shard_map/dot_general | solution.py:487
  22.7 3.3 %shard_map.73 = bf16[48,64,256]{2,1,0:T(8,128)(2,1)} custom-call(s32[48]{0:T(128)} %scatter_custom_fusion.1.src_ref, bf16[16,64,256]{2,1,0:T(8,128)(2,1)} %bitcast.30), custom_call_target="tpu_custom_call" | custom-call | tf_op jit(solution)/shard_map/pallas_call | solution.py:429
  26.0 98.4 %shard_map.74 = (bf16[16,192,256]{2,1,0:T(8,128)(2,1)}, f32[16,8,256]{2,1,0:T(8,128)}, bf16[16,192,256]{2,1,0:T(8,128)(2,1)}, f32[16,8,256]{2,1,0:T(8,128)}, bf16[16,256,256]{2,1,0:T(8,128)(2,1)}) custom-call(s32[16,256]{1,0:T(8,128)} %pad.4.send_e, bf16[16,192,256]{2,1,0:T(8,128)(2,1)} %bitcast.25, bf16[1024,512]{1,0:T(8,128)(2,1)} %bitcast.26, ...), custom_call_target="tpu_custom_call" | custom-call | tf_op jit(solution)/shard_map/pallas_call | solution.py:335
  124.4 5.7 %shard_map.75 = bf16[16,64,256]{2,1,0:T(8,128)(2,1)} custom-call(s32[32]{0:T(128)} %multiply_add_fusion.place_ref, s32[16]{0:T(128)} %count_ref.1, bf16[48,64,256]{2,1,0:T(8,128)(2,1)} %bitcast.28, f32[16,8,256]{2,1,0:T(8,128)} %get-tuple-element.9.stats_ref), custom_call_target="tpu_custom_call" | custom-call | tf_op jit(solution)/shard_map/pallas_call | solution.py:405
  130.1 79.8 %all-gather.2.cloned.1.call-done = bf16[16,1024,256]{2,1,0:T(8,128)(2,1)} async-done(((bf16[1,1024,256]{2,1,0:T(8,128)(2,1)}), bf16[16,1024,256]{2,1,0:T(8,128)(2,1)}) %all-gather.2.cloned.1.call-update) | async-done | bytes 8388624 | tf_op jit(solution)/shard_map/all_gather | solution.py:511
  210.0 7.1 %fusion = bf16[1024,256]{1,0:T(8,128)(2,1)} fusion(bf16[16,1024,256]{2,1,0:T(8,128)(2,1)} %all-gather.2.cloned.1.call-done, bf16[16,256,256]{2,1,0:T(8,128)(2,1)} %get-tuple-element.10), kind=kOutput, calls=%fused_computation.3 | convolution fusion | flops 2147745792 | bytes 11010048 | tf_op jit(solution)/shard_map/str,srf->tf/dot_general | solution.py:512
  (7 shorter events, 0.1 us)
Async XLA Ops:
  6.5 9.6 %copy-start = (bf16[4096,256]{1,0:T(8,128)(2,1)S(1)}, bf16[4096,256]{1,0:T(8,128)(2,1)}, u32[]{:S(2)}) copy-start(bf16[4096,256]{1,0:T(8,128)(2,1)} %param.8) | copy-start | bytes 6291460
  6.5 203.4 %all-gather.2.cloned.1.call-start = ((), (), s32[]{:S(2)}) async-start(), calls=%async_computation | async-start | bytes 8912896 | tf_op jit(solution)/shard_map/all_gather | solution.py:511
Sparse Core Ops, SparseCore 0:
  130.3 79.6 all-gather.1

commit v19 on v18

--- a/solution.py
+++ b/solution.py
@@ -416,7 +416,7 @@
         out_ref[p] = jnp.where(span >= 0, rows, jnp.zeros_like(rows))
         return carry
 
-    lax.fori_loop(0, out_ref.shape[0], one_place, 0)
+    lax.fori_loop(0, out_ref.shape[0], one_place, 0, unroll=8)
 
 
 def pack(queries, src_span, places):

time: 224 us -> 224 us (level)
  no operation moved by 1% of the time
where the time goes in v19:
time: 224 us
  Pallas kernels  107 us (48%)
  waiting for transfers between devices  79.8 us (36%)
  matrix products  13.6 us (6%)
  between operations  13.4 us (6%)
  local copies, waits for them, and re-layouts  7.31 us (3%)
  other arithmetic  2.3 us (1%)
    pallas_call x1, Pallas kernels, attend_back(): pl.pallas_call(functools.partial(attend_back_kernel, n_seq, n_db, heads,...  98.4 us
    all_gather x1, waiting for transfers between devices, on_device(): contexts = lax.all_gather(context, 'db', axis=0, tiled=False)  79.8 us
    dot_general x1, matrix products, on_device(): jnp.einsum('str,srf->tf', contexts, weight_cols, preferred_element_type=j...  7.1 us
    dot_general x1, matrix products, on_device(): jnp.dot(decoder_states, query_weight, preferred_element_type=jnp.float32)  6.5 us
    pallas_call x1, Pallas kernels, combine(): pl.pallas_call(functools.partial(combine_kernel, heads), grid_spec=grid_s...  5.71 us
  transfers between devices with their start and end apart: 1, of which 1 were waited for; matrix products, arithmetic and copies ran while one was open for 0% of the time, Pallas kernels for 0%

profile of v19, /device:TPU:1, one launch (start us, length us, event | category | flops | bytes accessed | tf_op | source)
XLA Modules:
  0.0 223.7 jit_solution(6765225494193557233)
XLA Ops:
  6.5 0.9 iota_compare_fusion.1
  7.4 0.1 lt.62
  7.5 0.1 lt.58
  7.6 0.7 broadcast_multiply_fusion
  8.3 0.8 copy.17
  9.1 0.1 copy.18
  9.1 0.1 mul.24
  9.2 0.8 copy.19
  10.0 0.1 reshape.106
  10.1 0.1 reshape.95
  10.2 0.2 convert_reduce_fusion
  10.4 0.6 multiply_add_fusion.place_ref
  10.9 0.7 scatter_custom_fusion
  11.6 0.1 reshape.97
  11.8 0.1 reshape.98
  11.8 0.6 pad.4.send_e
  12.5 2.5 %copy.20 = bf16[128,8,2,256]{3,1,2,0:T(8,128)(2,1)} copy(bf16[128,8,2,256]{3,2,1,0:T(2,128)(2,1)} %bitcast.29) | data formatting | bytes 2097152
  14.9 1.2 scatter_custom_fusion.1.src_ref
  16.2 6.5 %convolution_convert_fusion = bf16[1024,256]{1,0:T(8,128)(2,1)} fusion(bf16[1024,4096]{1,0:T(8,128)(2,1)} %param.7, bf16[4096,256]{1,0:T(8,128)(2,1)S(1)} %copy-done), kind=kOutput, calls=%fused_computation.4 | convolution fusion | flops 2147745792 | bytes 11010048 | tf_op jit(solution)/shard_map/dot_general | solution.py:487
  22.7 3.1 %shard_map.73 = bf16[48,64,256]{2,1,0:T(8,128)(2,1)} custom-call(s32[48]{0:T(128)} %scatter_custom_fusion.1.src_ref, bf16[16,64,256]{2,1,0:T(8,128)(2,1)} %bitcast.30), custom_call_target="tpu_custom_call" | custom-call | tf_op jit(solution)/shard_map/pallas_call | solution.py:429
  25.8 98.4 %shard_map.74 = (bf16[16,192,256]{2,1,0:T(8,128)(2,1)}, f32[16,8,256]{2,1,0:T(8,128)}, bf16[16,192,256]{2,1,0:T(8,128)(2,1)}, f32[16,8,256]{2,1,0:T(8,128)}, bf16[16,256,256]{2,1,0:T(8,128)(2,1)}) custom-call(s32[16,256]{1,0:T(8,128)} %pad.4.send_e, bf16[16,192,256]{2,1,0:T(8,128)(2,1)} %bitcast.25, bf16[1024,512]{1,0:T(8,128)(2,1)} %bitcast.26, ...), custom_call_target="tpu_custom_call" | custom-call | tf_op jit(solution)/shard_map/pallas_call | solution.py:335
  124.2 5.7 %shard_map.75 = bf16[16,64,256]{2,1,0:T(8,128)(2,1)} custom-call(s32[32]{0:T(128)} %multiply_add_fusion.place_ref, s32[16]{0:T(128)} %count_ref.1, bf16[48,64,256]{2,1,0:T(8,128)(2,1)} %bitcast.28, f32[16,8,256]{2,1,0:T(8,128)} %get-tuple-element.9.stats_ref), custom_call_target="tpu_custom_call" | custom-call | tf_op jit(solution)/shard_map/pallas_call | solution.py:405
  129.9 79.8 %all-gather.2.cloned.1.call-done = bf16[16,1024,256]{2,1,0:T(8,128)(2,1)} async-done(((bf16[1,1024,256]{2,1,0:T(8,128)(2,1)}), bf16[16,1024,256]{2,1,0:T(8,128)(2,1)}) %all-gather.2.cloned.1.call-update) | async-done | bytes 8388624 | tf_op jit(solution)/shard_map/all_gather | solution.py:511
  209.7 7.1 %fusion = bf16[1024,256]{1,0:T(8,128)(2,1)} fusion(bf16[16,1024,256]{2,1,0:T(8,128)(2,1)} %all-gather.2.cloned.1.call-done, bf16[16,256,256]{2,1,0:T(8,128)(2,1)} %get-tuple-element.10), kind=kOutput, calls=%fused_computation.3 | convolution fusion | flops 2147745792 | bytes 11010048 | tf_op jit(solution)/shard_map/str,srf->tf/dot_general | solution.py:512
  (7 shorter events, 0.1 us)
Async XLA Ops:
  6.5 9.6 %copy-start = (bf16[4096,256]{1,0:T(8,128)(2,1)S(1)}, bf16[4096,256]{1,0:T(8,128)(2,1)}, u32[]{:S(2)}) copy-start(bf16[4096,256]{1,0:T(8,128)(2,1)} %param.8) | copy-start | bytes 6291460
  6.5 203.2 %all-gather.2.cloned.1.call-start = ((), (), s32[]{:S(2)}) async-start(), calls=%async_computation | async-start | bytes 8912896 | tf_op jit(solution)/shard_map/all_gather | solution.py:511
Sparse Core Ops, SparseCore 0:
  130.0 79.6 all-gather.1

commit v20 on v19

--- a/solution.py
+++ b/solution.py
@@ -232,7 +232,6 @@
     def compute(d, slot):
         entry = recv_e[pl.ds(d, 1), 0:rows]
         named = key_block == entry
-        stats_v[slot] = jnp.zeros(stats_v.shape[1:], stats_v.dtype)
         for h in range(heads):
             q = recv_q[d, :, h * HD:(h + 1) * HD]
             k = kv_ref[:, h * HD:(h + 1) * HD]

time: 224 us -> 224 us (level)
  no operation moved by 1% of the time
where the time goes in v20:
time: 224 us
  Pallas kernels  107 us (48%)
  waiting for transfers between devices  79.9 us (36%)
  matrix products  13.6 us (6%)
  between operations  13.4 us (6%)
  local copies, waits for them, and re-layouts  7.31 us (3%)
  other arithmetic  2.3 us (1%)
    pallas_call x1, Pallas kernels, attend_back(): pl.pallas_call(functools.partial(attend_back_kernel, n_seq, n_db, heads,...  98.3 us
    all_gather x1, waiting for transfers between devices, on_device(): contexts = lax.all_gather(context, 'db', axis=0, tiled=False)  79.8 us
    dot_general x1, matrix products, on_device(): jnp.einsum('str,srf->tf', contexts, weight_cols, preferred_element_type=j...  7.1 us
    dot_general x1, matrix products, on_device(): jnp.dot(decoder_states, query_weight, preferred_element_type=jnp.float32)  6.5 us
    pallas_call x1, Pallas kernels, combine(): pl.pallas_call(functools.partial(combine_kernel, heads), grid_spec=grid_s...  5.71 us
  transfers between devices with their start and end apart: 1, of which 1 were waited for; matrix products, arithmetic and copies ran while one was open for 0% of the time, Pallas kernels for 0%

profile of v20, /device:TPU:1, one launch (start us, length us, event | category | flops | bytes accessed | tf_op | source)
XLA Modules:
  0.0 223.6 jit_solution(3781711658684882076)
XLA Ops:
  6.5 0.9 iota_compare_fusion.1
  7.4 0.1 lt.62
  7.5 0.1 lt.58
  7.6 0.7 broadcast_multiply_fusion
  8.3 0.8 copy.17
  9.1 0.1 copy.18
  9.1 0.1 mul.24
  9.2 0.8 copy.19
  10.0 0.1 reshape.106
  10.1 0.1 reshape.95
  10.2 0.2 convert_reduce_fusion
  10.4 0.6 multiply_add_fusion.place_ref
  10.9 0.7 scatter_custom_fusion
  11.6 0.1 reshape.97
  11.8 0.1 reshape.98
  11.8 0.6 pad.4.send_e
  12.5 2.5 %copy.20 = bf16[128,8,2,256]{3,1,2,0:T(8,128)(2,1)} copy(bf16[128,8,2,256]{3,2,1,0:T(2,128)(2,1)} %bitcast.29) | data formatting | bytes 2097152
  14.9 1.2 scatter_custom_fusion.1.src_ref
  16.2 6.5 %convolution_convert_fusion = bf16[1024,256]{1,0:T(8,128)(2,1)} fusion(bf16[1024,4096]{1,0:T(8,128)(2,1)} %param.7, bf16[4096,256]{1,0:T(8,128)(2,1)S(1)} %copy-done), kind=kOutput, calls=%fused_computation.4 | convolution fusion | flops 2147745792 | bytes 11010048 | tf_op jit(solution)/shard_map/dot_general | solution.py:486
  22.7 3.1 %shard_map.73 = bf16[48,64,256]{2,1,0:T(8,128)(2,1)} custom-call(s32[48]{0:T(128)} %scatter_custom_fusion.1.src_ref, bf16[16,64,256]{2,1,0:T(8,128)(2,1)} %bitcast.30), custom_call_target="tpu_custom_call" | custom-call | tf_op jit(solution)/shard_map/pallas_call | solution.py:428
  25.8 98.3 %shard_map.74 = (bf16[16,192,256]{2,1,0:T(8,128)(2,1)}, f32[16,8,256]{2,1,0:T(8,128)}, bf16[16,192,256]{2,1,0:T(8,128)(2,1)}, f32[16,8,256]{2,1,0:T(8,128)}, bf16[16,256,256]{2,1,0:T(8,128)(2,1)}) custom-call(s32[16,256]{1,0:T(8,128)} %pad.4.send_e, bf16[16,192,256]{2,1,0:T(8,128)(2,1)} %bitcast.25, bf16[1024,512]{1,0:T(8,128)(2,1)} %bitcast.26, ...), custom_call_target="tpu_custom_call" | custom-call | tf_op jit(solution)/shard_map/pallas_call | solution.py:334
  124.1 5.7 %shard_map.75 = bf16[16,64,256]{2,1,0:T(8,128)(2,1)} custom-call(s32[32]{0:T(128)} %multiply_add_fusion.place_ref, s32[16]{0:T(128)} %count_ref.1, bf16[48,64,256]{2,1,0:T(8,128)(2,1)} %bitcast.28, f32[16,8,256]{2,1,0:T(8,128)} %get-tuple-element.9.stats_ref), custom_call_target="tpu_custom_call" | custom-call | tf_op jit(solution)/shard_map/pallas_call | solution.py:404
  129.8 79.8 %all-gather.2.cloned.1.call-done = bf16[16,1024,256]{2,1,0:T(8,128)(2,1)} async-done(((bf16[1,1024,256]{2,1,0:T(8,128)(2,1)}), bf16[16,1024,256]{2,1,0:T(8,128)(2,1)}) %all-gather.2.cloned.1.call-update) | async-done | bytes 8388624 | tf_op jit(solution)/shard_map/all_gather | solution.py:510
  209.7 7.1 %fusion = bf16[1024,256]{1,0:T(8,128)(2,1)} fusion(bf16[16,1024,256]{2,1,0:T(8,128)(2,1)} %all-gather.2.cloned.1.call-done, bf16[16,256,256]{2,1,0:T(8,128)(2,1)} %get-tuple-element.10), kind=kOutput, calls=%fused_computation.3 | convolution fusion | flops 2147745792 | bytes 11010048 | tf_op jit(solution)/shard_map/str,srf->tf/dot_general | solution.py:511
  (7 shorter events, 0.1 us)
Async XLA Ops:
  6.5 9.6 %copy-start = (bf16[4096,256]{1,0:T(8,128)(2,1)S(1)}, bf16[4096,256]{1,0:T(8,128)(2,1)}, u32[]{:S(2)}) copy-start(bf16[4096,256]{1,0:T(8,128)(2,1)} %param.8) | copy-start | bytes 6291460
  6.5 203.1 %all-gather.2.cloned.1.call-start = ((), (), s32[]{:S(2)}) async-start(), calls=%async_computation | async-start | bytes 8912896 | tf_op jit(solution)/shard_map/all_gather | solution.py:510
Sparse Core Ops, SparseCore 0:
  130.0 79.6 all-gather.1
